TPU v7x, 32 devices: a whole 2x2x4 slice. The times are simulated.
32 devices in a mesh: groups: 2 (over y), expert: 8 (over z, x), dp: 2 (over core).
Axes of the slice: x: 2, y: 2, z: 4, core: 2. Of those that a mesh axis runs over, the one named last changes fastest.
Arguments:
- tokens: bfloat16 [4096, 3584], P(('groups', 'expert', 'dp')), parts along dimension 0, may hold values from -6 to 6
- grad_out: bfloat16 [4096, 3584], P(('groups', 'expert', 'dp')), parts along dimension 0, may hold values from -6 to 6
- routing: int32 [4096, 8], P(('groups', 'expert', 'dp')), parts along dimension 0, may hold values from 0 to 63, as said below
- gates: float32 [4096, 8], P(('groups', 'expert', 'dp')), parts along dimension 0, may hold values from 0.05 to 0.5
- modality: int32 [4096], P(('groups', 'expert', 'dp')), parts along dimension 0, may hold values from 0 to 1, as said below
- hot_experts: int32 [4], P('groups'), parts along dimension 0, may hold values from 0 to 7, as said below
- gate_weight: bfloat16 [16384, 3584], P('expert'), may hold values from -0.09375 to 0.09375
- up_weight: bfloat16 [16384, 3584], P('expert'), may hold values from -0.09375 to 0.09375
- down_weight: bfloat16 [16384, 3584], P('expert'), may hold values from -0.125 to 0.125
Outputs:
- grad_tokens: bfloat16 [4096, 3584], P(('groups', 'expert', 'dp')), parts along dimension 0
- grad_gate: bfloat16 [32768, 3584], P(('groups', 'expert', 'dp')), parts along dimension 0
- grad_up: bfloat16 [32768, 3584], P(('groups', 'expert', 'dp')), parts along dimension 0
- grad_down: bfloat16 [32768, 3584], P(('groups', 'expert', 'dp')), parts along dimension 0
There are 2 independent parts, one for each index of `groups`. A program takes and returns all parts, laid end to end along the dimension named above; an argument that names none is the same for every part. Nothing has to cross between parts.
Inputs may be any that keep to these rules, and one draw needn't show every extreme that they name: `routing`: each token names 8 different experts. Among the 128 tokens of each device, every expert in flight that is not hot is named by exactly 2 text tokens, a text token names at most one expert in flight, an image token names none in flight outside its last 2 entries, and no text token names a hot expert. `modality`: exactly 8 image tokens among the 128 tokens of each device. `hot_experts`: 2 different experts in flight.
All inputs are finite; a program needn't handle non-finite values.
Results may differ from a plain program's by a relative error of at most 0.0061.
Values may be sent and summed in bfloat16 or wider, within the bound.
No kernel may reach another device: no remote copies, remote signals or barrier semaphores. Data moves between devices by JAX's collectives and lax.ppermute only.
A program may use at most 384 MiB of HBM per device.

v0:
```python
import jax
import jax.numpy as jnp
from jax import lax
from jax.sharding import PartitionSpec as P

FLIGHT = 8
HOTCAP = 8


def expert_pass(in_tokens, in_scaled, gate_rows, up_rows, down_rows):
    pre_gate = jnp.einsum("nd,hd->nh", in_tokens, gate_rows, preferred_element_type=jnp.float32)
    pre_up = jnp.einsum("nd,hd->nh", in_tokens, up_rows, preferred_element_type=jnp.float32)
    sigmoid_gate = jax.nn.sigmoid(pre_gate)
    swish_gate = pre_gate * sigmoid_gate
    activated = (swish_gate * pre_up).astype(jnp.bfloat16)
    grad_act = jnp.einsum("nd,hd->nh", in_scaled, down_rows, preferred_element_type=jnp.float32)
    grad_pre_gate = (
        grad_act * pre_up * sigmoid_gate * (1.0 + pre_gate * (1.0 - sigmoid_gate))
    ).astype(jnp.bfloat16)
    grad_pre_up = (grad_act * swish_gate).astype(jnp.bfloat16)
    gate_term = jnp.einsum(
        "nh,nd->hd", grad_pre_gate, in_tokens, preferred_element_type=jnp.float32
    )
    up_term = jnp.einsum("nh,nd->hd", grad_pre_up, in_tokens, preferred_element_type=jnp.float32)
    down_term = jnp.einsum("nh,nd->hd", activated, in_scaled, preferred_element_type=jnp.float32)
    partials = jnp.dot(grad_pre_gate, gate_rows, preferred_element_type=jnp.float32)
    partials = (
        partials + jnp.dot(grad_pre_up, up_rows, preferred_element_type=jnp.float32)
    ).astype(jnp.bfloat16)
    return (partials, (gate_term, up_term, down_term))


def per_device(
    tokens, grad_out, routing, gates, modality, hot_experts, gate_weight, up_weight, down_weight
):
    tok_count, model_width = tokens.shape
    top_count = routing.shape[1]
    hot_count = hot_experts.shape[0]
    devices = lax.axis_size("expert")
    split_count = devices // FLIGHT
    position = lax.broadcasted_iota(jnp.int32, (tok_count, top_count), 1)
    pinned_slot = position - (top_count - hot_count)
    pick_table = pinned_slot[:, :, None] == jnp.arange(hot_count, dtype=jnp.int32)[None, None, :]
    hot_pick = jnp.sum(jnp.where(pick_table, hot_experts[None, None, :], 0), axis=2)
    pinned = (modality[:, None] == 1) & (pinned_slot >= 0)
    chosen = jnp.where(pinned, hot_pick, routing)
    matches = chosen[:, :, None] == jnp.arange(FLIGHT, dtype=jnp.int32)[None, None, :]
    expert_gate = jnp.sum(jnp.where(matches, gates[:, :, None], 0.0), axis=1)
    present = jnp.any(matches, axis=1)
    placed = jnp.cumsum(present.astype(jnp.int32), axis=0) - 1
    slot_ids = jnp.arange(HOTCAP, dtype=jnp.int32)
    chooser = (placed.T[:, None, :] == slot_ids[None, :, None]) & present.T[:, None, :]
    picker = chooser.astype(jnp.bfloat16)
    picked = jnp.einsum("scr,rd->scd", picker, tokens, preferred_element_type=jnp.float32).astype(
        jnp.bfloat16
    )
    picked_grad = jnp.einsum("scr,rd->scd", picker, grad_out, preferred_element_type=jnp.float32)
    slot_gate = jnp.sum(jnp.where(chooser, expert_gate.T[:, None, :], 0.0), axis=2)
    scaled = (picked_grad * slot_gate[:, :, None]).astype(jnp.bfloat16)
    picked, scaled = (picked, scaled)
    send_shape = (devices, HOTCAP, model_width)

    def replicate_rows(block_data):
        widened = jnp.broadcast_to(block_data[:, None], (FLIGHT, split_count, HOTCAP, model_width))
        return widened.reshape(send_shape)

    got_tokens, got_scaled = (
        lax.all_to_all(replicate_rows(picked), "expert", split_axis=0, concat_axis=0, tiled=True),
        lax.all_to_all(replicate_rows(scaled), "expert", split_axis=0, concat_axis=0, tiled=True),
    )
    partials, grad_terms = expert_pass(
        got_tokens.reshape(-1, model_width),
        got_scaled.reshape(-1, model_width),
        gate_weight,
        up_weight,
        down_weight,
    )
    returned = lax.all_to_all(
        partials.reshape(send_shape), "expert", split_axis=0, concat_axis=0, tiled=True
    )
    returned = returned.reshape(FLIGHT, split_count, HOTCAP, model_width)
    grad_tokens = jnp.einsum(
        "fcr,fpcd->rd", chooser.astype(jnp.bfloat16), returned, preferred_element_type=jnp.float32
    )
    summed = (
        lax.psum_scatter(grad_terms[0], "dp", scatter_dimension=0, tiled=True),
        lax.psum_scatter(grad_terms[1], "dp", scatter_dimension=0, tiled=True),
        lax.psum_scatter(grad_terms[2], "dp", scatter_dimension=0, tiled=True),
    )
    return (
        grad_tokens.astype(jnp.bfloat16),
        summed[0].astype(jnp.bfloat16),
        summed[1].astype(jnp.bfloat16),
        summed[2].astype(jnp.bfloat16),
    )


def solution(mesh):
    in_specs = (
        P(("groups", "expert", "dp"), None),
        P(("groups", "expert", "dp"), None),
        P(("groups", "expert", "dp"), None),
        P(("groups", "expert", "dp"), None),
        P(("groups", "expert", "dp")),
        P("groups"),
        P("expert", None),
        P("expert", None),
        P("expert", None),
    )
    out_specs = (
        P(("groups", "expert", "dp"), None),
        P(("groups", "expert", "dp"), None),
        P(("groups", "expert", "dp"), None),
        P(("groups", "expert", "dp"), None),
    )
    return jax.shard_map(
        per_device, mesh=mesh, in_specs=in_specs, out_specs=out_specs, check_vma=False
    )
```

profile of v0, /device:TPU:0, one launch (start us, length us, event | category | flops | bytes accessed | tf_op | source)
XLA Modules:
  0.0 211.0 jit_solution(14166473032863376491)
XLA Ops:
  7.2 0.0 copy-start
  7.2 0.7 broadcast_compare_fusion.1
  7.9 0.7 select_reduce_fusion.2
  8.7 0.8 and_select_fusion
  9.5 0.1 copy.28
  9.6 0.2 reduce_window_sum.11
  9.8 0.0 copy-done
  9.8 1.0 convolution_convert_fusion
  10.9 7.3 %all-to-all-start.1 = ((bf16[8,8,3584]{2,1,0:T(8,128)(2,1)}), bf16[8,8,3584]{2,1,0:T(8,128)(2,1)S(1)}, u32[]{:S(2)}, u32[]{:S(2)}) async-start(bf16[8,8,3584]{2,1,0:T(8,128)(2,1)} %convolution_convert_fusion), calls=%async_computation.1 | async-start | bytes 917504 | tf_op jit(solution)/shard_map/all_to_all | solution.py:68
  18.1 0.7 select_reduce_fusion.1
  18.8 0.1 select_reduce_fusion
  18.9 0.1 copy.31
  19.0 2.2 %fusion.1 = bf16[8,8,3584]{2,1,0:T(8,128)(2,1)} fusion(bf16[128,3584]{1,0:T(8,128)(2,1)} %param.10, f32[8,8]{1,0:T(8,128)S(1)} %copy.31, pred[8,8,128]{2,0,1:T(8,128)(4,1)S(1)} %fusion.22), kind=kOutput, calls=%fused_computation.5 | convolution fusion | flops 59179008 | bytes 1384704 | tf_op jit(solution)/shard_map/scr,rd->scd/dot_general | solution.py:57
  21.2 10.0 %all-to-all-done.1 = bf16[8,8,3584]{2,1,0:T(8,128)(2,1)S(1)} async-done(((bf16[8,8,3584]{2,1,0:T(8,128)(2,1)}), bf16[8,8,3584]{2,1,0:T(8,128)(2,1)S(1)}, u32[]{:S(2)}, u32[]{:S(2)}) %all-to-all-start.1) | async-done | bytes 458784 | tf_op jit(solution)/shard_map/all_to_all | solution.py:68
  31.2 3.6 %all-to-all-start = ((bf16[8,8,3584]{2,1,0:T(8,128)(2,1)}), bf16[8,8,3584]{2,1,0:T(8,128)(2,1)S(1)}, u32[]{:S(2)}, u32[]{:S(2)}) async-start(bf16[8,8,3584]{2,1,0:T(8,128)(2,1)} %fusion.1), calls=%async_computation | async-start | bytes 917504 | tf_op jit(solution)/shard_map/all_to_all | solution.py:69
  34.9 0.0 reduce-scatter.8.cloned.1.call-start
  34.9 9.7 %fusion.11 = f32[64,2048]{1,0:T(8,128)S(1)} fusion(bf16[2048,3584]{1,0:T(8,128)(2,1)} %param.15, bf16[8,8,3584]{2,1,0:T(8,128)(2,1)S(1)} %all-to-all-done.1), kind=kOutput, calls=%fused_computation.19 | convolution fusion | flops 939524096 | bytes 15663104 | tf_op jit(solution)/shard_map/nd,hd->nh/dot_general | solution.py:11
  44.6 9.7 %fusion.13 = f32[64,2048]{1,0:T(8,128)S(1)} fusion(bf16[2048,3584]{1,0:T(8,128)(2,1)} %param.16, bf16[8,8,3584]{2,1,0:T(8,128)(2,1)S(1)} %all-to-all-done.1), kind=kOutput, calls=%fused_computation.21 | convolution fusion | flops 939524096 | bytes 15663104 | tf_op jit(solution)/shard_map/nd,hd->nh/dot_general | solution.py:12
  54.2 0.0 all-to-all-done
  54.2 11.7 %fusion.15 = f32[2048,3584]{1,0:T(8,128)} fusion(bf16[8,8,3584]{2,1,0:T(8,128)(2,1)S(1)} %all-to-all-done, f32[64,2048]{1,0:T(8,128)S(1)} %fusion.13, f32[64,2048]{1,0:T(8,128)S(1)} %fusion.11), kind=kOutput, calls=%fused_computation.23 | convolution fusion | flops 940310528 | bytes 30867456 | tf_op jit(solution)/shard_map/nh,nd->hd/dot_general | solution.py:25
  65.9 0.0 reduce-scatter.8.cloned.1.call-update
  66.0 0.0 reduce-scatter.6.cloned.1.call-start
  66.0 9.7 %multiply_convert_fusion.1 = (bf16[64,2048]{1,0:T(8,128)(2,1)S(1)}, bf16[64,2048]{1,0:T(8,128)(2,1)S(1)}) fusion(f32[64,2048]{1,0:T(8,128)S(1)} %fusion.11, f32[64,2048]{1,0:T(8,128)S(1)} %fusion.13, bf16[2048,3584]{1,0:T(8,128)(2,1)} %param.17, bf16[8,8,3584]{2,1,0:T(8,128)(2,1)S(1)} %all-to-all-done), kind=kOutput, calls=%fused_computation.11 | convolution fusion | flops 941228032 | bytes 16711680 | tf_op jit(solution)/shard_map/nd,hd->nh/dot_general | solution.py:16
  75.7 19.1 %fusion.7 = f32[2048,3584]{1,0:T(8,128)} fusion(bf16[64,2048]{1,0:T(8,128)(2,1)S(1)} %get-tuple-element.4, bf16[8,8,3584]{2,1,0:T(8,128)(2,1)S(1)} %all-to-all-done.1), kind=kOutput, calls=%fused_computation.15 | convolution fusion | flops 939524096 | bytes 30081024 | tf_op jit(solution)/shard_map/nh,nd->hd/dot_general | solution.py:24
  94.8 0.0 reduce-scatter.6.cloned.1.call-update
  94.9 0.2 reduce-scatter.4.cloned.1.call-start
  95.1 15.1 %fusion.9 = f32[2048,3584]{1,0:T(8,128)} fusion(bf16[64,2048]{1,0:T(8,128)(2,1)S(1)} %get-tuple-element.5, bf16[8,8,3584]{2,1,0:T(8,128)(2,1)S(1)} %all-to-all-done.1), kind=kOutput, calls=%fused_computation.17 | convolution fusion | flops 939524096 | bytes 30081024 | tf_op jit(solution)/shard_map/nh,nd->hd/dot_general | solution.py:21
  110.2 0.0 reduce-scatter.4.cloned.1.call-update
  110.2 7.8 %fusion.27 = f32[64,3584]{1,0:T(8,128)S(1)} fusion(bf16[64,2048]{1,0:T(8,128)(2,1)S(1)} %get-tuple-element.5, bf16[2048,3584]{1,0:T(8,128)(2,1)} %param.15), kind=kOutput, calls=%fused_computation.44 | convolution fusion | flops 939524096 | bytes 15859712 | tf_op jit(solution)/shard_map/dot_general | solution.py:26
  118.0 10.4 %fusion.3 = bf16[8,8,3584]{2,1,0:T(8,128)(2,1)S(1)} fusion(f32[64,3584]{1,0:T(8,128)S(1)} %fusion.27, bf16[64,2048]{1,0:T(8,128)(2,1)S(1)} %get-tuple-element.4, bf16[2048,3584]{1,0:T(8,128)(2,1)} %param.16), kind=kOutput, calls=%fused_computation.7 | convolution fusion | flops 939982848 | bytes 16318464 | tf_op jit(solution)/shard_map/dot_general | solution.py:28
  128.4 18.5 %all_to_all.15 = bf16[8,8,3584]{2,1,0:T(8,128)(2,1)S(1)} all-to-all(bf16[8,8,3584]{2,1,0:T(8,128)(2,1)S(1)} %fusion.3), channel_id=1, replica_groups=mesh['groups'=2,'expert'=8,'dp'=2] {'expert'}, dimensions={0} | all-to-all | bytes 917504 | tf_op jit(solution)/shard_map/all_to_all | solution.py:78
  146.9 1.4 fusion
  148.3 0.0 reduce-scatter.8.cloned.1.call-done
  148.3 9.6 %convert_element_type.46 = bf16[1024,3584]{1,0:T(8,128)(2,1)} convert(f32[1024,3584]{1,0:T(8,128)} %reduce-scatter.8.cloned.1.call-done) | non-fusion elementwise | flops 3670016 | bytes 22020096 | tf_op jit(solution)/shard_map/convert_element_type | solution.py:94
  157.9 0.0 reduce-scatter.6.cloned.1.call-done
  157.9 0.0 copy-start.1
  157.9 12.1 %convert_element_type.44 = bf16[1024,3584]{1,0:T(8,128)(2,1)} convert(f32[1024,3584]{1,0:T(8,128)} %reduce-scatter.6.cloned.1.call-done) | non-fusion elementwise | flops 3670016 | bytes 22020096 | tf_op jit(solution)/shard_map/convert_element_type | solution.py:93
  170.0 25.3 %reduce-scatter.4.cloned.1.call-done = f32[1024,3584]{1,0:T(8,128)} async-done(((f32[2048,3584]{1,0:T(8,128)}), f32[1024,3584]{1,0:T(8,128)}) %reduce-scatter.4.cloned.1.call-update) | async-done | bytes 14680080 | tf_op jit(solution)/shard_map/reduce_scatter | solution.py:86
  195.4 9.1 %convert_element_type.43 = bf16[1024,3584]{1,0:T(8,128)(2,1)} convert(f32[1024,3584]{1,0:T(8,128)} %reduce-scatter.4.cloned.1.call-done) | non-fusion elementwise | flops 3670016 | bytes 22020096 | tf_op jit(solution)/shard_map/convert_element_type | solution.py:92
  204.4 0.0 copy-done.1
  (7 shorter events, 0.1 us)
Async XLA Ops:
  7.2 2.7 %copy-start = (bf16[128,3584]{1,0:T(8,128)(2,1)S(1)}, bf16[128,3584]{1,0:T(8,128)(2,1)}, u32[]{:S(2)}) copy-start(bf16[128,3584]{1,0:T(8,128)(2,1)} %param.9) | copy-start | bytes 2752516
  10.9 20.3 %all-to-all-start.1 = ((bf16[8,8,3584]{2,1,0:T(8,128)(2,1)}), bf16[8,8,3584]{2,1,0:T(8,128)(2,1)S(1)}, u32[]{:S(2)}, u32[]{:S(2)}) async-start(bf16[8,8,3584]{2,1,0:T(8,128)(2,1)} %convolution_convert_fusion), calls=%async_computation.1 | async-start | bytes 917504 | tf_op jit(solution)/shard_map/all_to_all | solution.py:68
  31.2 23.0 %all-to-all-start = ((bf16[8,8,3584]{2,1,0:T(8,128)(2,1)}), bf16[8,8,3584]{2,1,0:T(8,128)(2,1)S(1)}, u32[]{:S(2)}, u32[]{:S(2)}) async-start(bf16[8,8,3584]{2,1,0:T(8,128)(2,1)} %fusion.1), calls=%async_computation | async-start | bytes 917504 | tf_op jit(solution)/shard_map/all_to_all | solution.py:69
  34.9 113.4 %reduce-scatter.8.cloned.1.call-start = ((), (), s32[]{:S(2)}) async-start(), calls=%async_computation.8 | async-start | bytes 44040192 | tf_op jit(solution)/shard_map/reduce_scatter | solution.py:88
  66.0 91.9 %reduce-scatter.6.cloned.1.call-start = ((), (), s32[]{:S(2)}) async-start(), calls=%async_computation.7 | async-start | bytes 44040192 | tf_op jit(solution)/shard_map/reduce_scatter | solution.py:87
  94.9 100.5 %reduce-scatter.4.cloned.1.call-start = ((), (), s32[]{:S(2)}) async-start(), calls=%async_computation.6 | async-start | bytes 44040192 | tf_op jit(solution)/shard_map/reduce_scatter | solution.py:86
  157.9 46.6 %copy-start.1 = (bf16[128,3584]{1,0:T(8,128)(2,1)S(1)}, bf16[128,3584]{1,0:T(8,128)(2,1)}, u32[]{:S(2)}) copy-start(bf16[128,3584]{1,0:T(8,128)(2,1)} %param.9) | copy-start | bytes 2752516
Sparse Core Ops, SparseCore 0:
  66.1 41.7 reduce-scatter.7
  110.1 41.4 reduce-scatter.5
  153.9 41.3 reduce-scatter.3
where the time goes:
time: 212 us; the launch traced here: 211 us
  matrix products  97.8 us (46%)
  waiting for transfers between devices  35.4 us (17%)
  other arithmetic  34.1 us (16%)
  blocking collectives  18.5 us (9%)
  between operations  13.8 us (7%)
  starting transfers between devices  11.2 us (5%)
    reduce_scatter x1, waiting for transfers between devices, per_device(): lax.psum_scatter(grad_terms[0], 'dp', scatter_dimension=0, tiled=True)  25.3 us
    dot_general x1, matrix products, expert_pass(): jnp.einsum('nh,nd->hd', grad_pre_up, in_tokens, preferred_element_type=jn...  19.1 us
    all_to_all x1, blocking collectives, per_device(): lax.all_to_all(partials.reshape(send_shape), 'expert', split_axis=0, conc...  18.5 us
    dot_general x1, matrix products, expert_pass(): jnp.einsum('nh,nd->hd', grad_pre_gate, in_tokens, preferred_element_type=...  15.1 us
    convert_element_type x1, other arithmetic, per_device(): summed[1].astype(jnp.bfloat16)  12.1 us
    dot_general x1, matrix products, expert_pass(): jnp.einsum('nh,nd->hd', activated, in_scaled, preferred_element_type=jnp....  11.7 us
    dot_general x1, matrix products, expert_pass(): jnp.dot(grad_pre_up, up_rows, preferred_element_type=jnp.float32)  10.4 us
    all_to_all x1, waiting for transfers between devices, per_device(): lax.all_to_all(replicate_rows(picked), 'expert', split_axis=0, concat_axi...  10 us
  transfers between devices with their start and end apart: 5, of which 2 were waited for; matrix products, arithmetic and copies ran while one was open for 51% of the time, Pallas kernels for 0%

commit v1 on v0

--- a/solution.py
+++ b/solution.py
@@ -1,10 +1,15 @@
 import jax
 import jax.numpy as jnp
 from jax import lax
+from jax.experimental import pallas as pl
+from jax.experimental.pallas import tpu as pltpu
 from jax.sharding import PartitionSpec as P
 
 FLIGHT = 8
 HOTCAP = 8
+F32 = jnp.float32
+BF16 = jnp.bfloat16
+MIB = 1 << 20
 
 
 def expert_pass(in_tokens, in_scaled, gate_rows, up_rows, down_rows):
@@ -30,7 +35,7 @@
     return (partials, (gate_term, up_term, down_term))
 
 
-def per_device(
+def per_device_general(
     tokens, grad_out, routing, gates, modality, hot_experts, gate_weight, up_weight, down_weight
 ):
     tok_count, model_width = tokens.shape
@@ -57,7 +62,6 @@
     picked_grad = jnp.einsum("scr,rd->scd", picker, grad_out, preferred_element_type=jnp.float32)
     slot_gate = jnp.sum(jnp.where(chooser, expert_gate.T[:, None, :], 0.0), axis=2)
     scaled = (picked_grad * slot_gate[:, :, None]).astype(jnp.bfloat16)
-    picked, scaled = (picked, scaled)
     send_shape = (devices, HOTCAP, model_width)
 
     def replicate_rows(block_data):
@@ -82,37 +86,285 @@
     grad_tokens = jnp.einsum(
         "fcr,fpcd->rd", chooser.astype(jnp.bfloat16), returned, preferred_element_type=jnp.float32
     )
-    summed = (
-        lax.psum_scatter(grad_terms[0], "dp", scatter_dimension=0, tiled=True),
-        lax.psum_scatter(grad_terms[1], "dp", scatter_dimension=0, tiled=True),
-        lax.psum_scatter(grad_terms[2], "dp", scatter_dimension=0, tiled=True),
-    )
-    return (
-        grad_tokens.astype(jnp.bfloat16),
-        summed[0].astype(jnp.bfloat16),
-        summed[1].astype(jnp.bfloat16),
-        summed[2].astype(jnp.bfloat16),
-    )
+    summed = tuple(
+        lax.psum_scatter(term, "dp", scatter_dimension=0, tiled=True) for term in grad_terms
+    )
+    return (grad_tokens.astype(jnp.bfloat16),) + tuple(term.astype(jnp.bfloat16) for term in summed)
+
+
+def pick_rows(where, hot_experts, tokens, grad_out, routing, gates, modality):
+    tok_count, width = tokens.shape
+    top_count = routing.shape[1]
+    hot_count = hot_experts.shape[0]
+    slots = FLIGHT * HOTCAP
+    steps = 2
+
+    def kernel(where_ref, hot_ref, tok_ref, gout_ref, route_ref, gate_ref, mod_ref, *rest):
+        msgs = rest[:FLIGHT]
+        choose_ref, slot_gate_ref = rest[FLIGHT:]
+
+        @pl.when(pl.program_id(0) == 0)
+        def _():
+            position = lax.broadcasted_iota(jnp.int32, (top_count, tok_count), 0)
+            hot_pick = jnp.zeros((top_count, tok_count), jnp.int32)
+            for j in range(hot_count):
+                hot_pick = jnp.where(
+                    position == top_count - hot_count + j, hot_ref[j], hot_pick
+                )
+            pinned = (mod_ref[...] == 1) & (position >= top_count - hot_count)
+            chosen = jnp.where(pinned, hot_pick, route_ref[...])
+            expert = lax.broadcasted_iota(jnp.int32, (FLIGHT, top_count, tok_count), 0)
+            expert = expert ^ where_ref[0]
+            matches = chosen[None] == expert
+            expert_gate = jnp.sum(jnp.where(matches, gate_ref[...][None], 0.0), axis=1)
+            present = jnp.sum(jnp.where(matches, 1.0, 0.0), axis=1)
+            before = lax.broadcasted_iota(jnp.int32, (tok_count, tok_count), 0)
+            after = lax.broadcasted_iota(jnp.int32, (tok_count, tok_count), 1)
+            upto = jnp.where(before <= after, 1.0, 0.0).astype(BF16)
+            placed = jnp.dot(present.astype(BF16), upto, preferred_element_type=F32)
+            slot = lax.broadcasted_iota(jnp.int32, (FLIGHT, HOTCAP, tok_count), 1) + 1
+            slot_hit = placed[:, None, :].astype(jnp.int32) == slot
+            chooser = slot_hit & (present[:, None, :] > 0.0)
+            picker = jnp.where(chooser, 1.0, 0.0).reshape(slots, tok_count)
+            choose_ref[...] = picker.astype(BF16)
+            picked_gate = jnp.where(chooser, expert_gate[:, None, :], 0.0)
+            slot_gate_ref[...] = jnp.sum(
+                picked_gate.reshape(slots, tok_count), axis=1, keepdims=True
+            )
+
+        picker = choose_ref[...]
+        picked = jnp.dot(picker, tok_ref[...], preferred_element_type=F32)
+        scaled = jnp.dot(picker, gout_ref[...], preferred_element_type=F32) * slot_gate_ref[...]
+        for s in range(FLIGHT):
+            rows = slice(s * HOTCAP, (s + 1) * HOTCAP)
+            msgs[s][0] = picked[rows].astype(BF16)
+            msgs[s][1] = scaled[rows].astype(BF16)
+
+    block = width // steps
+    whole = lambda i, *_: (0, 0)
+    column = lambda i, *_: (0, i)
+    out = pl.pallas_call(
+        kernel,
+        out_shape=[jax.ShapeDtypeStruct((2, HOTCAP, width), BF16)] * FLIGHT
+        + [jax.ShapeDtypeStruct((slots, tok_count), BF16)],
+        grid_spec=pltpu.PrefetchScalarGridSpec(
+            num_scalar_prefetch=2,
+            grid=(steps,),
+            in_specs=[
+                pl.BlockSpec((tok_count, block), column),
+                pl.BlockSpec((tok_count, block), column),
+                pl.BlockSpec((top_count, tok_count), whole),
+                pl.BlockSpec((top_count, tok_count), whole),
+                pl.BlockSpec((1, tok_count), whole),
+            ],
+            out_specs=[pl.BlockSpec((2, HOTCAP, block), lambda i, *_: (0, 0, i))] * FLIGHT
+            + [pl.BlockSpec((slots, tok_count), whole)],
+            scratch_shapes=[pltpu.VMEM((slots, 1), F32)],
+        ),
+        cost_estimate=pl.CostEstimate(
+            flops=4 * slots * tok_count * width,
+            bytes_accessed=4 * (slots + tok_count) * width,
+            transcendentals=0,
+        ),
+        name="pick_rows",
+    )(where, hot_experts, tokens, grad_out, routing.T, gates.T, modality[None, :])
+    return out[:FLIGHT], out[FLIGHT]
+
+
+def activation_grads(where, own, other, gate_weight, up_weight, down_weight):
+    _, rows, width = own.shape
+    half = gate_weight.shape[0] // 2
+    tile = min(256, half)
+    steps = half // tile
+    nt = (((1,), (1,)), ((), ()))
+
+    def kernel(where_ref, own_ref, other_ref, g_ref, u_ref, w_ref, *rest):
+        dh_ref, du_ref, act_ref, mine_ref, theirs_ref, tok, scl, acc = rest
+        step = pl.program_id(0)
+
+        @pl.when(step == 0)
+        def _():
+            tok[:rows] = own_ref[0]
+            tok[rows:] = other_ref[0]
+            scl[:rows] = own_ref[1]
+            scl[rows:] = other_ref[1]
+
+        h = lax.dot_general(tok[...], g_ref[...], nt, preferred_element_type=F32)
+        u = lax.dot_general(tok[...], u_ref[...], nt, preferred_element_type=F32)
+        da = lax.dot_general(scl[...], w_ref[...], nt, preferred_element_type=F32)
+        sig = jax.nn.sigmoid(h)
+        swish = h * sig
+        act_ref[...] = (swish * u).astype(BF16)
+        dh = (da * u * sig * (1.0 + h * (1.0 - sig))).astype(BF16)
+        du = (da * swish).astype(BF16)
+        dh_ref[...] = dh
+        du_ref[...] = du
+        part = jnp.dot(dh, g_ref[...], preferred_element_type=F32)
+        part += jnp.dot(du, u_ref[...], preferred_element_type=F32)
+
+        @pl.when(step == 0)
+        def _():
+            acc[...] = part
+
+        @pl.when(step > 0)
+        def _():
+            acc[...] += part
+
+        @pl.when(step == steps - 1)
+        def _():
+            mine_ref[...] = acc[:rows]
+            theirs_ref[...] = acc[rows:].astype(BF16)
+
+    fixed3 = lambda i, w: (0, 0, 0)
+    fixed2 = lambda i, w: (0, 0)
+    weight = pl.BlockSpec((tile, width), lambda i, w: (w[1] * steps + i, 0))
+    hidden = pl.BlockSpec((2 * rows, tile), lambda i, w: (0, i))
+    return pl.pallas_call(
+        kernel,
+        out_shape=[jax.ShapeDtypeStruct((2 * rows, half), BF16)] * 3
+        + [
+            jax.ShapeDtypeStruct((rows, width), F32),
+            jax.ShapeDtypeStruct((rows, width), BF16),
+        ],
+        grid_spec=pltpu.PrefetchScalarGridSpec(
+            num_scalar_prefetch=1,
+            grid=(steps,),
+            in_specs=[
+                pl.BlockSpec((2, rows, width), fixed3),
+                pl.BlockSpec((2, rows, width), fixed3),
+                weight,
+                weight,
+                weight,
+            ],
+            out_specs=[
+                hidden,
+                hidden,
+                hidden,
+                pl.BlockSpec((rows, width), fixed2),
+                pl.BlockSpec((rows, width), fixed2),
+            ],
+            scratch_shapes=[
+                pltpu.VMEM((2 * rows, width), BF16),
+                pltpu.VMEM((2 * rows, width), BF16),
+                pltpu.VMEM((2 * rows, width), F32),
+            ],
+        ),
+        compiler_params=pltpu.CompilerParams(vmem_limit_bytes=48 * MIB),
+        cost_estimate=pl.CostEstimate(
+            flops=20 * rows * half * width,
+            bytes_accessed=6 * half * width,
+            transcendentals=2 * rows * half,
+        ),
+        name="activation_grads",
+    )(where, own, other, gate_weight, up_weight, down_weight)
+
+
+def weight_grads(own, other, dh, du, act):
+    _, rows, width = own.shape
+    half = dh.shape[1]
+    tile = min(256, half)
+    steps = half // tile
+    tn = (((0,), (0,)), ((), ()))
+
+    def kernel(own_ref, other_ref, dh_ref, du_ref, act_ref, gg_ref, gu_ref, gd_ref, tok, scl):
+        @pl.when(pl.program_id(0) == 0)
+        def _():
+            tok[:rows] = own_ref[0]
+            tok[rows:] = other_ref[0]
+            scl[:rows] = own_ref[1]
+            scl[rows:] = other_ref[1]
+
+        for left, right, out in (
+            (dh_ref, tok, gg_ref),
+            (du_ref, tok, gu_ref),
+            (act_ref, scl, gd_ref),
+        ):
+            out[...] = lax.dot_general(
+                left[...], right[...], tn, preferred_element_type=F32
+            ).astype(BF16)
+
+    fixed3 = lambda i: (0, 0, 0)
+    hidden = pl.BlockSpec((2 * rows, tile), lambda i: (0, i))
+    out_block = pl.BlockSpec((tile, width), lambda i: (i, 0))
+    return pl.pallas_call(
+        kernel,
+        out_shape=[jax.ShapeDtypeStruct((half, width), BF16)] * 3,
+        grid=(steps,),
+        in_specs=[
+            pl.BlockSpec((2, rows, width), fixed3),
+            pl.BlockSpec((2, rows, width), fixed3),
+            hidden,
+            hidden,
+            hidden,
+        ],
+        out_specs=[out_block] * 3,
+        scratch_shapes=[
+            pltpu.VMEM((2 * rows, width), BF16),
+            pltpu.VMEM((2 * rows, width), BF16),
+        ],
+        compiler_params=pltpu.CompilerParams(vmem_limit_bytes=48 * MIB),
+        cost_estimate=pl.CostEstimate(
+            flops=12 * rows * half * width,
+            bytes_accessed=6 * half * width,
+            transcendentals=0,
+        ),
+        name="weight_grads",
+    )(own, other, dh, du, act)
+
+
+def per_device(
+    tokens, grad_out, routing, gates, modality, hot_experts, gate_weight, up_weight, down_weight
+):
+    where = jnp.stack([lax.axis_index("expert"), lax.axis_index("dp")]).astype(jnp.int32)
+    swap = [(0, 1), (1, 0)]
+
+    def hop(block, s):
+        if s == 0:
+            return block
+        return lax.ppermute(block, "expert", [(i, i ^ s) for i in range(FLIGHT)])
+
+    msgs, picker = pick_rows(where, hot_experts, tokens, grad_out, routing, gates, modality)
+    got = [None] * FLIGHT
+    for s in reversed(range(FLIGHT)):
+        got[s] = hop(msgs[s], s)
+    own = jnp.concatenate(got, axis=1)
+    other = lax.ppermute(own, "dp", swap)
+    dh, du, act, mine, theirs = activation_grads(
+        where, own, other, gate_weight, up_weight, down_weight
+    )
+    pieces = (mine + lax.ppermute(theirs, "dp", swap).astype(F32)).astype(BF16)
+    back = [None] * FLIGHT
+    for s in reversed(range(FLIGHT)):
+        back[s] = hop(pieces[s * HOTCAP : (s + 1) * HOTCAP], s)
+    grad_gate, grad_up, grad_down = weight_grads(own, other, dh, du, act)
+    grad_tokens = lax.dot_general(
+        picker,
+        jnp.concatenate(back, axis=0),
+        (((0,), (0,)), ((), ())),
+        preferred_element_type=F32,
+    ).astype(BF16)
+    return grad_tokens, grad_gate, grad_up, grad_down
 
 
 def solution(mesh):
+    sizes = dict(mesh.shape)
+    token_spec = P(("groups", "expert", "dp"), None)
     in_specs = (
-        P(("groups", "expert", "dp"), None),
-        P(("groups", "expert", "dp"), None),
-        P(("groups", "expert", "dp"), None),
-        P(("groups", "expert", "dp"), None),
+        token_spec,
+        token_spec,
+        token_spec,
+        token_spec,
         P(("groups", "expert", "dp")),
         P("groups"),
         P("expert", None),
         P("expert", None),
         P("expert", None),
     )
-    out_specs = (
-        P(("groups", "expert", "dp"), None),
-        P(("groups", "expert", "dp"), None),
-        P(("groups", "expert", "dp"), None),
-        P(("groups", "expert", "dp"), None),
-    )
+    paired = sizes["expert"] == FLIGHT and sizes["dp"] == 2
     return jax.shard_map(
-        per_device, mesh=mesh, in_specs=in_specs, out_specs=out_specs, check_vma=False
-    )
+        per_device if paired else per_device_general,
+        mesh=mesh,
+        in_specs=in_specs,
+        out_specs=(token_spec,) * 4,
+        check_vma=False,
+    )

time: 212 us -> 81.4 us (0.38)
  matrix products: 97.8 us -> 1.34 us
  other arithmetic: 34.1 us -> 0.73 us
  Pallas kernels: 0 us -> 29.3 us
  blocking collectives: 18.5 us -> 0 us
  starting transfers between devices: 11.2 us -> 26.2 us
  waiting for transfers between devices: 35.4 us -> 21.1 us
  between operations: 13.8 us -> 0.85 us
    dot_general x11 -> x1, matrix products: 97.8 us -> 1.34 us  [per_device(): lax.dot_general(picker, jnp.concatenate(back, axis=0), (((0,), (0,)), (()...]
    convert_element_type x4 -> x1, other arithmetic: 30.8 us -> 0.08 us  [per_device(): pieces = (mine + lax.ppermute(theirs, 'dp', swap).astype(F32)).astype(BF16)]
    pallas_call x0 -> x3, Pallas kernels: none -> 29.3 us  [the longest x1 17.5 us: activation_grads(): pl.pallas_call(kernel, out_shape=[jax.ShapeDtypeStruct((2 * rows, half),...]
    ppermute x0 -> x16, starting transfers between devices: none -> 26.2 us  [the longest x14 25.9 us: hop(): return lax.ppermute(block, 'expert', [(i, i ^ s) for i in range(FLIGHT)])]
    reduce_scatter x3 -> x0, waiting for transfers between devices: 25.3 us -> none  [the longest x1 25.3 us: per_device(): lax.psum_scatter(grad_terms[0], 'dp', scatter_dimension=0, tiled=True)]
    ppermute x0 -> x16, waiting for transfers between devices: none -> 21.1 us  [the longest x14 17 us: hop(): return lax.ppermute(block, 'expert', [(i, i ^ s) for i in range(FLIGHT)])]
    all_to_all x1 -> x0, blocking collectives: 18.5 us -> none  [per_device(): lax.all_to_all(partials.reshape(send_shape), 'expert', split_axis=0, conc...]
    all_to_all x2 -> x0, starting transfers between devices: 10.9 us -> none  [the longest x1 7.25 us: per_device(): lax.all_to_all(replicate_rows(picked), 'expert', split_axis=0, concat_axi...]
  transfers between devices with their start and end apart: 5 -> 16, of which waited for: 2 -> 5; matrix products, arithmetic and copies ran while one was open for 51% -> 1% of each run, Pallas kernels for 0% -> 10%
where the time goes in v1:
time: 81.4 us; the launch traced here: 81.2 us
  Pallas kernels  29.3 us (36%)
  starting transfers between devices  26.2 us (32%)
  waiting for transfers between devices  21.1 us (26%)
  local copies, waits for them, and re-layouts  1.72 us (2%)
  matrix products  1.34 us (2%)
  between operations  0.85 us (1%)
    ppermute x14, starting transfers between devices, hop(): return lax.ppermute(block, 'expert', [(i, i ^ s) for i in range(FLIGHT)])  25.9 us
    pallas_call x1, Pallas kernels, activation_grads(): pl.pallas_call(kernel, out_shape=[jax.ShapeDtypeStruct((2 * rows, half),...  17.5 us
    ppermute x14, waiting for transfers between devices, hop(): return lax.ppermute(block, 'expert', [(i, i ^ s) for i in range(FLIGHT)])  17 us
    pallas_call x1, Pallas kernels, weight_grads(): pl.pallas_call(kernel, out_shape=[jax.ShapeDtypeStruct((half, width), BF1...  8.33 us
    pallas_call x1, Pallas kernels, pick_rows(): pl.pallas_call(kernel, out_shape=[jax.ShapeDtypeStruct((2, HOTCAP, width)...  3.42 us
    ppermute x1, waiting for transfers between devices, per_device(): other = lax.ppermute(own, 'dp', swap)  2.46 us
    ppermute x1, waiting for transfers between devices, per_device(): pieces = (mine + lax.ppermute(theirs, 'dp', swap).astype(F32)).astype(BF16)  1.67 us
    unnamed x17, local copies, waits for them, and re-layouts  1.67 us
  transfers between devices with their start and end apart: 16, of which 5 were waited for; matrix products, arithmetic and copies ran while one was open for 1% of the time, Pallas kernels for 10%

profile of v1, /device:TPU:0, one launch (start us, length us, event | category | flops | bytes accessed | tf_op | source)
XLA Modules:
  0.0 81.2 jit_solution(16434997898569792402)
XLA Ops:
  0.6 0.6 pad_add_fusion.where_ref
  1.3 3.4 %pick_rows.1 = (bf16[2,8,3584]{2,1,0:T(8,128)(2,1)}, bf16[2,8,3584]{2,1,0:T(8,128)(2,1)}, bf16[2,8,3584]{2,1,0:T(8,128)(2,1)}, bf16[2,8,3584]{2,1,0:T(8,128)(2,1...) custom-call(s32[2]{0:T(128)} %pad_add_fusion.where_ref, ...), custom_call_target="tpu_custom_call" | custom-call | flops 117440512 | bytes 2752512 | tf_op jit(solution)/shard_map/pick_rows/pallas_call | solution.py:146
  4.7 3.0 %collective-permute-start = (bf16[2,8,3584]{2,1,0:T(8,128)(2,1)}, bf16[2,8,3584]{2,1,0:T(8,128)(2,1)S(1)}, u32[]{:S(2)}, u32[]{:S(2)}) collective-permute-start(bf16[2,8,3584]{2,1,0:T(8,128)(2,1)} %get-tuple-element.23), channel_id=1, source_target_pairs={{0,2},{2,0},{4,6},{6,4},{8,10},{10,8},{12,14},{14,12},{1,3},{3,1},... | collective-permute-start | bytes 344072 | tf_op jit(solution)/shard_map/ppermute | solution.py:324
  7.7 1.6 %collective-permute-start.1 = (bf16[2,8,3584]{2,1,0:T(8,128)(2,1)}, bf16[2,8,3584]{2,1,0:T(8,128)(2,1)S(1)}, u32[]{:S(2)}, u32[]{:S(2)}) collective-permute-start(bf16[2,8,3584]{2,1,0:T(8,128)(2,1)} %get-tuple-element.24), channel_id=1, source_target_pairs={{0,4},{2,6},{4,0},{6,2},{8,12},{10,14},{12,8},{14,10},{1,5},{3,7},... | collective-permute-start | bytes 344072 | tf_op jit(solution)/shard_map/ppermute | solution.py:324
  9.3 0.0 collective-permute-start.2
  9.3 3.0 %collective-permute-start.3 = (bf16[2,8,3584]{2,1,0:T(8,128)(2,1)}, bf16[2,8,3584]{2,1,0:T(8,128)(2,1)S(1)}, u32[]{:S(2)}, u32[]{:S(2)}) collective-permute-start(bf16[2,8,3584]{2,1,0:T(8,128)(2,1)} %get-tuple-element.26), channel_id=1, source_target_pairs={{0,8},{2,10},{4,12},{6,14},{8,0},{10,2},{12,4},{14,6},{1,9},{3,11}... | collective-permute-start | bytes 344072 | tf_op jit(solution)/shard_map/ppermute | solution.py:324
  12.3 1.3 %collective-permute-start.4 = (bf16[2,8,3584]{2,1,0:T(8,128)(2,1)}, bf16[2,8,3584]{2,1,0:T(8,128)(2,1)S(1)}, u32[]{:S(2)}, u32[]{:S(2)}) collective-permute-start(bf16[2,8,3584]{2,1,0:T(8,128)(2,1)} %get-tuple-element.27), channel_id=1, source_target_pairs={{0,10},{2,8},{4,14},{6,12},{8,2},{10,0},{12,6},{14,4},{1,11},{3,9}... | collective-permute-start | bytes 344072 | tf_op jit(solution)/shard_map/ppermute | solution.py:324
  13.6 0.9 %constant_dynamic-update-slice_fusion.7 = bf16[2,64,3584]{2,1,0:T(8,128)(2,1)S(1)} fusion(bf16[2,8,3584]{2,1,0:T(8,128)(2,1)} %get-tuple-element.22), kind=kLoop, calls=%fused_computation.10 | loop fusion | bytes 229376
  14.5 0.0 collective-permute-done
  14.5 3.7 %collective-permute-start.5 = (bf16[2,8,3584]{2,1,0:T(8,128)(2,1)}, bf16[2,8,3584]{2,1,0:T(8,128)(2,1)S(1)}, u32[]{:S(2)}, u32[]{:S(2)}) collective-permute-start(bf16[2,8,3584]{2,1,0:T(8,128)(2,1)} %get-tuple-element.28), channel_id=1, source_target_pairs={{0,12},{2,14},{4,8},{6,10},{8,4},{10,6},{12,0},{14,2},{1,13},{3,15... | collective-permute-start | bytes 344072 | tf_op jit(solution)/shard_map/ppermute | solution.py:324
  18.2 0.0 collective-permute-done.1
  18.2 0.1 collective-permute-start.6
  18.3 0.0 collective-permute-done.2
  18.3 0.0 collective-permute-done.3
  18.3 11.4 %collective-permute-done.4 = bf16[2,8,3584]{2,1,0:T(8,128)(2,1)S(1)} collective-permute-done((bf16[2,8,3584]{2,1,0:T(8,128)(2,1)}, bf16[2,8,3584]{2,1,0:T(8,128)(2,1)S(1)}, u32[]{:S(2)}, u32[]{:S(2)}) %collective-permute-start.4) | collective-permute-done | bytes 114720 | tf_op jit(solution)/shard_map/ppermute | solution.py:324
  29.8 0.0 collective-permute-done.5
  29.8 0.0 collective-permute-done.6
  29.8 0.1 collective-permute-start.7
  29.9 2.5 %collective-permute-done.7.other_ref = bf16[2,64,3584]{2,1,0:T(8,128)(2,1)S(1)} collective-permute-done((bf16[2,64,3584]{2,1,0:T(8,128)(2,1)S(1)}, bf16[2,64,3584]{2,1,0:T(8,128)(2,1)S(1)}, u32[]{:S(2)}, u32[]{:S(2)}) %collective-permute-start.7) | collective-permute-done | bytes 917536 | tf_op jit(solution)/shard_map/ppermute | solution.py:331
  32.3 0.0 copy-start
  32.4 0.7 copy-done
  33.0 17.5 %activation_grads.1 = (bf16[128,1024]{1,0:T(8,128)(2,1)S(1)}, bf16[128,1024]{1,0:T(8,128)(2,1)S(1)}, bf16[128,1024]{1,0:T(8,128)(2,1)S(1)}, f32[64,3584]{1,0:T(8,128)S(1)}, bf16[64,3584]{1,0:T(8,128)(2,1)S(1)}) custom-call(s32[2]{0:T(128)S(1)} %copy-done, bf16[2,64,3584]{2,1,0:T(8,128)(2,1)S(1)} %constant_dynamic-update-slice_fusion.own_ref, ...), custom_call_target="tpu_custom_call" | custom-call | flops 4697620480 | bytes 22020096 | tf_op jit(solution)/shard_map/activation_grads/pallas_call | solution.py:222
  50.5 0.0 copy-start.1
  50.6 0.2 collective-permute-start.8
  50.8 1.7 %collective-permute-done.8 = bf16[64,3584]{1,0:T(8,128)(2,1)S(1)} collective-permute-done((bf16[64,3584]{1,0:T(8,128)(2,1)S(1)}, bf16[64,3584]{1,0:T(8,128)(2,1)S(1)}, u32[]{:S(2)}, u32[]{:S(2)}) %collective-permute-start.8) | collective-permute-done | bytes 458784 | tf_op jit(solution)/shard_map/ppermute | solution.py:335
  52.4 0.1 add_convert_fusion
  52.6 0.9 %collective-permute-start.9 = (bf16[8,3584]{1,0:T(8,128)(2,1)S(1)}, bf16[8,3584]{1,0:T(8,128)(2,1)S(1)}, u32[]{:S(2)}, u32[]{:S(2)}) collective-permute-start(bf16[8,3584]{1,0:T(8,128)(2,1)S(1)} %get-tuple-element.44), channel_id=1, source_target_pairs={{0,2},{2,0},{4,6},{6,4},{8,10},{10,8},{12,14},{14,12},{1,3},{3,1},... | collective-permute-start | bytes 172040 | tf_op jit(solution)/shard_map/ppermute | solution.py:324
  53.5 8.3 %weight_grads.1 = (bf16[1024,3584]{1,0:T(8,128)(2,1)}, bf16[1024,3584]{1,0:T(8,128)(2,1)}, bf16[1024,3584]{1,0:T(8,128)(2,1)}) custom-call(bf16[2,64,3584]{2,1,0:T(8,128)(2,1)S(1)} %constant_dynamic-update-slice_fusion.own_ref, bf16[2,64,3584]{2,1,0:T(8,128)(2,1)S(1)} %collective-permute-done.7.other_ref, bf16[128,1024]{1,0:T(8,128)(2,1)S(1)} %get-tuple-element.32.dh_ref, ...), custom_call_target="tpu_custom_call" | custom-call | flops 2818572288 | bytes 22020096 | tf_op jit(solution)/shard_map/weight_grads/pallas_call | solution.py:289
  61.8 3.6 %collective-permute-start.15 = (bf16[8,3584]{1,0:T(8,128)(2,1)S(1)}, bf16[8,3584]{1,0:T(8,128)(2,1)S(1)}, u32[]{:S(2)}, u32[]{:S(2)}) collective-permute-start(bf16[8,3584]{1,0:T(8,128)(2,1)S(1)} %get-tuple-element.38), channel_id=1, source_target_pairs={{0,14},{2,12},{4,10},{6,8},{8,6},{10,4},{12,2},{14,0},{1,15},{3,13... | collective-permute-start | bytes 172040 | tf_op jit(solution)/shard_map/ppermute | solution.py:324
  65.4 0.9 %collective-permute-start.14 = (bf16[8,3584]{1,0:T(8,128)(2,1)S(1)}, bf16[8,3584]{1,0:T(8,128)(2,1)S(1)}, u32[]{:S(2)}, u32[]{:S(2)}) collective-permute-start(bf16[8,3584]{1,0:T(8,128)(2,1)S(1)} %get-tuple-element.39), channel_id=1, source_target_pairs={{0,12},{2,14},{4,8},{6,10},{8,4},{10,6},{12,0},{14,2},{1,13},{3,15... | collective-permute-start | bytes 172040 | tf_op jit(solution)/shard_map/ppermute | solution.py:324
  66.2 4.1 %collective-permute-start.13 = (bf16[8,3584]{1,0:T(8,128)(2,1)S(1)}, bf16[8,3584]{1,0:T(8,128)(2,1)S(1)}, u32[]{:S(2)}, u32[]{:S(2)}) collective-permute-start(bf16[8,3584]{1,0:T(8,128)(2,1)S(1)} %get-tuple-element.40), channel_id=1, source_target_pairs={{0,10},{2,8},{4,14},{6,12},{8,2},{10,0},{12,6},{14,4},{1,11},{3,9}... | collective-permute-start | bytes 172040 | tf_op jit(solution)/shard_map/ppermute | solution.py:324
  70.3 0.0 collective-permute-start.12
  70.3 0.0 collective-permute-done.9
  70.3 1.6 %collective-permute-start.10 = (bf16[8,3584]{1,0:T(8,128)(2,1)S(1)}, bf16[8,3584]{1,0:T(8,128)(2,1)S(1)}, u32[]{:S(2)}, u32[]{:S(2)}) collective-permute-start(bf16[8,3584]{1,0:T(8,128)(2,1)S(1)} %get-tuple-element.43), channel_id=1, source_target_pairs={{0,4},{2,6},{4,0},{6,2},{8,12},{10,14},{12,8},{14,10},{1,5},{3,7},... | collective-permute-start | bytes 172040 | tf_op jit(solution)/shard_map/ppermute | solution.py:324
  71.9 2.8 %collective-permute-done.10 = bf16[8,3584]{1,0:T(8,128)(2,1)S(1)} collective-permute-done((bf16[8,3584]{1,0:T(8,128)(2,1)S(1)}, bf16[8,3584]{1,0:T(8,128)(2,1)S(1)}, u32[]{:S(2)}, u32[]{:S(2)}) %collective-permute-start.10) | collective-permute-done | bytes 57376 | tf_op jit(solution)/shard_map/ppermute | solution.py:324
  74.7 2.3 %collective-permute-start.11 = (bf16[8,3584]{1,0:T(8,128)(2,1)S(1)}, bf16[8,3584]{1,0:T(8,128)(2,1)S(1)}, u32[]{:S(2)}, u32[]{:S(2)}) collective-permute-start(bf16[8,3584]{1,0:T(8,128)(2,1)S(1)} %get-tuple-element.42), channel_id=1, source_target_pairs={{0,6},{2,4},{4,2},{6,0},{8,14},{10,12},{12,10},{14,8},{1,7},{3,5},... | collective-permute-start | bytes 172040 | tf_op jit(solution)/shard_map/ppermute | solution.py:324
  77.0 2.8 %collective-permute-done.11 = bf16[8,3584]{1,0:T(8,128)(2,1)S(1)} collective-permute-done((bf16[8,3584]{1,0:T(8,128)(2,1)S(1)}, bf16[8,3584]{1,0:T(8,128)(2,1)S(1)}, u32[]{:S(2)}, u32[]{:S(2)}) %collective-permute-start.11) | collective-permute-done | bytes 57376 | tf_op jit(solution)/shard_map/ppermute | solution.py:324
  79.8 0.0 collective-permute-done.12
  79.8 0.0 collective-permute-done.13
  79.8 0.0 collective-permute-done.14
  79.8 0.0 collective-permute-done.15
  79.9 0.0 copy-done.1
  79.9 1.3 %convolution_convert_fusion = bf16[128,3584]{1,0:T(8,128)(2,1)} fusion(bf16[64,128]{1,0:T(8,128)(2,1)S(1)} %copy-done.1, bf16[64,3584]{1,0:T(8,128)(2,1)S(1)} %constant_dynamic-update-slice_fusion.8), kind=kOutput, calls=%fused_computation | convolution fusion | flops 59179008 | bytes 1392640 | tf_op jit(solution)/shard_map/dot_general | solution.py:340
  (15 shorter events, 0.1 us)
Async XLA Ops:
  4.7 9.8 %collective-permute-start = (bf16[2,8,3584]{2,1,0:T(8,128)(2,1)}, bf16[2,8,3584]{2,1,0:T(8,128)(2,1)S(1)}, u32[]{:S(2)}, u32[]{:S(2)}) collective-permute-start(bf16[2,8,3584]{2,1,0:T(8,128)(2,1)} %get-tuple-element.23), channel_id=1, source_target_pairs={{0,2},{2,0},{4,6},{6,4},{8,10},{10,8},{12,14},{14,12},{1,3},{3,1},... | collective-permute-start | bytes 344072 | tf_op jit(solution)/shard_map/ppermute | solution.py:324
  7.7 10.4 %collective-permute-start.1 = (bf16[2,8,3584]{2,1,0:T(8,128)(2,1)}, bf16[2,8,3584]{2,1,0:T(8,128)(2,1)S(1)}, u32[]{:S(2)}, u32[]{:S(2)}) collective-permute-start(bf16[2,8,3584]{2,1,0:T(8,128)(2,1)} %get-tuple-element.24), channel_id=1, source_target_pairs={{0,4},{2,6},{4,0},{6,2},{8,12},{10,14},{12,8},{14,10},{1,5},{3,7},... | collective-permute-start | bytes 344072 | tf_op jit(solution)/shard_map/ppermute | solution.py:324
  9.3 9.0 %collective-permute-start.2 = (bf16[2,8,3584]{2,1,0:T(8,128)(2,1)}, bf16[2,8,3584]{2,1,0:T(8,128)(2,1)S(1)}, u32[]{:S(2)}, u32[]{:S(2)}) collective-permute-start(bf16[2,8,3584]{2,1,0:T(8,128)(2,1)} %get-tuple-element.25), channel_id=1, source_target_pairs={{0,6},{2,4},{4,2},{6,0},{8,14},{10,12},{12,10},{14,8},{1,7},{3,5},... | collective-permute-start | bytes 344072 | tf_op jit(solution)/shard_map/ppermute | solution.py:324
  9.3 9.0 %collective-permute-start.3 = (bf16[2,8,3584]{2,1,0:T(8,128)(2,1)}, bf16[2,8,3584]{2,1,0:T(8,128)(2,1)S(1)}, u32[]{:S(2)}, u32[]{:S(2)}) collective-permute-start(bf16[2,8,3584]{2,1,0:T(8,128)(2,1)} %get-tuple-element.26), channel_id=1, source_target_pairs={{0,8},{2,10},{4,12},{6,14},{8,0},{10,2},{12,4},{14,6},{1,9},{3,11}... | collective-permute-start | bytes 344072 | tf_op jit(solution)/shard_map/ppermute | solution.py:324
  12.3 17.4 %collective-permute-start.4 = (bf16[2,8,3584]{2,1,0:T(8,128)(2,1)}, bf16[2,8,3584]{2,1,0:T(8,128)(2,1)S(1)}, u32[]{:S(2)}, u32[]{:S(2)}) collective-permute-start(bf16[2,8,3584]{2,1,0:T(8,128)(2,1)} %get-tuple-element.27), channel_id=1, source_target_pairs={{0,10},{2,8},{4,14},{6,12},{8,2},{10,0},{12,6},{14,4},{1,11},{3,9}... | collective-permute-start | bytes 344072 | tf_op jit(solution)/shard_map/ppermute | solution.py:324
  14.5 15.3 %collective-permute-start.5 = (bf16[2,8,3584]{2,1,0:T(8,128)(2,1)}, bf16[2,8,3584]{2,1,0:T(8,128)(2,1)S(1)}, u32[]{:S(2)}, u32[]{:S(2)}) collective-permute-start(bf16[2,8,3584]{2,1,0:T(8,128)(2,1)} %get-tuple-element.28), channel_id=1, source_target_pairs={{0,12},{2,14},{4,8},{6,10},{8,4},{10,6},{12,0},{14,2},{1,13},{3,15... | collective-permute-start | bytes 344072 | tf_op jit(solution)/shard_map/ppermute | solution.py:324
  18.2 11.6 %collective-permute-start.6 = (bf16[2,8,3584]{2,1,0:T(8,128)(2,1)}, bf16[2,8,3584]{2,1,0:T(8,128)(2,1)S(1)}, u32[]{:S(2)}, u32[]{:S(2)}) collective-permute-start(bf16[2,8,3584]{2,1,0:T(8,128)(2,1)} %get-tuple-element.29), channel_id=1, source_target_pairs={{0,14},{2,12},{4,10},{6,8},{8,6},{10,4},{12,2},{14,0},{1,15},{3,13... | collective-permute-start | bytes 344072 | tf_op jit(solution)/shard_map/ppermute | solution.py:324
  29.8 2.5 %collective-permute-start.7 = (bf16[2,64,3584]{2,1,0:T(8,128)(2,1)S(1)}, bf16[2,64,3584]{2,1,0:T(8,128)(2,1)S(1)}, u32[]{:S(2)}, u32[]{:S(2)}) collective-permute-start(bf16[2,64,3584]{2,1,0:T(8,128)(2,1)S(1)} %constant_dynamic-update-slice_fusion.own_ref), channel_id=1, source_target_pairs={{0,1},{1,0},{2,3},{3,2},{4,5},{5,4},{6,7},{7,6},{8,9},{9,8},{10,11... | collective-permute-start | bytes 2752520 | tf_op jit(solution)/shard_map/ppermute | solution.py:331
  32.3 0.7 copy-start
  50.5 29.3 %copy-start.1 = (bf16[64,128]{1,0:T(8,128)(2,1)S(1)}, bf16[64,128]{1,0:T(8,128)(2,1)}, u32[]{:S(2)}) copy-start(bf16[64,128]{1,0:T(8,128)(2,1)} %get-tuple-element.21) | copy-start | bytes 49156
  50.6 1.9 %collective-permute-start.8 = (bf16[64,3584]{1,0:T(8,128)(2,1)S(1)}, bf16[64,3584]{1,0:T(8,128)(2,1)S(1)}, u32[]{:S(2)}, u32[]{:S(2)}) collective-permute-start(bf16[64,3584]{1,0:T(8,128)(2,1)S(1)} %get-tuple-element.31), channel_id=1, source_target_pairs={{0,1},{1,0},{2,3},{3,2},{4,5},{5,4},{6,7},{7,6},{8,9},{9,8},{10,11... | collective-permute-start | bytes 1376264 | tf_op jit(solution)/shard_map/ppermute | solution.py:335
  52.6 17.8 %collective-permute-start.9 = (bf16[8,3584]{1,0:T(8,128)(2,1)S(1)}, bf16[8,3584]{1,0:T(8,128)(2,1)S(1)}, u32[]{:S(2)}, u32[]{:S(2)}) collective-permute-start(bf16[8,3584]{1,0:T(8,128)(2,1)S(1)} %get-tuple-element.44), channel_id=1, source_target_pairs={{0,2},{2,0},{4,6},{6,4},{8,10},{10,8},{12,14},{14,12},{1,3},{3,1},... | collective-permute-start | bytes 172040 | tf_op jit(solution)/shard_map/ppermute | solution.py:324
  61.8 18.0 %collective-permute-start.15 = (bf16[8,3584]{1,0:T(8,128)(2,1)S(1)}, bf16[8,3584]{1,0:T(8,128)(2,1)S(1)}, u32[]{:S(2)}, u32[]{:S(2)}) collective-permute-start(bf16[8,3584]{1,0:T(8,128)(2,1)S(1)} %get-tuple-element.38), channel_id=1, source_target_pairs={{0,14},{2,12},{4,10},{6,8},{8,6},{10,4},{12,2},{14,0},{1,15},{3,13... | collective-permute-start | bytes 172040 | tf_op jit(solution)/shard_map/ppermute | solution.py:324
  65.4 14.4 %collective-permute-start.14 = (bf16[8,3584]{1,0:T(8,128)(2,1)S(1)}, bf16[8,3584]{1,0:T(8,128)(2,1)S(1)}, u32[]{:S(2)}, u32[]{:S(2)}) collective-permute-start(bf16[8,3584]{1,0:T(8,128)(2,1)S(1)} %get-tuple-element.39), channel_id=1, source_target_pairs={{0,12},{2,14},{4,8},{6,10},{8,4},{10,6},{12,0},{14,2},{1,13},{3,15... | collective-permute-start | bytes 172040 | tf_op jit(solution)/shard_map/ppermute | solution.py:324
  66.2 13.5 %collective-permute-start.13 = (bf16[8,3584]{1,0:T(8,128)(2,1)S(1)}, bf16[8,3584]{1,0:T(8,128)(2,1)S(1)}, u32[]{:S(2)}, u32[]{:S(2)}) collective-permute-start(bf16[8,3584]{1,0:T(8,128)(2,1)S(1)} %get-tuple-element.40), channel_id=1, source_target_pairs={{0,10},{2,8},{4,14},{6,12},{8,2},{10,0},{12,6},{14,4},{1,11},{3,9}... | collective-permute-start | bytes 172040 | tf_op jit(solution)/shard_map/ppermute | solution.py:324
  70.3 9.4 %collective-permute-start.12 = (bf16[8,3584]{1,0:T(8,128)(2,1)S(1)}, bf16[8,3584]{1,0:T(8,128)(2,1)S(1)}, u32[]{:S(2)}, u32[]{:S(2)}) collective-permute-start(bf16[8,3584]{1,0:T(8,128)(2,1)S(1)} %get-tuple-element.41), channel_id=1, source_target_pairs={{0,8},{2,10},{4,12},{6,14},{8,0},{10,2},{12,4},{14,6},{1,9},{3,11}... | collective-permute-start | bytes 172040 | tf_op jit(solution)/shard_map/ppermute | solution.py:324
  70.3 4.3 %collective-permute-start.10 = (bf16[8,3584]{1,0:T(8,128)(2,1)S(1)}, bf16[8,3584]{1,0:T(8,128)(2,1)S(1)}, u32[]{:S(2)}, u32[]{:S(2)}) collective-permute-start(bf16[8,3584]{1,0:T(8,128)(2,1)S(1)} %get-tuple-element.43), channel_id=1, source_target_pairs={{0,4},{2,6},{4,0},{6,2},{8,12},{10,14},{12,8},{14,10},{1,5},{3,7},... | collective-permute-start | bytes 172040 | tf_op jit(solution)/shard_map/ppermute | solution.py:324
  74.7 5.1 %collective-permute-start.11 = (bf16[8,3584]{1,0:T(8,128)(2,1)S(1)}, bf16[8,3584]{1,0:T(8,128)(2,1)S(1)}, u32[]{:S(2)}, u32[]{:S(2)}) collective-permute-start(bf16[8,3584]{1,0:T(8,128)(2,1)S(1)} %get-tuple-element.42), channel_id=1, source_target_pairs={{0,6},{2,4},{4,2},{6,0},{8,14},{10,12},{12,10},{14,8},{1,7},{3,5},... | collective-permute-start | bytes 172040 | tf_op jit(solution)/shard_map/ppermute | solution.py:324

commit v2 on v0

--- a/solution.py
+++ b/solution.py
@@ -1,10 +1,15 @@
 import jax
 import jax.numpy as jnp
 from jax import lax
+from jax.experimental import pallas as pl
+from jax.experimental.pallas import tpu as pltpu
 from jax.sharding import PartitionSpec as P
 
 FLIGHT = 8
 HOTCAP = 8
+F32 = jnp.float32
+BF16 = jnp.bfloat16
+MIB = 1 << 20
 
 
 def expert_pass(in_tokens, in_scaled, gate_rows, up_rows, down_rows):
@@ -30,7 +35,7 @@
     return (partials, (gate_term, up_term, down_term))
 
 
-def per_device(
+def per_device_general(
     tokens, grad_out, routing, gates, modality, hot_experts, gate_weight, up_weight, down_weight
 ):
     tok_count, model_width = tokens.shape
@@ -57,7 +62,6 @@
     picked_grad = jnp.einsum("scr,rd->scd", picker, grad_out, preferred_element_type=jnp.float32)
     slot_gate = jnp.sum(jnp.where(chooser, expert_gate.T[:, None, :], 0.0), axis=2)
     scaled = (picked_grad * slot_gate[:, :, None]).astype(jnp.bfloat16)
-    picked, scaled = (picked, scaled)
     send_shape = (devices, HOTCAP, model_width)
 
     def replicate_rows(block_data):
@@ -82,37 +86,335 @@
     grad_tokens = jnp.einsum(
         "fcr,fpcd->rd", chooser.astype(jnp.bfloat16), returned, preferred_element_type=jnp.float32
     )
-    summed = (
-        lax.psum_scatter(grad_terms[0], "dp", scatter_dimension=0, tiled=True),
-        lax.psum_scatter(grad_terms[1], "dp", scatter_dimension=0, tiled=True),
-        lax.psum_scatter(grad_terms[2], "dp", scatter_dimension=0, tiled=True),
-    )
-    return (
-        grad_tokens.astype(jnp.bfloat16),
-        summed[0].astype(jnp.bfloat16),
-        summed[1].astype(jnp.bfloat16),
-        summed[2].astype(jnp.bfloat16),
-    )
+    summed = tuple(
+        lax.psum_scatter(term, "dp", scatter_dimension=0, tiled=True) for term in grad_terms
+    )
+    return (grad_tokens.astype(jnp.bfloat16),) + tuple(term.astype(jnp.bfloat16) for term in summed)
+
+
+HOPS = (7, 4, 2, 1)
+
+
+def pick_tokens(where, hot_experts, tokens, routing, gates, modality):
+    tok_count, width = tokens.shape
+    top_count = routing.shape[1]
+    hot_count = hot_experts.shape[0]
+    slots = FLIGHT * HOTCAP
+    hops = len(HOPS)
+
+    def kernel(where_ref, hot_ref, tok_ref, route_ref, gate_ref, mod_ref, *outs):
+        keeps = outs[:hops]
+        give_ref, choose_ref, slot_gate_ref = outs[hops:]
+        position = lax.broadcasted_iota(jnp.int32, (top_count, tok_count), 0)
+        hot_pick = jnp.zeros((top_count, tok_count), jnp.int32)
+        for j in range(hot_count):
+            hot_pick = jnp.where(position == top_count - hot_count + j, hot_ref[j], hot_pick)
+        pinned = (mod_ref[...] == 1) & (position >= top_count - hot_count)
+        chosen = jnp.where(pinned, hot_pick, route_ref[...])
+        index = lax.broadcasted_iota(jnp.int32, (FLIGHT, top_count, tok_count), 0)
+        hop = jnp.zeros_like(index)
+        for k, value in enumerate(HOPS):
+            hop = jnp.where(index % hops == k, value, hop)
+        expert = hop ^ (index // hops) ^ where_ref[0] ^ where_ref[1]
+        matches = chosen[None] == expert
+        expert_gate = jnp.sum(jnp.where(matches, gate_ref[...][None], 0.0), axis=1)
+        present = jnp.sum(jnp.where(matches, 1.0, 0.0), axis=1)
+        before = lax.broadcasted_iota(jnp.int32, (tok_count, tok_count), 0)
+        after = lax.broadcasted_iota(jnp.int32, (tok_count, tok_count), 1)
+        upto = jnp.where(before <= after, 1.0, 0.0).astype(BF16)
+        placed = jnp.dot(present.astype(BF16), upto, preferred_element_type=F32)
+        slot = lax.broadcasted_iota(jnp.int32, (FLIGHT, HOTCAP, tok_count), 1) + 1
+        slot_hit = placed[:, None, :].astype(jnp.int32) == slot
+        chooser = slot_hit & (present[:, None, :] > 0.0)
+        picker = jnp.where(chooser, 1.0, 0.0).reshape(slots, tok_count).astype(BF16)
+        choose_ref[...] = picker
+        picked_gate = jnp.where(chooser, expert_gate[:, None, :], 0.0)
+        slot_gate_ref[...] = jnp.sum(picked_gate.reshape(slots, tok_count), axis=1, keepdims=True)
+        picked = jnp.dot(picker, tok_ref[...], preferred_element_type=F32)
+        for k in range(hops):
+            keeps[k][...] = picked[k * HOTCAP : (k + 1) * HOTCAP].astype(BF16)
+        give_ref[...] = picked[hops * HOTCAP :].astype(BF16)
+
+    smem = pl.BlockSpec(memory_space=pltpu.SMEM)
+    vmem = pl.BlockSpec(memory_space=pltpu.VMEM)
+    out = pl.pallas_call(
+        kernel,
+        out_shape=[jax.ShapeDtypeStruct((HOTCAP, width), BF16)] * hops
+        + [
+            jax.ShapeDtypeStruct((hops * HOTCAP, width), BF16),
+            jax.ShapeDtypeStruct((slots, tok_count), BF16),
+            jax.ShapeDtypeStruct((slots, 1), F32),
+        ],
+        in_specs=[smem, smem, vmem, vmem, vmem, vmem],
+        out_specs=[vmem] * (hops + 3),
+        cost_estimate=pl.CostEstimate(
+            flops=2 * slots * tok_count * width,
+            bytes_accessed=2 * (slots + tok_count) * width,
+            transcendentals=0,
+        ),
+        name="pick_tokens",
+    )(where, hot_experts, tokens, routing.T, gates.T, modality[None, :])
+    return out[:hops], out[hops], out[hops + 1], out[hops + 2]
+
+
+def pick_scaled(grad_out, picker, slot_gate):
+    tok_count, width = grad_out.shape
+    slots = picker.shape[0]
+    hops = len(HOPS)
+
+    def kernel(gout_ref, choose_ref, slot_gate_ref, *outs):
+        scaled = jnp.dot(choose_ref[...], gout_ref[...], preferred_element_type=F32)
+        scaled = scaled * slot_gate_ref[...]
+        for k in range(hops):
+            outs[k][...] = scaled[k * HOTCAP : (k + 1) * HOTCAP].astype(BF16)
+        outs[hops][...] = scaled[hops * HOTCAP :].astype(BF16)
+
+    vmem = pl.BlockSpec(memory_space=pltpu.VMEM)
+    out = pl.pallas_call(
+        kernel,
+        out_shape=[jax.ShapeDtypeStruct((HOTCAP, width), BF16)] * hops
+        + [jax.ShapeDtypeStruct((hops * HOTCAP, width), BF16)],
+        in_specs=[vmem] * 3,
+        out_specs=[vmem] * (hops + 1),
+        cost_estimate=pl.CostEstimate(
+            flops=2 * slots * tok_count * width,
+            bytes_accessed=2 * (slots + tok_count) * width,
+            transcendentals=0,
+        ),
+        name="pick_scaled",
+    )(grad_out, picker, slot_gate)
+    return out[:hops], out[hops]
+
+
+NT = (((1,), (1,)), ((), ()))
+TN = (((0,), (0,)), ((), ()))
+
+
+def pre_activations(where, own, other, gate_weight, up_weight):
+    rows, width = own.shape
+    half = gate_weight.shape[0] // 2
+    tile = min(256, half)
+    steps = half // tile
+
+    def kernel(where_ref, own_ref, other_ref, g_ref, u_ref, h_ref, u_out_ref, tok):
+        @pl.when(pl.program_id(0) == 0)
+        def _():
+            tok[:rows] = own_ref[...]
+            tok[rows:] = other_ref[...]
+
+        h_ref[...] = lax.dot_general(g_ref[...], tok[...], NT, preferred_element_type=F32)
+        u_out_ref[...] = lax.dot_general(u_ref[...], tok[...], NT, preferred_element_type=F32)
+
+    fixed = lambda i, w: (0, 0)
+    weight = pl.BlockSpec((tile, width), lambda i, w: (w[1] * steps + i, 0))
+    hidden = pl.BlockSpec((tile, 2 * rows), lambda i, w: (i, 0))
+    return pl.pallas_call(
+        kernel,
+        out_shape=[jax.ShapeDtypeStruct((half, 2 * rows), F32)] * 2,
+        grid_spec=pltpu.PrefetchScalarGridSpec(
+            num_scalar_prefetch=1,
+            grid=(steps,),
+            in_specs=[pl.BlockSpec((rows, width), fixed)] * 2 + [weight] * 2,
+            out_specs=[hidden] * 2,
+            scratch_shapes=[pltpu.VMEM((2 * rows, width), BF16)],
+        ),
+        compiler_params=pltpu.CompilerParams(vmem_limit_bytes=50 * MIB),
+        cost_estimate=pl.CostEstimate(
+            flops=8 * rows * half * width,
+            bytes_accessed=4 * half * width,
+            transcendentals=0,
+        ),
+        name="pre_activations",
+    )(where, own, other, gate_weight, up_weight)
+
+
+def activation_grads(where, own, other, h, u, gate_weight, up_weight, down_weight):
+    rows, width = own.shape
+    half = gate_weight.shape[0] // 2
+    tile = min(256, half)
+    steps = half // tile
+
+    def kernel(where_ref, own_ref, other_ref, h_in, u_in, g_ref, u_ref, w_ref, *rest):
+        dh_ref, du_ref, act_ref, mine_ref, theirs_ref, scl, acc = rest
+        step = pl.program_id(0)
+
+        @pl.when(step == 0)
+        def _():
+            scl[:rows] = own_ref[...]
+            scl[rows:] = other_ref[...]
+
+        da = lax.dot_general(w_ref[...], scl[...], NT, preferred_element_type=F32)
+        pre, up = h_in[...], u_in[...]
+        sig = jax.nn.sigmoid(pre)
+        swish = pre * sig
+        act_ref[...] = (swish * up).astype(BF16)
+        dh = (da * up * sig * (1.0 + pre * (1.0 - sig))).astype(BF16)
+        du = (da * swish).astype(BF16)
+        dh_ref[...] = dh
+        du_ref[...] = du
+        part = lax.dot_general(dh, g_ref[...], TN, preferred_element_type=F32)
+        part += lax.dot_general(du, u_ref[...], TN, preferred_element_type=F32)
+
+        @pl.when(step == 0)
+        def _():
+            acc[...] = part
+
+        @pl.when(step > 0)
+        def _():
+            acc[...] += part
+
+        @pl.when(step == steps - 1)
+        def _():
+            mine_ref[...] = acc[:rows]
+            theirs_ref[...] = acc[rows:].astype(BF16)
+
+    fixed = lambda i, w: (0, 0)
+    weight = pl.BlockSpec((tile, width), lambda i, w: (w[1] * steps + i, 0))
+    hidden = pl.BlockSpec((tile, 2 * rows), lambda i, w: (i, 0))
+    full = pl.BlockSpec((rows, width), fixed)
+    return pl.pallas_call(
+        kernel,
+        out_shape=[jax.ShapeDtypeStruct((half, 2 * rows), BF16)] * 3
+        + [
+            jax.ShapeDtypeStruct((rows, width), F32),
+            jax.ShapeDtypeStruct((rows, width), BF16),
+        ],
+        grid_spec=pltpu.PrefetchScalarGridSpec(
+            num_scalar_prefetch=1,
+            grid=(steps,),
+            in_specs=[full, full, hidden, hidden, weight, weight, weight],
+            out_specs=[hidden, hidden, hidden, full, full],
+            scratch_shapes=[
+                pltpu.VMEM((2 * rows, width), BF16),
+                pltpu.VMEM((2 * rows, width), F32),
+            ],
+        ),
+        compiler_params=pltpu.CompilerParams(vmem_limit_bytes=50 * MIB),
+        cost_estimate=pl.CostEstimate(
+            flops=12 * rows * half * width,
+            bytes_accessed=6 * half * width,
+            transcendentals=2 * rows * half,
+        ),
+        name="activation_grads",
+    )(where, own, other, h, u, gate_weight, up_weight, down_weight)
+
+
+def weight_grads(own_tok, other_tok, own_scl, other_scl, dh, du, act):
+    rows, width = own_tok.shape
+    half = dh.shape[0]
+    tile = min(256, half)
+    steps = half // tile
+
+    def kernel(own_t, other_t, own_s, other_s, dh_ref, du_ref, act_ref, *rest):
+        gg_ref, gu_ref, gd_ref, tok, scl = rest
+
+        @pl.when(pl.program_id(0) == 0)
+        def _():
+            tok[:rows] = own_t[...]
+            tok[rows:] = other_t[...]
+            scl[:rows] = own_s[...]
+            scl[rows:] = other_s[...]
+
+        for left, right, out in (
+            (dh_ref, tok, gg_ref),
+            (du_ref, tok, gu_ref),
+            (act_ref, scl, gd_ref),
+        ):
+            out[...] = jnp.dot(left[...], right[...], preferred_element_type=F32).astype(BF16)
+
+    full = pl.BlockSpec((rows, width), lambda i: (0, 0))
+    hidden = pl.BlockSpec((tile, 2 * rows), lambda i: (i, 0))
+    return pl.pallas_call(
+        kernel,
+        out_shape=[jax.ShapeDtypeStruct((half, width), BF16)] * 3,
+        grid=(steps,),
+        in_specs=[full] * 4 + [hidden] * 3,
+        out_specs=[pl.BlockSpec((tile, width), lambda i: (i, 0))] * 3,
+        scratch_shapes=[pltpu.VMEM((2 * rows, width), BF16)] * 2,
+        compiler_params=pltpu.CompilerParams(vmem_limit_bytes=50 * MIB),
+        cost_estimate=pl.CostEstimate(
+            flops=12 * rows * half * width,
+            bytes_accessed=6 * half * width,
+            transcendentals=0,
+        ),
+        name="weight_grads",
+    )(own_tok, other_tok, own_scl, other_scl, dh, du, act)
+
+
+def per_device(
+    tokens, grad_out, routing, gates, modality, hot_experts, gate_weight, up_weight, down_weight
+):
+    where = jnp.stack([lax.axis_index("expert"), lax.axis_index("dp")]).astype(jnp.int32)
+    hops = len(HOPS)
+
+    def swap(block):
+        return lax.ppermute(block, "dp", [(0, 1), (1, 0)])
+
+    def travel(block, hop):
+        moves = [
+            (2 * i + c, 2 * (i ^ hop ^ c) + c) for i in range(FLIGHT) for c in range(2)
+        ]
+        return lax.ppermute(block, ("expert", "dp"), moves)
+
+    def dispatch(keeps, give):
+        taken = swap(give)
+        got = []
+        for k, hop in enumerate(HOPS):
+            theirs = taken[k * HOTCAP : (k + 1) * HOTCAP]
+            got.append(travel(jnp.concatenate([keeps[k], theirs], axis=0), hop))
+        return got
+
+    tok_keeps, tok_give, picker, slot_gate = pick_tokens(
+        where, hot_experts, tokens, routing, gates, modality
+    )
+    scl_keeps, scl_give = pick_scaled(grad_out, picker, slot_gate)
+    own_tok = jnp.concatenate(dispatch(tok_keeps, tok_give), axis=0)
+    got_scl = dispatch(scl_keeps, scl_give)
+    other_tok = swap(own_tok)
+    h, u = pre_activations(where, own_tok, other_tok, gate_weight, up_weight)
+    got_scl, h, u = lax.optimization_barrier((got_scl, h, u))
+    own_scl = jnp.concatenate(got_scl, axis=0)
+    other_scl = swap(own_scl)
+    dh, du, act, mine, theirs = activation_grads(
+        where, own_scl, other_scl, h, u, gate_weight, up_weight, down_weight
+    )
+    pieces = (mine + swap(theirs).astype(F32)).astype(BF16)
+    back = []
+    for k, hop in enumerate(HOPS):
+        back.append(travel(pieces[2 * k * HOTCAP : 2 * (k + 1) * HOTCAP], hop))
+    grad_gate, grad_up, grad_down = weight_grads(
+        own_tok, other_tok, own_scl, other_scl, dh, du, act
+    )
+    back, grad_gate, grad_up, grad_down = lax.optimization_barrier(
+        (back, grad_gate, grad_up, grad_down)
+    )
+    kept = jnp.concatenate([block[:HOTCAP] for block in back], axis=0)
+    given = swap(jnp.concatenate([block[HOTCAP:] for block in back], axis=0))
+    grad_tokens = lax.dot_general(
+        picker, jnp.concatenate([kept, given], axis=0), TN, preferred_element_type=F32
+    ).astype(BF16)
+    return grad_tokens, grad_gate, grad_up, grad_down
 
 
 def solution(mesh):
+    sizes = dict(mesh.shape)
+    token_spec = P(("groups", "expert", "dp"), None)
     in_specs = (
-        P(("groups", "expert", "dp"), None),
-        P(("groups", "expert", "dp"), None),
-        P(("groups", "expert", "dp"), None),
-        P(("groups", "expert", "dp"), None),
+        token_spec,
+        token_spec,
+        token_spec,
+        token_spec,
         P(("groups", "expert", "dp")),
         P("groups"),
         P("expert", None),
         P("expert", None),
         P("expert", None),
     )
-    out_specs = (
-        P(("groups", "expert", "dp"), None),
-        P(("groups", "expert", "dp"), None),
-        P(("groups", "expert", "dp"), None),
-        P(("groups", "expert", "dp"), None),
-    )
+    paired = sizes["expert"] == FLIGHT and sizes["dp"] == 2
     return jax.shard_map(
-        per_device, mesh=mesh, in_specs=in_specs, out_specs=out_specs, check_vma=False
-    )
+        per_device if paired else per_device_general,
+        mesh=mesh,
+        in_specs=in_specs,
+        out_specs=(token_spec,) * 4,
+        check_vma=False,
+    )

time: 212 us -> 81.2 us (0.38)
  matrix products: 97.8 us -> 1.34 us
  Pallas kernels: 0 us -> 36.4 us
  waiting for transfers between devices: 35.4 us -> 5.25 us
  other arithmetic: 34.1 us -> 8.59 us
  blocking collectives: 18.5 us -> 0 us
  starting transfers between devices: 11.2 us -> 27.1 us
  between operations: 13.8 us -> 0.94 us
    dot_general x11 -> x1, matrix products: 97.8 us -> 1.34 us  [per_device(): lax.dot_general(picker, jnp.concatenate([kept, given], axis=0), TN, prefe...]
    pallas_call x0 -> x5, Pallas kernels: none -> 36.4 us  [the longest x1 14 us: activation_grads(): pl.pallas_call(kernel, out_shape=[jax.ShapeDtypeStruct((half, 2 * rows),...]
    convert_element_type x4 -> x1, other arithmetic: 30.8 us -> 1.3 us  [per_device(): pieces = (mine + swap(theirs).astype(F32)).astype(BF16)]
    ppermute x0 -> x18, starting transfers between devices: none -> 27.1 us  [the longest x12 26.3 us: travel(): return lax.ppermute(block, ('expert', 'dp'), moves)]
    reduce_scatter x3 -> x0, waiting for transfers between devices: 25.3 us -> none  [the longest x1 25.3 us: per_device(): lax.psum_scatter(grad_terms[0], 'dp', scatter_dimension=0, tiled=True)]
    all_to_all x1 -> x0, blocking collectives: 18.5 us -> none  [per_device(): lax.all_to_all(partials.reshape(send_shape), 'expert', split_axis=0, conc...]
    all_to_all x2 -> x0, starting transfers between devices: 10.9 us -> none  [the longest x1 7.25 us: per_device(): lax.all_to_all(replicate_rows(picked), 'expert', split_axis=0, concat_axi...]
    all_to_all x2 -> x0, waiting for transfers between devices: 10 us -> none  [the longest x1 10 us: per_device(): lax.all_to_all(replicate_rows(picked), 'expert', split_axis=0, concat_axi...]
  transfers between devices with their start and end apart: 5 -> 18, of which waited for: 2 -> 4; matrix products, arithmetic and copies ran while one was open for 51% -> 8% of each run, Pallas kernels for 0% -> 25%
where the time goes in v2:
time: 81.2 us; the launch traced here: 80.5 us
  Pallas kernels  36.4 us (45%)
  starting transfers between devices  27.1 us (33%)
  other arithmetic  8.59 us (11%)
  waiting for transfers between devices  5.25 us (6%)
  matrix products  1.34 us (2%)
  between operations  0.94 us (1%)
  local copies, waits for them, and re-layouts  0.86 us (1%)
    ppermute x12, starting transfers between devices, travel(): return lax.ppermute(block, ('expert', 'dp'), moves)  26.3 us
    pallas_call x1, Pallas kernels, activation_grads(): pl.pallas_call(kernel, out_shape=[jax.ShapeDtypeStruct((half, 2 * rows),...  14 us
    pallas_call x1, Pallas kernels, weight_grads(): pl.pallas_call(kernel, out_shape=[jax.ShapeDtypeStruct((half, width), BF1...  9.49 us
    pallas_call x1, Pallas kernels, pre_activations(): pl.pallas_call(kernel, out_shape=[jax.ShapeDtypeStruct((half, 2 * rows),...  8.29 us
    concatenate x8, other arithmetic, dispatch(): got.append(travel(jnp.concatenate([keeps[k], theirs], axis=0), hop))  6.62 us
    ppermute x6, waiting for transfers between devices, swap(): return lax.ppermute(block, 'dp', [(0, 1), (1, 0)])  4.96 us
    pallas_call x1, Pallas kernels, pick_tokens(): pl.pallas_call(kernel, out_shape=[jax.ShapeDtypeStruct((HOTCAP, width), B...  2.37 us
    pallas_call x1, Pallas kernels, pick_scaled(): pl.pallas_call(kernel, out_shape=[jax.ShapeDtypeStruct((HOTCAP, width), B...  2.23 us
  transfers between devices with their start and end apart: 18, of which 4 were waited for; matrix products, arithmetic and copies ran while one was open for 8% of the time, Pallas kernels for 25%

profile of v2, /device:TPU:0, one launch (start us, length us, event | category | flops | bytes accessed | tf_op | source)
XLA Modules:
  0.0 80.5 jit_solution(1046475009795292086)
XLA Ops:
  0.6 0.7 pad_add_fusion.where_ref
  1.3 2.4 %pick_tokens.1 = (bf16[8,3584]{1,0:T(8,128)(2,1)}, bf16[8,3584]{1,0:T(8,128)(2,1)}, bf16[8,3584]{1,0:T(8,128)(2,1)}, bf16[8,3584]{1,0:T(8,128)(2,1)}, bf16[32,35...) custom-call(s32[2]{0:T(128)} %pad_add_fusion.where_ref, s32[2]{0:T(128)} %hot_ref.1, ...), custom_call_target="tpu_custom_call" | custom-call | flops 58720256 | bytes 1376256 | tf_op jit(solution)/shard_map/pick_tokens/pallas_call | solution.py:140
  3.7 0.4 collective-permute-start.5
  4.1 2.2 %pick_scaled.1 = (bf16[8,3584]{1,0:T(8,128)(2,1)}, bf16[8,3584]{1,0:T(8,128)(2,1)}, bf16[8,3584]{1,0:T(8,128)(2,1)}, bf16[8,3584]{1,0:T(8,128)(2,1)}, bf16[32,3584]{1,0:T(8,128)(2,1)}) custom-call(bf16[128,3584]{1,0:T(8,128)(2,1)} %gout_ref.1, bf16[64,128]{1,0:T(8,128)(2,1)} %get-tuple-element.39.choose_ref, f32[64,1]{1,0:T(8,128)} %get-tuple-element.40.slot_gate_ref), custom_call_target="tpu_custom_call" | custom-call | flops 58720256 | bytes 1376256 | tf_op jit(solution)/shard_map/pick_scaled/pallas_call | solution.py:173
  6.3 0.1 collective-permute-start
  6.4 0.0 collective-permute-done.5
  6.4 0.8 %pad_maximum_fusion.5 = bf16[16,3584]{1,0:T(8,128)(2,1)S(1)} fusion(bf16[8,3584]{1,0:T(8,128)(2,1)S(1)} %get-tuple-element.81, bf16[8,3584]{1,0:T(8,128)(2,1)} %get-tuple-element.46), kind=kLoop, calls=%fused_computation.7 | loop fusion | flops 229376 | bytes 229376 | tf_op jit(solution)/shard_map/concatenate | solution.py:364
  7.2 6.0 %collective-permute-start.6 = (bf16[16,3584]{1,0:T(8,128)(2,1)S(1)}, bf16[16,3584]{1,0:T(8,128)(2,1)S(1)}, u32[]{:S(2)}, u32[]{:S(2)}) collective-permute-start(bf16[16,3584]{1,0:T(8,128)(2,1)S(1)} %pad_maximum_fusion.5), channel_id=1, source_target_pairs={{0,14},{1,13},{2,12},{3,15},{4,10},{5,9},{6,8},{7,11},{8,6},{9,5},... | collective-permute-start | bytes 344072 | tf_op jit(solution)/shard_map/ppermute | solution.py:357
  13.2 0.8 %pad_maximum_fusion.6 = bf16[16,3584]{1,0:T(8,128)(2,1)S(1)} fusion(bf16[8,3584]{1,0:T(8,128)(2,1)S(1)} %get-tuple-element.80, bf16[8,3584]{1,0:T(8,128)(2,1)} %get-tuple-element.48), kind=kLoop, calls=%fused_computation.8 | loop fusion | flops 229376 | bytes 229376 | tf_op jit(solution)/shard_map/concatenate | solution.py:364
  14.0 0.0 collective-permute-start.7
  14.1 0.8 %pad_maximum_fusion.7 = bf16[16,3584]{1,0:T(8,128)(2,1)S(1)} fusion(bf16[8,3584]{1,0:T(8,128)(2,1)S(1)} %get-tuple-element.79, bf16[8,3584]{1,0:T(8,128)(2,1)} %get-tuple-element.49), kind=kLoop, calls=%fused_computation.9 | loop fusion | flops 229376 | bytes 229376 | tf_op jit(solution)/shard_map/concatenate | solution.py:364
  14.9 0.8 collective-permute-start.8
  15.7 0.8 %pad_maximum_fusion.8 = bf16[16,3584]{1,0:T(8,128)(2,1)S(1)} fusion(bf16[8,3584]{1,0:T(8,128)(2,1)S(1)} %get-tuple-element.78, bf16[8,3584]{1,0:T(8,128)(2,1)} %get-tuple-element.50), kind=kLoop, calls=%fused_computation.10 | loop fusion | flops 229376 | bytes 229376 | tf_op jit(solution)/shard_map/concatenate | solution.py:364
  16.5 2.2 %collective-permute-start.9 = (bf16[16,3584]{1,0:T(8,128)(2,1)S(1)}, bf16[16,3584]{1,0:T(8,128)(2,1)S(1)}, u32[]{:S(2)}, u32[]{:S(2)}) collective-permute-start(bf16[16,3584]{1,0:T(8,128)(2,1)S(1)} %pad_maximum_fusion.8), channel_id=1, source_target_pairs={{0,2},{1,1},{2,0},{3,3},{4,6},{5,5},{6,4},{7,7},{8,10},{9,9},{10,8... | collective-permute-start | bytes 344072 | tf_op jit(solution)/shard_map/ppermute | solution.py:357
  18.7 0.0 collective-permute-done
  18.8 0.8 %pad_maximum_fusion.1 = bf16[16,3584]{1,0:T(8,128)(2,1)S(1)} fusion(bf16[8,3584]{1,0:T(8,128)(2,1)S(1)} %get-tuple-element.85, bf16[8,3584]{1,0:T(8,128)(2,1)} %get-tuple-element.41), kind=kLoop, calls=%fused_computation.3 | loop fusion | flops 229376 | bytes 229376 | tf_op jit(solution)/shard_map/concatenate | solution.py:364
  19.6 4.7 %collective-permute-start.1 = (bf16[16,3584]{1,0:T(8,128)(2,1)S(1)}, bf16[16,3584]{1,0:T(8,128)(2,1)S(1)}, u32[]{:S(2)}, u32[]{:S(2)}) collective-permute-start(bf16[16,3584]{1,0:T(8,128)(2,1)S(1)} %pad_maximum_fusion.1), channel_id=1, source_target_pairs={{0,14},{1,13},{2,12},{3,15},{4,10},{5,9},{6,8},{7,11},{8,6},{9,5},... | collective-permute-start | bytes 344072 | tf_op jit(solution)/shard_map/ppermute | solution.py:357
  24.3 0.8 %pad_maximum_fusion.2 = bf16[16,3584]{1,0:T(8,128)(2,1)S(1)} fusion(bf16[8,3584]{1,0:T(8,128)(2,1)S(1)} %get-tuple-element.84, bf16[8,3584]{1,0:T(8,128)(2,1)} %get-tuple-element.43), kind=kLoop, calls=%fused_computation.4 | loop fusion | flops 229376 | bytes 229376 | tf_op jit(solution)/shard_map/concatenate | solution.py:364
  25.1 0.0 collective-permute-done.6
  25.2 0.1 collective-permute-start.2
  25.2 0.3 collective-permute-done.7
  25.5 0.0 collective-permute-done.8
  25.6 0.1 collective-permute-start.10
  25.7 0.8 %pad_maximum_fusion.3 = bf16[16,3584]{1,0:T(8,128)(2,1)S(1)} fusion(bf16[8,3584]{1,0:T(8,128)(2,1)S(1)} %get-tuple-element.83, bf16[8,3584]{1,0:T(8,128)(2,1)} %get-tuple-element.44), kind=kLoop, calls=%fused_computation.5 | loop fusion | flops 229376 | bytes 229376 | tf_op jit(solution)/shard_map/concatenate | solution.py:364
  26.5 0.5 collective-permute-start.3
  27.0 0.8 %pad_maximum_fusion.4 = bf16[16,3584]{1,0:T(8,128)(2,1)S(1)} fusion(bf16[8,3584]{1,0:T(8,128)(2,1)S(1)} %get-tuple-element.82, bf16[8,3584]{1,0:T(8,128)(2,1)} %get-tuple-element.45), kind=kLoop, calls=%fused_computation.6 | loop fusion | flops 229376 | bytes 229376 | tf_op jit(solution)/shard_map/concatenate | solution.py:364
  27.8 4.1 %collective-permute-start.4 = (bf16[16,3584]{1,0:T(8,128)(2,1)S(1)}, bf16[16,3584]{1,0:T(8,128)(2,1)S(1)}, u32[]{:S(2)}, u32[]{:S(2)}) collective-permute-start(bf16[16,3584]{1,0:T(8,128)(2,1)S(1)} %pad_maximum_fusion.4), channel_id=1, source_target_pairs={{0,2},{1,1},{2,0},{3,3},{4,6},{5,5},{6,4},{7,7},{8,10},{9,9},{10,8... | collective-permute-start | bytes 344072 | tf_op jit(solution)/shard_map/ppermute | solution.py:357
  31.9 0.0 collective-permute-done.10.other_ref.other_t
  32.0 0.7 copy-done
  32.6 8.3 %pre_activations.1 = (f32[1024,128]{1,0:T(8,128)S(1)}, f32[1024,128]{1,0:T(8,128)S(1)}) custom-call(s32[2]{0:T(128)S(1)} %copy-done, bf16[64,3584]{1,0:T(8,128)(2,1)S(1)} %constant_dynamic-update-slice_fusion.own_ref.own_t, bf16[64,3584]{1,0:T(8,128)(2,1)S(1)} %collective-permute-done.10.other_ref.other_t, bf16[2048,3584]{1,0:T(8,128)(2,1)} %g_ref.3, ...), custom_call_target="tpu_custom_call" | custom-call | flops 1879048192 | bytes 14680064 | tf_op jit(solution)/shard_map/pre_activations/pallas_call | solution.py:211
  40.9 0.0 collective-permute-done.1
  41.0 0.0 collective-permute-done.4
  41.0 0.1 collective-permute-start.11
  41.1 1.8 %collective-permute-done.11.other_ref.other_s = bf16[64,3584]{1,0:T(8,128)(2,1)S(1)} collective-permute-done((bf16[64,3584]{1,0:T(8,128)(2,1)S(1)}, bf16[64,3584]{1,0:T(8,128)(2,1)S(1)}, u32[]{:S(2)}, u32[]{:S(2)}) %collective-permute-start.11) | collective-permute-done | bytes 458784 | tf_op jit(solution)/shard_map/ppermute | solution.py:351
  42.9 14.0 %activation_grads.1 = (bf16[1024,128]{1,0:T(8,128)(2,1)S(1)}, bf16[1024,128]{1,0:T(8,128)(2,1)S(1)}, bf16[1024,128]{1,0:T(8,128)(2,1)S(1)}, f32[64,3584]{1,0:T(8,128)}, bf16[64,3584]{1,0:T(8,128)(2,1)S(1)}) custom-call(s32[2]{0:T(128)S(1)} %copy-done.1, bf16[64,3584]{1,0:T(8,128)(2,1)S(1)} %constant_dynamic-update-slice_fusion.4.own_ref.own_s, ...), custom_call_target="tpu_custom_call" | custom-call | flops 2818572288 | bytes 22020096 | tf_op jit(solution)/shard_map/activation_grads/pallas_call | solution.py:275
  56.9 0.1 collective-permute-start.12
  57.1 1.7 %collective-permute-done.12 = bf16[64,3584]{1,0:T(8,128)(2,1)S(1)} collective-permute-done((bf16[64,3584]{1,0:T(8,128)(2,1)S(1)}, bf16[64,3584]{1,0:T(8,128)(2,1)S(1)}, u32[]{:S(2)}, u32[]{:S(2)}) %collective-permute-start.12) | collective-permute-done | bytes 458784 | tf_op jit(solution)/shard_map/ppermute | solution.py:351
  58.7 1.3 %add_convert_fusion = bf16[64,3584]{1,0:T(8,128)(2,1)S(1)} fusion(f32[64,3584]{1,0:T(8,128)} %get-tuple-element.59, bf16[64,3584]{1,0:T(8,128)(2,1)S(1)} %collective-permute-done.12), kind=kLoop, calls=%fused_computation.1 | loop fusion | flops 688128 | bytes 1835008 | tf_op jit(solution)/shard_map/convert_element_type | solution.py:381
  60.1 1.9 %collective-permute-start.16 = (bf16[16,3584]{1,0:T(8,128)(2,1)S(1)}, bf16[16,3584]{1,0:T(8,128)(2,1)S(1)}, u32[]{:S(2)}, u32[]{:S(2)}) collective-permute-start(bf16[16,3584]{1,0:T(8,128)(2,1)S(1)} %get-tuple-element.74), channel_id=1, source_target_pairs={{0,2},{1,1},{2,0},{3,3},{4,6},{5,5},{6,4},{7,7},{8,10},{9,9},{10,8... | collective-permute-start | bytes 344072 | tf_op jit(solution)/shard_map/ppermute | solution.py:357
  62.0 2.1 %collective-permute-start.15 = (bf16[16,3584]{1,0:T(8,128)(2,1)S(1)}, bf16[16,3584]{1,0:T(8,128)(2,1)S(1)}, u32[]{:S(2)}, u32[]{:S(2)}) collective-permute-start(bf16[16,3584]{1,0:T(8,128)(2,1)S(1)} %get-tuple-element.75), channel_id=1, source_target_pairs={{0,4},{1,7},{2,6},{3,5},{4,0},{5,3},{6,2},{7,1},{8,12},{9,15},{10,... | collective-permute-start | bytes 344072 | tf_op jit(solution)/shard_map/ppermute | solution.py:357
  64.1 2.0 %collective-permute-start.14 = (bf16[16,3584]{1,0:T(8,128)(2,1)S(1)}, bf16[16,3584]{1,0:T(8,128)(2,1)S(1)}, u32[]{:S(2)}, u32[]{:S(2)}) collective-permute-start(bf16[16,3584]{1,0:T(8,128)(2,1)S(1)} %get-tuple-element.76), channel_id=1, source_target_pairs={{0,8},{1,11},{2,10},{3,9},{4,12},{5,15},{6,14},{7,13},{8,0},{9,3},... | collective-permute-start | bytes 344072 | tf_op jit(solution)/shard_map/ppermute | solution.py:357
  66.0 1.9 %collective-permute-start.13 = (bf16[16,3584]{1,0:T(8,128)(2,1)S(1)}, bf16[16,3584]{1,0:T(8,128)(2,1)S(1)}, u32[]{:S(2)}, u32[]{:S(2)}) collective-permute-start(bf16[16,3584]{1,0:T(8,128)(2,1)S(1)} %get-tuple-element.77), channel_id=1, source_target_pairs={{0,14},{1,13},{2,12},{3,15},{4,10},{5,9},{6,8},{7,11},{8,6},{9,5},... | collective-permute-start | bytes 344072 | tf_op jit(solution)/shard_map/ppermute | solution.py:357
  68.0 9.5 %weight_grads.1 = (bf16[1024,3584]{1,0:T(8,128)(2,1)}, bf16[1024,3584]{1,0:T(8,128)(2,1)}, bf16[1024,3584]{1,0:T(8,128)(2,1)}) custom-call(bf16[64,3584]{1,0:T(8,128)(2,1)S(1)} %constant_dynamic-update-slice_fusion.own_ref.own_t, bf16[64,3584]{1,0:T(8,128)(2,1)S(1)} %collective-permute-done.10.other_ref.other_t, ...), custom_call_target="tpu_custom_call" | custom-call | flops 2818572288 | bytes 22020096 | tf_op jit(solution)/shard_map/weight_grads/pallas_call | solution.py:327
  77.5 0.0 collective-permute-done.16
  77.5 0.0 collective-permute-done.13
  77.6 0.1 collective-permute-start.17
  77.6 1.5 %collective-permute-done.17 = bf16[32,3584]{1,0:T(8,128)(2,1)S(1)} collective-permute-done((bf16[32,3584]{1,0:T(8,128)(2,1)S(1)}, bf16[32,3584]{1,0:T(8,128)(2,1)S(1)}, u32[]{:S(2)}, u32[]{:S(2)}) %collective-permute-start.17) | collective-permute-done | bytes 229408 | tf_op jit(solution)/shard_map/ppermute | solution.py:351
  79.2 1.3 %convolution_convert_fusion = bf16[128,3584]{1,0:T(8,128)(2,1)} fusion(bf16[64,128]{1,0:T(8,128)(2,1)S(1)} %copy-done.2, bf16[64,3584]{1,0:T(8,128)(2,1)S(1)} %constant_dynamic-update-slice_fusion.8), kind=kOutput, calls=%fused_computation | convolution fusion | flops 59179008 | bytes 1392640 | tf_op jit(solution)/shard_map/dot_general | solution.py:393
  (27 shorter events, 0.2 us)
Async XLA Ops:
  3.7 2.7 %collective-permute-start.5 = (bf16[32,3584]{1,0:T(8,128)(2,1)}, bf16[32,3584]{1,0:T(8,128)(2,1)S(1)}, u32[]{:S(2)}, u32[]{:S(2)}) collective-permute-start(bf16[32,3584]{1,0:T(8,128)(2,1)} %get-tuple-element.47), channel_id=1, source_target_pairs={{0,1},{1,0},{2,3},{3,2},{4,5},{5,4},{6,7},{7,6},{8,9},{9,8},{10,11... | collective-permute-start | bytes 688136 | tf_op jit(solution)/shard_map/ppermute | solution.py:351
  6.3 12.4 %collective-permute-start = (bf16[32,3584]{1,0:T(8,128)(2,1)}, bf16[32,3584]{1,0:T(8,128)(2,1)S(1)}, u32[]{:S(2)}, u32[]{:S(2)}) collective-permute-start(bf16[32,3584]{1,0:T(8,128)(2,1)} %get-tuple-element.42), channel_id=1, source_target_pairs={{0,1},{1,0},{2,3},{3,2},{4,5},{5,4},{6,7},{7,6},{8,9},{9,8},{10,11... | collective-permute-start | bytes 688136 | tf_op jit(solution)/shard_map/ppermute | solution.py:351
  7.2 17.9 %collective-permute-start.6 = (bf16[16,3584]{1,0:T(8,128)(2,1)S(1)}, bf16[16,3584]{1,0:T(8,128)(2,1)S(1)}, u32[]{:S(2)}, u32[]{:S(2)}) collective-permute-start(bf16[16,3584]{1,0:T(8,128)(2,1)S(1)} %pad_maximum_fusion.5), channel_id=1, source_target_pairs={{0,14},{1,13},{2,12},{3,15},{4,10},{5,9},{6,8},{7,11},{8,6},{9,5},... | collective-permute-start | bytes 344072 | tf_op jit(solution)/shard_map/ppermute | solution.py:357
  14.0 11.5 %collective-permute-start.7 = (bf16[16,3584]{1,0:T(8,128)(2,1)S(1)}, bf16[16,3584]{1,0:T(8,128)(2,1)S(1)}, u32[]{:S(2)}, u32[]{:S(2)}) collective-permute-start(bf16[16,3584]{1,0:T(8,128)(2,1)S(1)} %pad_maximum_fusion.6), channel_id=1, source_target_pairs={{0,8},{1,11},{2,10},{3,9},{4,12},{5,15},{6,14},{7,13},{8,0},{9,3},... | collective-permute-start | bytes 344072 | tf_op jit(solution)/shard_map/ppermute | solution.py:357
  14.9 10.6 %collective-permute-start.8 = (bf16[16,3584]{1,0:T(8,128)(2,1)S(1)}, bf16[16,3584]{1,0:T(8,128)(2,1)S(1)}, u32[]{:S(2)}, u32[]{:S(2)}) collective-permute-start(bf16[16,3584]{1,0:T(8,128)(2,1)S(1)} %pad_maximum_fusion.7), channel_id=1, source_target_pairs={{0,4},{1,7},{2,6},{3,5},{4,0},{5,3},{6,2},{7,1},{8,12},{9,15},{10,... | collective-permute-start | bytes 344072 | tf_op jit(solution)/shard_map/ppermute | solution.py:357
  16.5 9.1 %collective-permute-start.9 = (bf16[16,3584]{1,0:T(8,128)(2,1)S(1)}, bf16[16,3584]{1,0:T(8,128)(2,1)S(1)}, u32[]{:S(2)}, u32[]{:S(2)}) collective-permute-start(bf16[16,3584]{1,0:T(8,128)(2,1)S(1)} %pad_maximum_fusion.8), channel_id=1, source_target_pairs={{0,2},{1,1},{2,0},{3,3},{4,6},{5,5},{6,4},{7,7},{8,10},{9,9},{10,8... | collective-permute-start | bytes 344072 | tf_op jit(solution)/shard_map/ppermute | solution.py:357
  19.6 21.3 %collective-permute-start.1 = (bf16[16,3584]{1,0:T(8,128)(2,1)S(1)}, bf16[16,3584]{1,0:T(8,128)(2,1)S(1)}, u32[]{:S(2)}, u32[]{:S(2)}) collective-permute-start(bf16[16,3584]{1,0:T(8,128)(2,1)S(1)} %pad_maximum_fusion.1), channel_id=1, source_target_pairs={{0,14},{1,13},{2,12},{3,15},{4,10},{5,9},{6,8},{7,11},{8,6},{9,5},... | collective-permute-start | bytes 344072 | tf_op jit(solution)/shard_map/ppermute | solution.py:357
  25.2 15.8 %collective-permute-start.2 = (bf16[16,3584]{1,0:T(8,128)(2,1)S(1)}, bf16[16,3584]{1,0:T(8,128)(2,1)S(1)}, u32[]{:S(2)}, u32[]{:S(2)}) collective-permute-start(bf16[16,3584]{1,0:T(8,128)(2,1)S(1)} %pad_maximum_fusion.2), channel_id=1, source_target_pairs={{0,8},{1,11},{2,10},{3,9},{4,12},{5,15},{6,14},{7,13},{8,0},{9,3},... | collective-permute-start | bytes 344072 | tf_op jit(solution)/shard_map/ppermute | solution.py:357
  25.6 6.4 %collective-permute-start.10 = (bf16[64,3584]{1,0:T(8,128)(2,1)S(1)}, bf16[64,3584]{1,0:T(8,128)(2,1)S(1)}, u32[]{:S(2)}, u32[]{:S(2)}) collective-permute-start(bf16[64,3584]{1,0:T(8,128)(2,1)S(1)} %constant_dynamic-update-slice_fusion.own_ref.own_t), channel_id=1, source_target_pairs={{0,1},{1,0},{2,3},{3,2},{4,5},{5,4},{6,7},{7,6},{8,9},{9,8},{10,11... | collective-permute-start | bytes 1376264 | tf_op jit(solution)/shard_map/ppermute | solution.py:351
  26.5 14.5 %collective-permute-start.3 = (bf16[16,3584]{1,0:T(8,128)(2,1)S(1)}, bf16[16,3584]{1,0:T(8,128)(2,1)S(1)}, u32[]{:S(2)}, u32[]{:S(2)}) collective-permute-start(bf16[16,3584]{1,0:T(8,128)(2,1)S(1)} %pad_maximum_fusion.3), channel_id=1, source_target_pairs={{0,4},{1,7},{2,6},{3,5},{4,0},{5,3},{6,2},{7,1},{8,12},{9,15},{10,... | collective-permute-start | bytes 344072 | tf_op jit(solution)/shard_map/ppermute | solution.py:357
  27.0 15.9 %copy-start.1 = (s32[2]{0:T(128)S(1)}, s32[2]{0:T(128)}, u32[]{:S(2)}) copy-start(s32[2]{0:T(128)} %pad_add_fusion.where_ref) | copy-start | bytes 28
  27.8 13.1 %collective-permute-start.4 = (bf16[16,3584]{1,0:T(8,128)(2,1)S(1)}, bf16[16,3584]{1,0:T(8,128)(2,1)S(1)}, u32[]{:S(2)}, u32[]{:S(2)}) collective-permute-start(bf16[16,3584]{1,0:T(8,128)(2,1)S(1)} %pad_maximum_fusion.4), channel_id=1, source_target_pairs={{0,2},{1,1},{2,0},{3,3},{4,6},{5,5},{6,4},{7,7},{8,10},{9,9},{10,8... | collective-permute-start | bytes 344072 | tf_op jit(solution)/shard_map/ppermute | solution.py:357
  32.0 0.7 copy-start
  41.0 1.9 %collective-permute-start.11 = (bf16[64,3584]{1,0:T(8,128)(2,1)S(1)}, bf16[64,3584]{1,0:T(8,128)(2,1)S(1)}, u32[]{:S(2)}, u32[]{:S(2)}) collective-permute-start(bf16[64,3584]{1,0:T(8,128)(2,1)S(1)} %constant_dynamic-update-slice_fusion.4.own_ref.own_s), channel_id=1, source_target_pairs={{0,1},{1,0},{2,3},{3,2},{4,5},{5,4},{6,7},{7,6},{8,9},{9,8},{10,11... | collective-permute-start | bytes 1376264 | tf_op jit(solution)/shard_map/ppermute | solution.py:351
  56.9 1.8 %collective-permute-start.12 = (bf16[64,3584]{1,0:T(8,128)(2,1)S(1)}, bf16[64,3584]{1,0:T(8,128)(2,1)S(1)}, u32[]{:S(2)}, u32[]{:S(2)}) collective-permute-start(bf16[64,3584]{1,0:T(8,128)(2,1)S(1)} %get-tuple-element.60), channel_id=1, source_target_pairs={{0,1},{1,0},{2,3},{3,2},{4,5},{5,4},{6,7},{7,6},{8,9},{9,8},{10,11... | collective-permute-start | bytes 1376264 | tf_op jit(solution)/shard_map/ppermute | solution.py:351
  58.7 20.4 %copy-start.2 = (bf16[64,128]{1,0:T(8,128)(2,1)S(1)}, bf16[64,128]{1,0:T(8,128)(2,1)}, u32[]{:S(2)}) copy-start(bf16[64,128]{1,0:T(8,128)(2,1)} %get-tuple-element.39.choose_ref) | copy-start | bytes 49156
  60.1 17.4 %collective-permute-start.16 = (bf16[16,3584]{1,0:T(8,128)(2,1)S(1)}, bf16[16,3584]{1,0:T(8,128)(2,1)S(1)}, u32[]{:S(2)}, u32[]{:S(2)}) collective-permute-start(bf16[16,3584]{1,0:T(8,128)(2,1)S(1)} %get-tuple-element.74), channel_id=1, source_target_pairs={{0,2},{1,1},{2,0},{3,3},{4,6},{5,5},{6,4},{7,7},{8,10},{9,9},{10,8... | collective-permute-start | bytes 344072 | tf_op jit(solution)/shard_map/ppermute | solution.py:357
  62.0 15.4 %collective-permute-start.15 = (bf16[16,3584]{1,0:T(8,128)(2,1)S(1)}, bf16[16,3584]{1,0:T(8,128)(2,1)S(1)}, u32[]{:S(2)}, u32[]{:S(2)}) collective-permute-start(bf16[16,3584]{1,0:T(8,128)(2,1)S(1)} %get-tuple-element.75), channel_id=1, source_target_pairs={{0,4},{1,7},{2,6},{3,5},{4,0},{5,3},{6,2},{7,1},{8,12},{9,15},{10,... | collective-permute-start | bytes 344072 | tf_op jit(solution)/shard_map/ppermute | solution.py:357
  64.1 13.4 %collective-permute-start.14 = (bf16[16,3584]{1,0:T(8,128)(2,1)S(1)}, bf16[16,3584]{1,0:T(8,128)(2,1)S(1)}, u32[]{:S(2)}, u32[]{:S(2)}) collective-permute-start(bf16[16,3584]{1,0:T(8,128)(2,1)S(1)} %get-tuple-element.76), channel_id=1, source_target_pairs={{0,8},{1,11},{2,10},{3,9},{4,12},{5,15},{6,14},{7,13},{8,0},{9,3},... | collective-permute-start | bytes 344072 | tf_op jit(solution)/shard_map/ppermute | solution.py:357
  66.0 11.4 %collective-permute-start.13 = (bf16[16,3584]{1,0:T(8,128)(2,1)S(1)}, bf16[16,3584]{1,0:T(8,128)(2,1)S(1)}, u32[]{:S(2)}, u32[]{:S(2)}) collective-permute-start(bf16[16,3584]{1,0:T(8,128)(2,1)S(1)} %get-tuple-element.77), channel_id=1, source_target_pairs={{0,14},{1,13},{2,12},{3,15},{4,10},{5,9},{6,8},{7,11},{8,6},{9,5},... | collective-permute-start | bytes 344072 | tf_op jit(solution)/shard_map/ppermute | solution.py:357
  77.6 1.6 %collective-permute-start.17 = (bf16[32,3584]{1,0:T(8,128)(2,1)S(1)}, bf16[32,3584]{1,0:T(8,128)(2,1)S(1)}, u32[]{:S(2)}, u32[]{:S(2)}) collective-permute-start(bf16[32,3584]{1,0:T(8,128)(2,1)S(1)} %pad_maximum_fusion), channel_id=1, source_target_pairs={{0,1},{1,0},{2,3},{3,2},{4,5},{5,4},{6,7},{7,6},{8,9},{9,8},{10,11... | collective-permute-start | bytes 688136 | tf_op jit(solution)/shard_map/ppermute | solution.py:351

commit v3 on v0

--- a/solution.py
+++ b/solution.py
@@ -1,10 +1,15 @@
 import jax
 import jax.numpy as jnp
 from jax import lax
+from jax.experimental import pallas as pl
+from jax.experimental.pallas import tpu as pltpu
 from jax.sharding import PartitionSpec as P
 
 FLIGHT = 8
 HOTCAP = 8
+F32 = jnp.float32
+BF16 = jnp.bfloat16
+MIB = 1 << 20
 
 
 def expert_pass(in_tokens, in_scaled, gate_rows, up_rows, down_rows):
@@ -30,7 +35,7 @@
     return (partials, (gate_term, up_term, down_term))
 
 
-def per_device(
+def per_device_general(
     tokens, grad_out, routing, gates, modality, hot_experts, gate_weight, up_weight, down_weight
 ):
     tok_count, model_width = tokens.shape
@@ -57,7 +62,6 @@
     picked_grad = jnp.einsum("scr,rd->scd", picker, grad_out, preferred_element_type=jnp.float32)
     slot_gate = jnp.sum(jnp.where(chooser, expert_gate.T[:, None, :], 0.0), axis=2)
     scaled = (picked_grad * slot_gate[:, :, None]).astype(jnp.bfloat16)
-    picked, scaled = (picked, scaled)
     send_shape = (devices, HOTCAP, model_width)
 
     def replicate_rows(block_data):
@@ -82,37 +86,344 @@
     grad_tokens = jnp.einsum(
         "fcr,fpcd->rd", chooser.astype(jnp.bfloat16), returned, preferred_element_type=jnp.float32
     )
-    summed = (
-        lax.psum_scatter(grad_terms[0], "dp", scatter_dimension=0, tiled=True),
-        lax.psum_scatter(grad_terms[1], "dp", scatter_dimension=0, tiled=True),
-        lax.psum_scatter(grad_terms[2], "dp", scatter_dimension=0, tiled=True),
-    )
-    return (
-        grad_tokens.astype(jnp.bfloat16),
-        summed[0].astype(jnp.bfloat16),
-        summed[1].astype(jnp.bfloat16),
-        summed[2].astype(jnp.bfloat16),
-    )
+    summed = tuple(
+        lax.psum_scatter(term, "dp", scatter_dimension=0, tiled=True) for term in grad_terms
+    )
+    return (grad_tokens.astype(jnp.bfloat16),) + tuple(term.astype(jnp.bfloat16) for term in summed)
+
+
+HOPS = (7, 4, 2, 1)
+FAR = 2
+CARRIED = len(HOPS) * HOTCAP
+NT = (((1,), (1,)), ((), ()))
+SMEM = pl.BlockSpec(memory_space=pltpu.SMEM)
+VMEM = pl.BlockSpec(memory_space=pltpu.VMEM)
+HBM = pl.BlockSpec(memory_space=pltpu.HBM)
+
+
+def route(hot_experts, routing, gates, modality, tokens, grad_out):
+    tok_count, top_count = routing.shape
+    hot_count = hot_experts.shape[0]
+    slots = FLIGHT * HOTCAP
+    hops = len(HOPS)
+
+    def kernel(hot_ref, route_ref, gate_ref, mod_ref, tok_in, gout_in, *rest):
+        choose_ref, keep_ref, give_ref, tok_ref, gout_ref, sem = rest
+        loads = (
+            pltpu.make_async_copy(tok_in, tok_ref, sem.at[0]),
+            pltpu.make_async_copy(gout_in, gout_ref, sem.at[1]),
+        )
+        for load in loads:
+            load.start()
+        position = lax.broadcasted_iota(jnp.int32, (top_count, tok_count), 0)
+        hot_pick = jnp.zeros((top_count, tok_count), jnp.int32)
+        for j in range(hot_count):
+            hot_pick = jnp.where(position == top_count - hot_count + j, hot_ref[j], hot_pick)
+        pinned = (mod_ref[...] == 1) & (position >= top_count - hot_count)
+        chosen = jnp.where(pinned, hot_pick, route_ref[...])
+        index = lax.broadcasted_iota(jnp.int32, (FLIGHT, top_count, tok_count), 0)
+        hop = jnp.zeros_like(index)
+        for k, value in enumerate(HOPS):
+            hop = jnp.where(index % hops == k, value, hop)
+        expert = hop ^ (index // hops) ^ lax.axis_index("expert") ^ lax.axis_index("dp")
+        matches = chosen[None] == expert
+        expert_gate = jnp.sum(jnp.where(matches, gate_ref[...][None], 0.0), axis=1)
+        present = jnp.sum(jnp.where(matches, 1.0, 0.0), axis=1)
+        before = lax.broadcasted_iota(jnp.int32, (tok_count, tok_count), 0)
+        after = lax.broadcasted_iota(jnp.int32, (tok_count, tok_count), 1)
+        upto = jnp.where(before <= after, 1.0, 0.0).astype(BF16)
+        placed = jnp.dot(present.astype(BF16), upto, preferred_element_type=F32)
+        slot = lax.broadcasted_iota(jnp.int32, (FLIGHT, HOTCAP, tok_count), 1) + 1
+        slot_hit = placed[:, None, :].astype(jnp.int32) == slot
+        chooser = slot_hit & (present[:, None, :] > 0.0)
+        picker = jnp.where(chooser, 1.0, 0.0).reshape(slots, tok_count)
+        gated = jnp.where(chooser, expert_gate[:, None, :], 0.0).reshape(slots, tok_count)
+        choose_ref[...] = picker.astype(BF16)
+        keep_ref[...] = gated[:CARRIED]
+        give_ref[...] = gated[CARRIED:]
+        for load in loads:
+            load.wait()
+
+    return pl.pallas_call(
+        kernel,
+        out_shape=[
+            pltpu.VMEM((slots, tok_count), BF16),
+            pltpu.VMEM((CARRIED, tok_count), F32),
+            pltpu.VMEM((slots - CARRIED, tok_count), F32),
+            pltpu.VMEM(tokens.shape, BF16),
+            pltpu.VMEM(grad_out.shape, BF16),
+        ],
+        in_specs=[SMEM, VMEM, VMEM, VMEM, HBM, HBM],
+        out_specs=[VMEM] * 5,
+        scratch_shapes=[pltpu.SemaphoreType.DMA((2,))],
+        name="route",
+    )(
+        hot_experts,
+        routing.T,
+        gates.T,
+        modality[None, :],
+        pltpu.with_memory_space_constraint(tokens, pltpu.HBM),
+        pltpu.with_memory_space_constraint(grad_out, pltpu.HBM),
+    )
+
+
+def pick(slots, tokens, grads, parts, work, name):
+    tok_count, width = tokens[0].shape
+    sources = [rows for rows in (tokens, grads) if rows is not None]
+
+    def kernel(*refs):
+        outs = refs[2 + 2 * len(sources) :]
+        for core in range(2):
+            gated = refs[core][...]
+            picker = jnp.where(gated != 0.0, 1.0, 0.0).astype(BF16)
+            first = min(k for k, _ in parts) * HOTCAP
+            picker = picker[first:]
+            gate = jnp.sum(gated[first:], axis=1, keepdims=True)
+            rows = [
+                jnp.dot(picker, refs[2 + 2 * n + core][...], preferred_element_type=F32)
+                for n in range(len(sources))
+            ]
+            if grads is not None:
+                rows[1] = rows[1] * gate
+            for (k, carried), out in zip(parts, outs):
+                slot = slice(k * HOTCAP - first, (k + 1) * HOTCAP - first)
+                for place, n in enumerate(carried):
+                    start = (2 * place + core) * HOTCAP
+                    out[start : start + HOTCAP] = rows[n][slot].astype(BF16)
+
+    return pl.pallas_call(
+        kernel,
+        out_shape=[
+            pltpu.VMEM((2 * HOTCAP * len(carried), width), BF16) for _, carried in parts
+        ],
+        in_specs=[VMEM] * (2 + 2 * len(sources)),
+        out_specs=[VMEM] * len(parts),
+        compiler_params=pltpu.CompilerParams(vmem_limit_bytes=16 * MIB),
+        cost_estimate=pl.CostEstimate(
+            flops=4 * work * CARRIED * tok_count * width,
+            bytes_accessed=4 * work * (CARRIED + tok_count) * width,
+            transcendentals=0,
+        ),
+        name=name,
+    )(*slots, *(block for pair in sources for block in pair))
+
+
+def pre_activations(own, other, gate_weight, up_weight, down_weight):
+    rows, width = own.shape
+    half = gate_weight.shape[0] // 2
+    tile = min(256, half)
+    steps = half // tile
+
+    def kernel(own_ref, other_ref, g_in, u_in, w_in, h_ref, up_ref, g_ref, u_ref, w_ref, *rest):
+        columns, sem = rest
+        first = pl.multiple_of(lax.axis_index("dp") * half, half)
+        order = [(lane, i) for i in range(steps) for lane in (0, 1)]
+        order += [(2, i) for i in range(steps)]
+
+        def load(lane, i):
+            source, target = ((g_in, g_ref), (u_in, u_ref), (w_in, w_ref))[lane]
+            return pltpu.make_async_copy(
+                source.at[pl.ds(first + i * tile, tile)],
+                target.at[pl.ds(i * tile, tile)],
+                sem.at[lane, i],
+            )
+
+        depth = 3
+        for lane, i in order[:depth]:
+            load(lane, i).start()
+        columns[:, :rows] = own_ref[...].T
+        columns[:, rows:] = other_ref[...].T
+        for n, (lane, i) in enumerate(order):
+            load(lane, i).wait()
+            if n + depth < len(order):
+                load(*order[n + depth]).start()
+            if lane < 2:
+                part = slice(i * tile, (i + 1) * tile)
+                weight, out = ((g_ref, h_ref), (u_ref, up_ref))[lane]
+                out[part] = jnp.dot(weight[part], columns[...], preferred_element_type=F32)
+
+    return pl.pallas_call(
+        kernel,
+        out_shape=[pltpu.VMEM((half, 2 * rows), F32)] * 2
+        + [pltpu.VMEM((half, width), BF16)] * 3,
+        in_specs=[VMEM, VMEM, HBM, HBM, HBM],
+        out_specs=[VMEM] * 5,
+        scratch_shapes=[
+            pltpu.VMEM((width, 2 * rows), BF16),
+            pltpu.SemaphoreType.DMA((3, steps)),
+        ],
+        compiler_params=pltpu.CompilerParams(vmem_limit_bytes=12 * MIB),
+        cost_estimate=pl.CostEstimate(flops=1000, bytes_accessed=1000, transcendentals=0),
+        name="pre_activations",
+    )(
+        own,
+        other,
+        *(
+            pltpu.with_memory_space_constraint(weight, pltpu.HBM)
+            for weight in (gate_weight, up_weight, down_weight)
+        ),
+    )
+
+
+def activation_grads(own, other, h, u, gate_half, up_half, down_half):
+    rows, width = own.shape
+    half = h.shape[0]
+    tile = min(256, half)
+    chunk = 512 if width % 512 == 0 else width
+
+    def kernel(own_ref, other_ref, h_ref, up_ref, g_ref, u_ref, w_ref, *rest):
+        dh_ref, du_ref, act_ref, mine_ref, theirs_ref, scl, dh_rows, du_rows = rest
+        scl[:rows] = own_ref[...]
+        scl[rows:] = other_ref[...]
+        for i in range(half // tile):
+            part = slice(i * tile, (i + 1) * tile)
+            da = lax.dot_general(w_ref[part], scl[...], NT, preferred_element_type=F32)
+            pre, up = h_ref[part], up_ref[part]
+            sig = jax.nn.sigmoid(pre)
+            swish = pre * sig
+            act_ref[part] = (swish * up).astype(BF16)
+            dh = (da * up * sig * (1.0 + pre * (1.0 - sig))).astype(BF16)
+            du = (da * swish).astype(BF16)
+            dh_ref[part] = dh
+            du_ref[part] = du
+            dh_rows[:, part] = dh.T
+            du_rows[:, part] = du.T
+        for c in range(0, width, chunk):
+            cols = slice(c, c + chunk)
+            piece = jnp.dot(dh_rows[...], g_ref[:, cols], preferred_element_type=F32)
+            piece += jnp.dot(du_rows[...], u_ref[:, cols], preferred_element_type=F32)
+            mine_ref[:, cols] = piece[:rows]
+            theirs_ref[:, cols] = piece[rows:].astype(BF16)
+
+    return pl.pallas_call(
+        kernel,
+        out_shape=[pltpu.VMEM((half, 2 * rows), BF16)] * 3
+        + [pltpu.VMEM((rows, width), F32), pltpu.VMEM((rows, width), BF16)],
+        in_specs=[VMEM] * 7,
+        out_specs=[VMEM] * 5,
+        scratch_shapes=[
+            pltpu.VMEM((2 * rows, width), BF16),
+            pltpu.VMEM((2 * rows, half), BF16),
+            pltpu.VMEM((2 * rows, half), BF16),
+        ],
+        compiler_params=pltpu.CompilerParams(vmem_limit_bytes=12 * MIB),
+        cost_estimate=pl.CostEstimate(
+            flops=12 * rows * half * width,
+            bytes_accessed=6 * half * width,
+            transcendentals=2 * rows * half,
+        ),
+        name="activation_grads",
+    )(own, other, h, u, gate_half, up_half, down_half)
+
+
+def weight_grads(own, other, lefts, name):
+    rows, width = own.shape
+    half = lefts[0].shape[0]
+    tile = min(256, half)
+    count = len(lefts)
+
+    def kernel(own_ref, other_ref, *rest):
+        sides, outs, both = rest[:count], rest[count : 2 * count], rest[2 * count]
+
+        @pl.when(pl.program_id(0) == 0)
+        def _():
+            both[:rows] = own_ref[...]
+            both[rows:] = other_ref[...]
+
+        for left, out in zip(sides, outs):
+            out[...] = jnp.dot(left[...], both[...], preferred_element_type=F32).astype(BF16)
+
+    full = pl.BlockSpec((rows, width), lambda i: (0, 0))
+    hidden = pl.BlockSpec((tile, 2 * rows), lambda i: (i, 0))
+    return pl.pallas_call(
+        kernel,
+        out_shape=[jax.ShapeDtypeStruct((half, width), BF16)] * count,
+        grid=(half // tile,),
+        in_specs=[full] * 2 + [hidden] * count,
+        out_specs=[pl.BlockSpec((tile, width), lambda i: (i, 0))] * count,
+        scratch_shapes=[pltpu.VMEM((2 * rows, width), BF16)],
+        compiler_params=pltpu.CompilerParams(vmem_limit_bytes=24 * MIB),
+        cost_estimate=pl.CostEstimate(
+            flops=4 * count * rows * half * width,
+            bytes_accessed=2 * count * half * width,
+            transcendentals=0,
+        ),
+        name=name,
+    )(own, other, *lefts)
+
+
+def per_device(
+    tokens, grad_out, routing, gates, modality, hot_experts, gate_weight, up_weight, down_weight
+):
+    def swap(block):
+        return lax.ppermute(block, "dp", [(0, 1), (1, 0)])
+
+    def travel(block, hop):
+        moves = [
+            (2 * i + c, 2 * (i ^ hop ^ c) + c) for i in range(FLIGHT) for c in range(2)
+        ]
+        return lax.ppermute(block, ("expert", "dp"), moves)
+
+    picker, keep, give, my_tokens, my_grads = route(
+        hot_experts, routing, gates, modality, tokens, grad_out
+    )
+    slots = (keep, swap(give))
+    tok_rows = (my_tokens, swap(tokens))
+    grad_rows = (my_grads, swap(grad_out))
+    hops = range(len(HOPS))
+    tok_msgs = pick(slots, tok_rows, None, [(k, (0,)) for k in hops[:FAR]], 1, "pick_far")
+    rest = [(k, (1,)) for k in hops[:FAR]] + [(k, (0, 1)) for k in hops[FAR:]]
+    rest_msgs = pick(slots, tok_rows, grad_rows, rest, 2, "pick_rest")
+    scl_msgs, near_msgs = rest_msgs[:FAR], rest_msgs[FAR:]
+    got_tok = [travel(m, hop) for m, hop in zip(tok_msgs, HOPS)]
+    got_near = [travel(m, hop) for m, hop in zip(near_msgs, HOPS[FAR:])]
+    got_scl = [travel(m, hop) for m, hop in zip(scl_msgs, HOPS)]
+    half = 2 * HOTCAP
+    own_tok = jnp.concatenate(got_tok + [block[:half] for block in got_near], axis=0)
+    other_tok = swap(own_tok)
+    pre = pre_activations(own_tok, other_tok, gate_weight, up_weight, down_weight)
+    got_scl, pre = lax.optimization_barrier((got_scl, pre))
+    own_scl = jnp.concatenate(got_scl + [block[half:] for block in got_near], axis=0)
+    other_scl = swap(own_scl)
+    dh, du, act, mine, theirs = activation_grads(own_scl, other_scl, *pre)
+    (grad_down,) = weight_grads(own_scl, other_scl, [act], "down_grad")
+    added, grad_down = lax.optimization_barrier((swap(theirs), grad_down))
+    pieces = (mine + added.astype(F32)).astype(BF16)
+    back = [
+        travel(pieces[2 * k * HOTCAP : 2 * (k + 1) * HOTCAP], hop) for k, hop in enumerate(HOPS)
+    ]
+    grad_gate, grad_up = weight_grads(own_tok, other_tok, [dh, du], "gate_up_grads")
+    back, grad_gate, grad_up = lax.optimization_barrier((back, grad_gate, grad_up))
+    kept = jnp.concatenate([block[:HOTCAP] for block in back], axis=0)
+    given = swap(jnp.concatenate([block[HOTCAP:] for block in back], axis=0))
+    grad_tokens = lax.dot_general(
+        picker,
+        jnp.concatenate([kept, given], axis=0),
+        (((0,), (0,)), ((), ())),
+        preferred_element_type=F32,
+    ).astype(BF16)
+    return grad_tokens, grad_gate, grad_up, grad_down
 
 
 def solution(mesh):
+    sizes = dict(mesh.shape)
+    token_spec = P(("groups", "expert", "dp"), None)
     in_specs = (
-        P(("groups", "expert", "dp"), None),
-        P(("groups", "expert", "dp"), None),
-        P(("groups", "expert", "dp"), None),
-        P(("groups", "expert", "dp"), None),
+        token_spec,
+        token_spec,
+        token_spec,
+        token_spec,
         P(("groups", "expert", "dp")),
         P("groups"),
         P("expert", None),
         P("expert", None),
         P("expert", None),
     )
-    out_specs = (
-        P(("groups", "expert", "dp"), None),
-        P(("groups", "expert", "dp"), None),
-        P(("groups", "expert", "dp"), None),
-        P(("groups", "expert", "dp"), None),
-    )
+    paired = sizes["expert"] == FLIGHT and sizes["dp"] == 2
     return jax.shard_map(
-        per_device, mesh=mesh, in_specs=in_specs, out_specs=out_specs, check_vma=False
-    )
+        per_device if paired else per_device_general,
+        mesh=mesh,
+        in_specs=in_specs,
+        out_specs=(token_spec,) * 4,
+        check_vma=False,
+    )

time: 212 us -> 65.8 us (0.31)
  matrix products: 97.8 us -> 1.34 us
  other arithmetic: 34.1 us -> 0.16 us
  Pallas kernels: 0 us -> 28.3 us
  waiting for transfers between devices: 35.4 us -> 13.6 us
  blocking collectives: 18.5 us -> 0 us
  between operations: 13.8 us -> 0.82 us
  starting transfers between devices: 11.2 us -> 21.1 us
    dot_general x11 -> x1, matrix products: 97.8 us -> 1.34 us  [per_device(): lax.dot_general(picker, jnp.concatenate([kept, given], axis=0), (((0,), (...]
    convert_element_type x4 -> x1, other arithmetic: 30.8 us -> 0.08 us  [per_device(): pieces = (mine + added.astype(F32)).astype(BF16)]
    pallas_call x0 -> x7, Pallas kernels: none -> 28.3 us  [the longest x2 11.2 us: weight_grads(): pl.pallas_call(kernel, out_shape=[jax.ShapeDtypeStruct((half, width), BF1...]
    reduce_scatter x3 -> x0, waiting for transfers between devices: 25.3 us -> none  [the longest x1 25.3 us: per_device(): lax.psum_scatter(grad_terms[0], 'dp', scatter_dimension=0, tiled=True)]
    ppermute x0 -> x17, starting transfers between devices: none -> 21.1 us  [the longest x10 19.5 us: travel(): return lax.ppermute(block, ('expert', 'dp'), moves)]
    all_to_all x1 -> x0, blocking collectives: 18.5 us -> none  [per_device(): lax.all_to_all(partials.reshape(send_shape), 'expert', split_axis=0, conc...]
    ppermute x0 -> x17, waiting for transfers between devices: none -> 13.6 us  [the longest x10 9.45 us: travel(): return lax.ppermute(block, ('expert', 'dp'), moves)]
    all_to_all x2 -> x0, starting transfers between devices: 10.9 us -> none  [the longest x1 7.25 us: per_device(): lax.all_to_all(replicate_rows(picked), 'expert', split_axis=0, concat_axi...]
  transfers between devices with their start and end apart: 5 -> 17, of which waited for: 2 -> 7; matrix products, arithmetic and copies ran while one was open for 51% -> 0% of each run, Pallas kernels for 0% -> 34%
where the time goes in v3:
time: 65.8 us; the launch traced here: 65.6 us
  Pallas kernels  28.3 us (43%)
  starting transfers between devices  21.1 us (32%)
  waiting for transfers between devices  13.6 us (21%)
  matrix products  1.34 us (2%)
  between operations  0.82 us (1%)
    ppermute x10, starting transfers between devices, travel(): return lax.ppermute(block, ('expert', 'dp'), moves)  19.5 us
    pallas_call x2, Pallas kernels, weight_grads(): pl.pallas_call(kernel, out_shape=[jax.ShapeDtypeStruct((half, width), BF1...  11.2 us
    ppermute x10, waiting for transfers between devices, travel(): return lax.ppermute(block, ('expert', 'dp'), moves)  9.45 us
    pallas_call x1, Pallas kernels, pre_activations(): pl.pallas_call(kernel, out_shape=[pltpu.VMEM((half, 2 * rows), F32)] * 2...  8.59 us
    ppermute x7, waiting for transfers between devices, swap(): return lax.ppermute(block, 'dp', [(0, 1), (1, 0)])  4.18 us
    pallas_call x1, Pallas kernels, activation_grads(): pl.pallas_call(kernel, out_shape=[pltpu.VMEM((half, 2 * rows), BF16)] * 3...  4.12 us
    pallas_call x1, Pallas kernels, route(): pl.pallas_call(kernel, out_shape=[pltpu.VMEM((slots, tok_count), BF16), p...  2.27 us
    pallas_call x2, Pallas kernels, pick(): pl.pallas_call(kernel, out_shape=[pltpu.VMEM((2 * HOTCAP * len(carried),...  2.14 us
  transfers between devices with their start and end apart: 17, of which 7 were waited for; matrix products, arithmetic and copies ran while one was open for 0% of the time, Pallas kernels for 34%

profile of v3, /device:TPU:0, one launch (start us, length us, event | category | flops | bytes accessed | tf_op | source)
XLA Modules:
  0.0 65.6 jit_solution(11002040533420556644)
XLA Ops:
  0.6 0.5 collective-permute-start.1
  1.2 0.1 collective-permute-start.2
  1.2 2.3 %route.1 = (bf16[64,128]{1,0:T(8,128)(2,1)S(1)}, f32[32,128]{1,0:T(8,128)S(1)}, f32[32,128]{1,0:T(8,128)S(1)}, bf16[128,3584]{1,0:T(8,128)(2,1)S(1)}, bf16[128,3584]{1,0:T(8,128)(2,1)S(1)}) custom-call(s32[2]{0:T(128)} %hot_ref.1, s32[8,128]{1,0:T(8,128)} %bitcast.5, f32[8,128]{1,0:T(8,128)} %bitcast.6, s32[1,128]{1,0:T(1,128)} %bitcast.7, ...), custom_call_target="tpu_custom_call" | custom-call | tf_op jit(solution)/shard_map/route/pallas_call | solution.py:147
  3.5 0.5 collective-permute-start
  4.0 0.8 %collective-permute-done.refs_1_ = f32[32,128]{1,0:T(8,128)S(1)} collective-permute-done((f32[32,128]{1,0:T(8,128)S(1)}, f32[32,128]{1,0:T(8,128)S(1)}, u32[]{:S(2)}, u32[]{:S(2)}) %collective-permute-start) | collective-permute-done | bytes 16416 | tf_op jit(solution)/shard_map/ppermute | solution.py:359
  4.8 0.0 collective-permute-done.1.refs_3_
  4.8 0.1 collective-permute-done.2.refs_5_
  4.9 1.8 %pick_rest.1 = (bf16[16,3584]{1,0:T(8,128)(2,1)S(1)}, bf16[16,3584]{1,0:T(8,128)(2,1)S(1)}, bf16[32,3584]{1,0:T(8,128)(2,1)S(1)}, bf16[32,3584]{1,0:T(8,128)(2,1)S(1)}) custom-call(f32[32,128]{1,0:T(8,128)S(1)} %get-tuple-element.43.refs_0_, f32[32,128]{1,0:T(8,128)S(1)} %collective-permute-done.refs_1_, bf16[128,3584]{1,0:T(8,128)(2,1)S(1)} %get-tuple-element.45.refs_2_, ...), custom_call_target="tpu_custom_call" | custom-call | flops 117440512 | bytes 4587520 | tf_op jit(solution)/shard_map/pick_rest/pallas_call | solution.py:194
  6.7 3.0 %collective-permute-start.7 = (bf16[32,3584]{1,0:T(8,128)(2,1)S(1)}, bf16[32,3584]{1,0:T(8,128)(2,1)S(1)}, u32[]{:S(2)}, u32[]{:S(2)}) collective-permute-start(bf16[32,3584]{1,0:T(8,128)(2,1)S(1)} %get-tuple-element.51), channel_id=1, source_target_pairs={{0,4},{1,7},{2,6},{3,5},{4,0},{5,3},{6,2},{7,1},{8,12},{9,15},{10,... | collective-permute-start | bytes 688136 | tf_op jit(solution)/shard_map/ppermute | solution.py:365
  9.7 0.4 pick_far.1
  10.1 3.5 %collective-permute-start.5 = (bf16[16,3584]{1,0:T(8,128)(2,1)S(1)}, bf16[16,3584]{1,0:T(8,128)(2,1)S(1)}, u32[]{:S(2)}, u32[]{:S(2)}) collective-permute-start(bf16[16,3584]{1,0:T(8,128)(2,1)S(1)} %get-tuple-element.49), channel_id=1, source_target_pairs={{0,14},{1,13},{2,12},{3,15},{4,10},{5,9},{6,8},{7,11},{8,6},{9,5},... | collective-permute-start | bytes 344072 | tf_op jit(solution)/shard_map/ppermute | solution.py:365
  13.5 0.0 collective-permute-start.6
  13.5 2.6 %collective-permute-start.8 = (bf16[32,3584]{1,0:T(8,128)(2,1)S(1)}, bf16[32,3584]{1,0:T(8,128)(2,1)S(1)}, u32[]{:S(2)}, u32[]{:S(2)}) collective-permute-start(bf16[32,3584]{1,0:T(8,128)(2,1)S(1)} %get-tuple-element.52), channel_id=1, source_target_pairs={{0,2},{1,1},{2,0},{3,3},{4,6},{5,5},{6,4},{7,7},{8,10},{9,9},{10,8... | collective-permute-start | bytes 688136 | tf_op jit(solution)/shard_map/ppermute | solution.py:365
  16.2 0.0 collective-permute-done.7
  16.2 6.6 %collective-permute-done.8 = bf16[32,3584]{1,0:T(8,128)(2,1)S(1)} collective-permute-done((bf16[32,3584]{1,0:T(8,128)(2,1)S(1)}, bf16[32,3584]{1,0:T(8,128)(2,1)S(1)}, u32[]{:S(2)}, u32[]{:S(2)}) %collective-permute-start.8) | collective-permute-done | bytes 229408 | tf_op jit(solution)/shard_map/ppermute | solution.py:365
  22.9 0.0 collective-permute-done.5
  22.9 1.3 %collective-permute-done.6 = bf16[16,3584]{1,0:T(8,128)(2,1)S(1)} collective-permute-done((bf16[16,3584]{1,0:T(8,128)(2,1)S(1)}, bf16[16,3584]{1,0:T(8,128)(2,1)S(1)}, u32[]{:S(2)}, u32[]{:S(2)}) %collective-permute-start.6) | collective-permute-done | bytes 114720 | tf_op jit(solution)/shard_map/ppermute | solution.py:365
  24.2 0.2 collective-permute-start.9
  24.5 2.5 %collective-permute-start.3 = (bf16[16,3584]{1,0:T(8,128)(2,1)S(1)}, bf16[16,3584]{1,0:T(8,128)(2,1)S(1)}, u32[]{:S(2)}, u32[]{:S(2)}) collective-permute-start(bf16[16,3584]{1,0:T(8,128)(2,1)S(1)} %get-tuple-element.47), channel_id=1, source_target_pairs={{0,14},{1,13},{2,12},{3,15},{4,10},{5,9},{6,8},{7,11},{8,6},{9,5},... | collective-permute-start | bytes 344072 | tf_op jit(solution)/shard_map/ppermute | solution.py:365
  27.0 0.0 collective-permute-start.4
  27.0 0.0 collective-permute-done.9.other_ref
  27.0 8.6 %pre_activations.1 = (f32[1024,128]{1,0:T(8,128)S(1)}, f32[1024,128]{1,0:T(8,128)S(1)}, bf16[1024,3584]{1,0:T(8,128)(2,1)S(1)}, bf16[1024,3584]{1,0:T(8,128)(2,1)S(1)}, bf16[1024,3584]{1,0:T(8,128)(2,1)S(1)}) custom-call(bf16[64,3584]{1,0:T(8,128)(2,1)S(1)} %pad_maximum_fusion.own_ref, bf16[64,3584]{1,0:T(8,128)(2,1)S(1)} %collective-permute-done.9.other_ref, ...), custom_call_target="tpu_custom_call" | custom-call | flops 1000 | bytes 1000 | tf_op jit(solution)/shard_map/pre_activations/pallas_call | solution.py:245
  35.6 0.0 collective-permute-done.3
  35.6 1.5 %collective-permute-done.4 = bf16[16,3584]{1,0:T(8,128)(2,1)S(1)} collective-permute-done((bf16[16,3584]{1,0:T(8,128)(2,1)S(1)}, bf16[16,3584]{1,0:T(8,128)(2,1)S(1)}, u32[]{:S(2)}, u32[]{:S(2)}) %collective-permute-start.4) | collective-permute-done | bytes 114720 | tf_op jit(solution)/shard_map/ppermute | solution.py:365
  37.1 0.1 collective-permute-start.10
  37.2 1.8 %collective-permute-done.10.other_ref = bf16[64,3584]{1,0:T(8,128)(2,1)S(1)} collective-permute-done((bf16[64,3584]{1,0:T(8,128)(2,1)S(1)}, bf16[64,3584]{1,0:T(8,128)(2,1)S(1)}, u32[]{:S(2)}, u32[]{:S(2)}) %collective-permute-start.10) | collective-permute-done | bytes 458784 | tf_op jit(solution)/shard_map/ppermute | solution.py:359
  39.0 4.1 %activation_grads.1 = (bf16[1024,128]{1,0:T(8,128)(2,1)S(1)}, bf16[1024,128]{1,0:T(8,128)(2,1)S(1)}, bf16[1024,128]{1,0:T(8,128)(2,1)S(1)}, f32[64,3584]{1,0:T(8,128)S(1)}, bf16[64,3584]{1,0:T(8,128)(2,1)S(1)}) custom-call(bf16[64,3584]{1,0:T(8,128)(2,1)S(1)} %pad_maximum_fusion.1.own_ref, bf16[64,3584]{1,0:T(8,128)(2,1)S(1)} %collective-permute-done.10.other_ref, ...), custom_call_target="tpu_custom_call" | custom-call | flops 2818572288 | bytes 22020096 | tf_op jit(solution)/shard_map/activation_grads/pallas_call | solution.py:298
  43.1 0.2 collective-permute-start.11
  43.4 4.4 %down_grad.1 = bf16[1024,3584]{1,0:T(8,128)(2,1)} custom-call(bf16[64,3584]{1,0:T(8,128)(2,1)S(1)} %pad_maximum_fusion.1.own_ref, bf16[64,3584]{1,0:T(8,128)(2,1)S(1)} %collective-permute-done.10.other_ref, bf16[1024,128]{1,0:T(8,128)(2,1)S(1)} %get-tuple-element.67.rest_0_), custom_call_target="tpu_custom_call" | custom-call | flops 939524096 | bytes 7340032 | tf_op jit(solution)/shard_map/down_grad/pallas_call | solution.py:338
  47.8 0.0 collective-permute-done.11
  47.8 0.1 add_convert_fusion
  47.9 2.7 %collective-permute-start.15 = (bf16[16,3584]{1,0:T(8,128)(2,1)S(1)}, bf16[16,3584]{1,0:T(8,128)(2,1)S(1)}, u32[]{:S(2)}, u32[]{:S(2)}) collective-permute-start(bf16[16,3584]{1,0:T(8,128)(2,1)S(1)} %get-tuple-element.80), channel_id=1, source_target_pairs={{0,2},{1,1},{2,0},{3,3},{4,6},{5,5},{6,4},{7,7},{8,10},{9,9},{10,8... | collective-permute-start | bytes 344072 | tf_op jit(solution)/shard_map/ppermute | solution.py:365
  50.6 1.1 %collective-permute-start.14 = (bf16[16,3584]{1,0:T(8,128)(2,1)S(1)}, bf16[16,3584]{1,0:T(8,128)(2,1)S(1)}, u32[]{:S(2)}, u32[]{:S(2)}) collective-permute-start(bf16[16,3584]{1,0:T(8,128)(2,1)S(1)} %get-tuple-element.81), channel_id=1, source_target_pairs={{0,4},{1,7},{2,6},{3,5},{4,0},{5,3},{6,2},{7,1},{8,12},{9,15},{10,... | collective-permute-start | bytes 344072 | tf_op jit(solution)/shard_map/ppermute | solution.py:365
  51.7 2.0 %collective-permute-start.13 = (bf16[16,3584]{1,0:T(8,128)(2,1)S(1)}, bf16[16,3584]{1,0:T(8,128)(2,1)S(1)}, u32[]{:S(2)}, u32[]{:S(2)}) collective-permute-start(bf16[16,3584]{1,0:T(8,128)(2,1)S(1)} %get-tuple-element.82), channel_id=1, source_target_pairs={{0,8},{1,11},{2,10},{3,9},{4,12},{5,15},{6,14},{7,13},{8,0},{9,3},... | collective-permute-start | bytes 344072 | tf_op jit(solution)/shard_map/ppermute | solution.py:365
  53.7 2.0 %collective-permute-start.12 = (bf16[16,3584]{1,0:T(8,128)(2,1)S(1)}, bf16[16,3584]{1,0:T(8,128)(2,1)S(1)}, u32[]{:S(2)}, u32[]{:S(2)}) collective-permute-start(bf16[16,3584]{1,0:T(8,128)(2,1)S(1)} %get-tuple-element.83), channel_id=1, source_target_pairs={{0,14},{1,13},{2,12},{3,15},{4,10},{5,9},{6,8},{7,11},{8,6},{9,5},... | collective-permute-start | bytes 344072 | tf_op jit(solution)/shard_map/ppermute | solution.py:365
  55.7 6.8 %gate_up_grads.1 = (bf16[1024,3584]{1,0:T(8,128)(2,1)}, bf16[1024,3584]{1,0:T(8,128)(2,1)}) custom-call(bf16[64,3584]{1,0:T(8,128)(2,1)S(1)} %pad_maximum_fusion.own_ref, bf16[64,3584]{1,0:T(8,128)(2,1)S(1)} %collective-permute-done.9.other_ref, bf16[1024,128]{1,0:T(8,128)(2,1)S(1)} %get-tuple-element.69.rest_0_, bf16[1024,128]{1,0:T(8,128)(2,1)S(1)} %get-tuple-element.70.rest_1_), custom_call_target="tpu_custom_call" | custom-call | flops 1879048192 | bytes 14680064 | tf_op jit(solution)/shard_map/gate_up_grads/pallas_call | solution.py:338
  62.5 0.0 collective-permute-done.15
  62.5 0.0 collective-permute-done.14
  62.5 0.0 collective-permute-done.13
  62.5 0.0 collective-permute-done.12
  62.6 0.1 collective-permute-start.16
  62.7 1.5 %collective-permute-done.16 = bf16[32,3584]{1,0:T(8,128)(2,1)S(1)} collective-permute-done((bf16[32,3584]{1,0:T(8,128)(2,1)S(1)}, bf16[32,3584]{1,0:T(8,128)(2,1)S(1)}, u32[]{:S(2)}, u32[]{:S(2)}) %collective-permute-start.16) | collective-permute-done | bytes 229408 | tf_op jit(solution)/shard_map/ppermute | solution.py:359
  64.2 1.3 %convolution_convert_fusion = bf16[128,3584]{1,0:T(8,128)(2,1)} fusion(bf16[64,128]{1,0:T(8,128)(2,1)S(1)} %get-tuple-element.42, bf16[64,3584]{1,0:T(8,128)(2,1)S(1)} %constant_dynamic-update-slice_fusion), kind=kOutput, calls=%fused_computation | convolution fusion | flops 59179008 | bytes 1392640 | tf_op jit(solution)/shard_map/dot_general | solution.py:399
  (11 shorter events, 0.2 us)
Async XLA Ops:
  0.6 4.2 %collective-permute-start.1 = (bf16[128,3584]{1,0:T(8,128)(2,1)}, bf16[128,3584]{1,0:T(8,128)(2,1)S(1)}, u32[]{:S(2)}, u32[]{:S(2)}) collective-permute-start(bf16[128,3584]{1,0:T(8,128)(2,1)} %tok_in.1), channel_id=1, source_target_pairs={{0,1},{1,0},{2,3},{3,2},{4,5},{5,4},{6,7},{7,6},{8,9},{9,8},{10,11... | collective-permute-start | bytes 2752520 | tf_op jit(solution)/shard_map/ppermute | solution.py:359
  1.2 3.8 %collective-permute-start.2 = (bf16[128,3584]{1,0:T(8,128)(2,1)}, bf16[128,3584]{1,0:T(8,128)(2,1)}, u32[]{:S(2)}, u32[]{:S(2)}) collective-permute-start(bf16[128,3584]{1,0:T(8,128)(2,1)} %gout_in.1), channel_id=1, source_target_pairs={{0,1},{1,0},{2,3},{3,2},{4,5},{5,4},{6,7},{7,6},{8,9},{9,8},{10,11... | collective-permute-start | bytes 2752520 | tf_op jit(solution)/shard_map/ppermute | solution.py:359
  3.5 1.3 %collective-permute-start = (f32[32,128]{1,0:T(8,128)S(1)}, f32[32,128]{1,0:T(8,128)S(1)}, u32[]{:S(2)}, u32[]{:S(2)}) collective-permute-start(f32[32,128]{1,0:T(8,128)S(1)} %get-tuple-element.44), channel_id=1, source_target_pairs={{0,1},{1,0},{2,3},{3,2},{4,5},{5,4},{6,7},{7,6},{8,9},{9,8},{10,11... | collective-permute-start | bytes 49160 | tf_op jit(solution)/shard_map/ppermute | solution.py:359
  6.7 9.5 %collective-permute-start.7 = (bf16[32,3584]{1,0:T(8,128)(2,1)S(1)}, bf16[32,3584]{1,0:T(8,128)(2,1)S(1)}, u32[]{:S(2)}, u32[]{:S(2)}) collective-permute-start(bf16[32,3584]{1,0:T(8,128)(2,1)S(1)} %get-tuple-element.51), channel_id=1, source_target_pairs={{0,4},{1,7},{2,6},{3,5},{4,0},{5,3},{6,2},{7,1},{8,12},{9,15},{10,... | collective-permute-start | bytes 688136 | tf_op jit(solution)/shard_map/ppermute | solution.py:365
  10.1 12.8 %collective-permute-start.5 = (bf16[16,3584]{1,0:T(8,128)(2,1)S(1)}, bf16[16,3584]{1,0:T(8,128)(2,1)S(1)}, u32[]{:S(2)}, u32[]{:S(2)}) collective-permute-start(bf16[16,3584]{1,0:T(8,128)(2,1)S(1)} %get-tuple-element.49), channel_id=1, source_target_pairs={{0,14},{1,13},{2,12},{3,15},{4,10},{5,9},{6,8},{7,11},{8,6},{9,5},... | collective-permute-start | bytes 344072 | tf_op jit(solution)/shard_map/ppermute | solution.py:365
  13.5 10.7 %collective-permute-start.6 = (bf16[16,3584]{1,0:T(8,128)(2,1)S(1)}, bf16[16,3584]{1,0:T(8,128)(2,1)S(1)}, u32[]{:S(2)}, u32[]{:S(2)}) collective-permute-start(bf16[16,3584]{1,0:T(8,128)(2,1)S(1)} %get-tuple-element.50), channel_id=1, source_target_pairs={{0,8},{1,11},{2,10},{3,9},{4,12},{5,15},{6,14},{7,13},{8,0},{9,3},... | collective-permute-start | bytes 344072 | tf_op jit(solution)/shard_map/ppermute | solution.py:365
  13.5 9.3 %collective-permute-start.8 = (bf16[32,3584]{1,0:T(8,128)(2,1)S(1)}, bf16[32,3584]{1,0:T(8,128)(2,1)S(1)}, u32[]{:S(2)}, u32[]{:S(2)}) collective-permute-start(bf16[32,3584]{1,0:T(8,128)(2,1)S(1)} %get-tuple-element.52), channel_id=1, source_target_pairs={{0,2},{1,1},{2,0},{3,3},{4,6},{5,5},{6,4},{7,7},{8,10},{9,9},{10,8... | collective-permute-start | bytes 688136 | tf_op jit(solution)/shard_map/ppermute | solution.py:365
  24.2 2.8 %collective-permute-start.9 = (bf16[64,3584]{1,0:T(8,128)(2,1)S(1)}, bf16[64,3584]{1,0:T(8,128)(2,1)S(1)}, u32[]{:S(2)}, u32[]{:S(2)}) collective-permute-start(bf16[64,3584]{1,0:T(8,128)(2,1)S(1)} %pad_maximum_fusion.own_ref), channel_id=1, source_target_pairs={{0,1},{1,0},{2,3},{3,2},{4,5},{5,4},{6,7},{7,6},{8,9},{9,8},{10,11... | collective-permute-start | bytes 1376264 | tf_op jit(solution)/shard_map/ppermute | solution.py:359
  24.5 11.1 %collective-permute-start.3 = (bf16[16,3584]{1,0:T(8,128)(2,1)S(1)}, bf16[16,3584]{1,0:T(8,128)(2,1)S(1)}, u32[]{:S(2)}, u32[]{:S(2)}) collective-permute-start(bf16[16,3584]{1,0:T(8,128)(2,1)S(1)} %get-tuple-element.47), channel_id=1, source_target_pairs={{0,14},{1,13},{2,12},{3,15},{4,10},{5,9},{6,8},{7,11},{8,6},{9,5},... | collective-permute-start | bytes 344072 | tf_op jit(solution)/shard_map/ppermute | solution.py:365
  27.0 10.1 %collective-permute-start.4 = (bf16[16,3584]{1,0:T(8,128)(2,1)S(1)}, bf16[16,3584]{1,0:T(8,128)(2,1)S(1)}, u32[]{:S(2)}, u32[]{:S(2)}) collective-permute-start(bf16[16,3584]{1,0:T(8,128)(2,1)S(1)} %get-tuple-element.48), channel_id=1, source_target_pairs={{0,8},{1,11},{2,10},{3,9},{4,12},{5,15},{6,14},{7,13},{8,0},{9,3},... | collective-permute-start | bytes 344072 | tf_op jit(solution)/shard_map/ppermute | solution.py:365
  37.1 1.9 %collective-permute-start.10 = (bf16[64,3584]{1,0:T(8,128)(2,1)S(1)}, bf16[64,3584]{1,0:T(8,128)(2,1)S(1)}, u32[]{:S(2)}, u32[]{:S(2)}) collective-permute-start(bf16[64,3584]{1,0:T(8,128)(2,1)S(1)} %pad_maximum_fusion.1.own_ref), channel_id=1, source_target_pairs={{0,1},{1,0},{2,3},{3,2},{4,5},{5,4},{6,7},{7,6},{8,9},{9,8},{10,11... | collective-permute-start | bytes 1376264 | tf_op jit(solution)/shard_map/ppermute | solution.py:359
  43.1 4.6 %collective-permute-start.11 = (bf16[64,3584]{1,0:T(8,128)(2,1)S(1)}, bf16[64,3584]{1,0:T(8,128)(2,1)S(1)}, u32[]{:S(2)}, u32[]{:S(2)}) collective-permute-start(bf16[64,3584]{1,0:T(8,128)(2,1)S(1)} %get-tuple-element.66), channel_id=1, source_target_pairs={{0,1},{1,0},{2,3},{3,2},{4,5},{5,4},{6,7},{7,6},{8,9},{9,8},{10,11... | collective-permute-start | bytes 1376264 | tf_op jit(solution)/shard_map/ppermute | solution.py:359
  47.9 14.6 %collective-permute-start.15 = (bf16[16,3584]{1,0:T(8,128)(2,1)S(1)}, bf16[16,3584]{1,0:T(8,128)(2,1)S(1)}, u32[]{:S(2)}, u32[]{:S(2)}) collective-permute-start(bf16[16,3584]{1,0:T(8,128)(2,1)S(1)} %get-tuple-element.80), channel_id=1, source_target_pairs={{0,2},{1,1},{2,0},{3,3},{4,6},{5,5},{6,4},{7,7},{8,10},{9,9},{10,8... | collective-permute-start | bytes 344072 | tf_op jit(solution)/shard_map/ppermute | solution.py:365
  50.6 12.0 %collective-permute-start.14 = (bf16[16,3584]{1,0:T(8,128)(2,1)S(1)}, bf16[16,3584]{1,0:T(8,128)(2,1)S(1)}, u32[]{:S(2)}, u32[]{:S(2)}) collective-permute-start(bf16[16,3584]{1,0:T(8,128)(2,1)S(1)} %get-tuple-element.81), channel_id=1, source_target_pairs={{0,4},{1,7},{2,6},{3,5},{4,0},{5,3},{6,2},{7,1},{8,12},{9,15},{10,... | collective-permute-start | bytes 344072 | tf_op jit(solution)/shard_map/ppermute | solution.py:365
  51.7 10.8 %collective-permute-start.13 = (bf16[16,3584]{1,0:T(8,128)(2,1)S(1)}, bf16[16,3584]{1,0:T(8,128)(2,1)S(1)}, u32[]{:S(2)}, u32[]{:S(2)}) collective-permute-start(bf16[16,3584]{1,0:T(8,128)(2,1)S(1)} %get-tuple-element.82), channel_id=1, source_target_pairs={{0,8},{1,11},{2,10},{3,9},{4,12},{5,15},{6,14},{7,13},{8,0},{9,3},... | collective-permute-start | bytes 344072 | tf_op jit(solution)/shard_map/ppermute | solution.py:365
  53.7 8.9 %collective-permute-start.12 = (bf16[16,3584]{1,0:T(8,128)(2,1)S(1)}, bf16[16,3584]{1,0:T(8,128)(2,1)S(1)}, u32[]{:S(2)}, u32[]{:S(2)}) collective-permute-start(bf16[16,3584]{1,0:T(8,128)(2,1)S(1)} %get-tuple-element.83), channel_id=1, source_target_pairs={{0,14},{1,13},{2,12},{3,15},{4,10},{5,9},{6,8},{7,11},{8,6},{9,5},... | collective-permute-start | bytes 344072 | tf_op jit(solution)/shard_map/ppermute | solution.py:365
  62.6 1.6 %collective-permute-start.16 = (bf16[32,3584]{1,0:T(8,128)(2,1)S(1)}, bf16[32,3584]{1,0:T(8,128)(2,1)S(1)}, u32[]{:S(2)}, u32[]{:S(2)}) collective-permute-start(bf16[32,3584]{1,0:T(8,128)(2,1)S(1)} %pad_maximum_fusion.2), channel_id=1, source_target_pairs={{0,1},{1,0},{2,3},{3,2},{4,5},{5,4},{6,7},{7,6},{8,9},{9,8},{10,11... | collective-permute-start | bytes 688136 | tf_op jit(solution)/shard_map/ppermute | solution.py:359

commit v4 on v3

--- a/solution.py
+++ b/solution.py
@@ -93,7 +93,6 @@
 
 
 HOPS = (7, 4, 2, 1)
-FAR = 2
 CARRIED = len(HOPS) * HOTCAP
 NT = (((1,), (1,)), ((), ()))
 SMEM = pl.BlockSpec(memory_space=pltpu.SMEM)
@@ -167,118 +166,96 @@
     )
 
 
-def pick(slots, tokens, grads, parts, work, name):
-    tok_count, width = tokens[0].shape
-    sources = [rows for rows in (tokens, grads) if rows is not None]
+def pick(mine, theirs, my_tokens, their_tokens, my_grads, their_grads):
+    tok_count, width = my_tokens.shape
+
+    def kernel(mine_ref, theirs_ref, my_tok, their_tok, my_grad, their_grad, *outs):
+        for core, slot_ref, tok_ref, grad_ref in (
+            (0, mine_ref, my_tok, my_grad),
+            (1, theirs_ref, their_tok, their_grad),
+        ):
+            gated = slot_ref[...]
+            picker = jnp.where(gated != 0.0, 1.0, 0.0).astype(BF16)
+            rows = jnp.dot(picker, tok_ref[...], preferred_element_type=F32)
+            scaled = jnp.dot(picker, grad_ref[...], preferred_element_type=F32)
+            scaled = scaled * jnp.sum(gated, axis=1, keepdims=True)
+            for k, out in enumerate(outs):
+                slot = slice(k * HOTCAP, (k + 1) * HOTCAP)
+                out[core * HOTCAP : (core + 1) * HOTCAP] = rows[slot].astype(BF16)
+                out[(core + 2) * HOTCAP : (core + 3) * HOTCAP] = scaled[slot].astype(BF16)
+
+    return pl.pallas_call(
+        kernel,
+        out_shape=[pltpu.VMEM((4 * HOTCAP, width), BF16)] * len(HOPS),
+        in_specs=[VMEM] * 6,
+        out_specs=[VMEM] * len(HOPS),
+        compiler_params=pltpu.CompilerParams(vmem_limit_bytes=16 * MIB),
+        cost_estimate=pl.CostEstimate(
+            flops=8 * CARRIED * tok_count * width,
+            bytes_accessed=8 * (CARRIED + tok_count) * width,
+            transcendentals=0,
+        ),
+        name="pick",
+    )(mine, theirs, my_tokens, their_tokens, my_grads, their_grads)
+
+
+def load_weights(*weights):
+    half = weights[0].shape[0] // 2
+    width = weights[0].shape[1]
+    count = len(weights)
 
     def kernel(*refs):
-        outs = refs[2 + 2 * len(sources) :]
-        for core in range(2):
-            gated = refs[core][...]
-            picker = jnp.where(gated != 0.0, 1.0, 0.0).astype(BF16)
-            first = min(k for k, _ in parts) * HOTCAP
-            picker = picker[first:]
-            gate = jnp.sum(gated[first:], axis=1, keepdims=True)
-            rows = [
-                jnp.dot(picker, refs[2 + 2 * n + core][...], preferred_element_type=F32)
-                for n in range(len(sources))
-            ]
-            if grads is not None:
-                rows[1] = rows[1] * gate
-            for (k, carried), out in zip(parts, outs):
-                slot = slice(k * HOTCAP - first, (k + 1) * HOTCAP - first)
-                for place, n in enumerate(carried):
-                    start = (2 * place + core) * HOTCAP
-                    out[start : start + HOTCAP] = rows[n][slot].astype(BF16)
-
-    return pl.pallas_call(
-        kernel,
-        out_shape=[
-            pltpu.VMEM((2 * HOTCAP * len(carried), width), BF16) for _, carried in parts
-        ],
-        in_specs=[VMEM] * (2 + 2 * len(sources)),
-        out_specs=[VMEM] * len(parts),
-        compiler_params=pltpu.CompilerParams(vmem_limit_bytes=16 * MIB),
-        cost_estimate=pl.CostEstimate(
-            flops=4 * work * CARRIED * tok_count * width,
-            bytes_accessed=4 * work * (CARRIED + tok_count) * width,
-            transcendentals=0,
-        ),
-        name=name,
-    )(*slots, *(block for pair in sources for block in pair))
-
-
-def pre_activations(own, other, gate_weight, up_weight, down_weight):
-    rows, width = own.shape
-    half = gate_weight.shape[0] // 2
-    tile = min(256, half)
-    steps = half // tile
-
-    def kernel(own_ref, other_ref, g_in, u_in, w_in, h_ref, up_ref, g_ref, u_ref, w_ref, *rest):
-        columns, sem = rest
         first = pl.multiple_of(lax.axis_index("dp") * half, half)
-        order = [(lane, i) for i in range(steps) for lane in (0, 1)]
-        order += [(2, i) for i in range(steps)]
-
-        def load(lane, i):
-            source, target = ((g_in, g_ref), (u_in, u_ref), (w_in, w_ref))[lane]
-            return pltpu.make_async_copy(
-                source.at[pl.ds(first + i * tile, tile)],
-                target.at[pl.ds(i * tile, tile)],
-                sem.at[lane, i],
+        loads = [
+            pltpu.make_async_copy(
+                refs[i].at[pl.ds(first, half)], refs[count + i], refs[2 * count].at[i]
             )
-
-        depth = 3
-        for lane, i in order[:depth]:
-            load(lane, i).start()
-        columns[:, :rows] = own_ref[...].T
-        columns[:, rows:] = other_ref[...].T
-        for n, (lane, i) in enumerate(order):
-            load(lane, i).wait()
-            if n + depth < len(order):
-                load(*order[n + depth]).start()
-            if lane < 2:
-                part = slice(i * tile, (i + 1) * tile)
-                weight, out = ((g_ref, h_ref), (u_ref, up_ref))[lane]
-                out[part] = jnp.dot(weight[part], columns[...], preferred_element_type=F32)
-
-    return pl.pallas_call(
-        kernel,
-        out_shape=[pltpu.VMEM((half, 2 * rows), F32)] * 2
-        + [pltpu.VMEM((half, width), BF16)] * 3,
-        in_specs=[VMEM, VMEM, HBM, HBM, HBM],
-        out_specs=[VMEM] * 5,
-        scratch_shapes=[
-            pltpu.VMEM((width, 2 * rows), BF16),
-            pltpu.SemaphoreType.DMA((3, steps)),
-        ],
-        compiler_params=pltpu.CompilerParams(vmem_limit_bytes=12 * MIB),
-        cost_estimate=pl.CostEstimate(flops=1000, bytes_accessed=1000, transcendentals=0),
-        name="pre_activations",
-    )(
-        own,
-        other,
-        *(
-            pltpu.with_memory_space_constraint(weight, pltpu.HBM)
-            for weight in (gate_weight, up_weight, down_weight)
-        ),
-    )
-
-
-def activation_grads(own, other, h, u, gate_half, up_half, down_half):
-    rows, width = own.shape
-    half = h.shape[0]
+            for i in range(count)
+        ]
+        for load in loads:
+            load.start()
+        for load in loads:
+            load.wait()
+
+    return pl.pallas_call(
+        kernel,
+        out_shape=[pltpu.VMEM((half, width), BF16)] * count,
+        in_specs=[HBM] * count,
+        out_specs=[VMEM] * count,
+        scratch_shapes=[pltpu.SemaphoreType.DMA((count,))],
+        compiler_params=pltpu.CompilerParams(vmem_limit_bytes=2 * MIB),
+        cost_estimate=pl.CostEstimate(
+            flops=0, bytes_accessed=4 * count * half * width, transcendentals=0
+        ),
+        name="load_weights",
+    )(*(pltpu.with_memory_space_constraint(weight, pltpu.HBM) for weight in weights))
+
+
+def activation_grads(blocks, gate_half, up_half, down_half):
+    width = blocks[0].shape[1]
+    rows = 2 * HOTCAP * len(HOPS)
+    half = gate_half.shape[0]
     tile = min(256, half)
     chunk = 512 if width % 512 == 0 else width
 
-    def kernel(own_ref, other_ref, h_ref, up_ref, g_ref, u_ref, w_ref, *rest):
-        dh_ref, du_ref, act_ref, mine_ref, theirs_ref, scl, dh_rows, du_rows = rest
-        scl[:rows] = own_ref[...]
-        scl[rows:] = other_ref[...]
+    def kernel(*refs):
+        ins, refs = refs[: len(blocks)], refs[len(blocks) :]
+        g_ref, u_ref, w_ref, tok_ref, scl_ref, dh_ref, du_ref, act_ref = refs[:8]
+        mine_ref, theirs_ref, tok_cols, scl_cols, dh_rows, du_rows = refs[8:]
+        message = 2 * HOTCAP
+        place = 0
+        for block in ins:
+            for start in range(0, block.shape[0], 2 * message):
+                tok_ref[place : place + message] = block[start : start + message]
+                scl_ref[place : place + message] = block[start + message : start + 2 * message]
+                place += message
+        tok_cols[...] = tok_ref[...].T
+        scl_cols[...] = scl_ref[...].T
         for i in range(half // tile):
             part = slice(i * tile, (i + 1) * tile)
-            da = lax.dot_general(w_ref[part], scl[...], NT, preferred_element_type=F32)
-            pre, up = h_ref[part], up_ref[part]
+            pre = jnp.dot(g_ref[part], tok_cols[...], preferred_element_type=F32)
+            up = jnp.dot(u_ref[part], tok_cols[...], preferred_element_type=F32)
+            da = jnp.dot(w_ref[part], scl_cols[...], preferred_element_type=F32)
             sig = jax.nn.sigmoid(pre)
             swish = pre * sig
             act_ref[part] = (swish * up).astype(BF16)
@@ -297,59 +274,161 @@
 
     return pl.pallas_call(
         kernel,
-        out_shape=[pltpu.VMEM((half, 2 * rows), BF16)] * 3
+        out_shape=[pltpu.VMEM((2 * rows, width), BF16)] * 2
+        + [pltpu.VMEM((half, 2 * rows), BF16)] * 3
         + [pltpu.VMEM((rows, width), F32), pltpu.VMEM((rows, width), BF16)],
-        in_specs=[VMEM] * 7,
-        out_specs=[VMEM] * 5,
+        in_specs=[VMEM] * (len(blocks) + 3),
+        out_specs=[VMEM] * 7,
         scratch_shapes=[
-            pltpu.VMEM((2 * rows, width), BF16),
+            pltpu.VMEM((width, 2 * rows), BF16),
+            pltpu.VMEM((width, 2 * rows), BF16),
             pltpu.VMEM((2 * rows, half), BF16),
             pltpu.VMEM((2 * rows, half), BF16),
         ],
         compiler_params=pltpu.CompilerParams(vmem_limit_bytes=12 * MIB),
         cost_estimate=pl.CostEstimate(
-            flops=12 * rows * half * width,
+            flops=20 * rows * half * width,
             bytes_accessed=6 * half * width,
             transcendentals=2 * rows * half,
         ),
         name="activation_grads",
-    )(own, other, h, u, gate_half, up_half, down_half)
-
-
-def weight_grads(own, other, lefts, name):
-    rows, width = own.shape
-    half = lefts[0].shape[0]
-    tile = min(256, half)
-    count = len(lefts)
-
-    def kernel(own_ref, other_ref, *rest):
-        sides, outs, both = rest[:count], rest[count : 2 * count], rest[2 * count]
-
-        @pl.when(pl.program_id(0) == 0)
-        def _():
-            both[:rows] = own_ref[...]
-            both[rows:] = other_ref[...]
-
-        for left, out in zip(sides, outs):
-            out[...] = jnp.dot(left[...], both[...], preferred_element_type=F32).astype(BF16)
-
-    full = pl.BlockSpec((rows, width), lambda i: (0, 0))
-    hidden = pl.BlockSpec((tile, 2 * rows), lambda i: (i, 0))
-    return pl.pallas_call(
-        kernel,
-        out_shape=[jax.ShapeDtypeStruct((half, width), BF16)] * count,
-        grid=(half // tile,),
-        in_specs=[full] * 2 + [hidden] * count,
-        out_specs=[pl.BlockSpec((tile, width), lambda i: (i, 0))] * count,
-        scratch_shapes=[pltpu.VMEM((2 * rows, width), BF16)],
-        compiler_params=pltpu.CompilerParams(vmem_limit_bytes=24 * MIB),
-        cost_estimate=pl.CostEstimate(
-            flops=4 * count * rows * half * width,
-            bytes_accessed=2 * count * half * width,
+    )(*blocks, gate_half, up_half, down_half)
+
+
+def weight_grad(rows, left, name):
+    count, width = rows.shape
+    half = left.shape[0]
+    chunk = 512 if width % 512 == 0 else width
+
+    def kernel(rows_ref, left_ref, out_ref):
+        for c in range(0, width, chunk):
+            cols = slice(c, c + chunk)
+            out_ref[:, cols] = jnp.dot(
+                left_ref[...], rows_ref[:, cols], preferred_element_type=F32
+            ).astype(BF16)
+
+    return pl.pallas_call(
+        kernel,
+        out_shape=pltpu.VMEM((half, width), BF16),
+        in_specs=[VMEM, VMEM],
+        out_specs=VMEM,
+        compiler_params=pltpu.CompilerParams(vmem_limit_bytes=8 * MIB),
+        cost_estimate=pl.CostEstimate(
+            flops=2 * count * half * width, bytes_accessed=2 * half * width, transcendentals=0
+        ),
+        name=name,
+    )(rows, left)
+
+
+def gate_up_grads(rows, gate_left, up_left, down):
+    count, width = rows.shape
+    half = gate_left.shape[0]
+    chunk = 512 if width % 512 == 0 else width
+
+    def kernel(rows_ref, gate_ref, up_ref, down_ref, gate_out, down_out, up_out, held, sem):
+        copies = [pltpu.make_async_copy(down_ref, down_out, sem.at[0])]
+        copies[0].start()
+        for n, c in enumerate(range(0, width, chunk)):
+            cols = slice(c, c + chunk)
+            held[:, cols] = jnp.dot(
+                gate_ref[...], rows_ref[:, cols], preferred_element_type=F32
+            ).astype(BF16)
+            copies.append(
+                pltpu.make_async_copy(held.at[:, cols], gate_out.at[:, cols], sem.at[1 + n])
+            )
+            copies[-1].start()
+        for c in range(0, width, chunk):
+            cols = slice(c, c + chunk)
+            up_out[:, cols] = jnp.dot(
+                up_ref[...], rows_ref[:, cols], preferred_element_type=F32
+            ).astype(BF16)
+        for copy in copies:
+            copy.wait()
+
+    full = jax.ShapeDtypeStruct((half, width), BF16)
+    return pl.pallas_call(
+        kernel,
+        out_shape=[full, full, pltpu.VMEM((half, width), BF16)],
+        in_specs=[VMEM] * 4,
+        out_specs=[HBM, HBM, VMEM],
+        scratch_shapes=[
+            pltpu.VMEM((half, width), BF16),
+            pltpu.SemaphoreType.DMA((1 + width // chunk,)),
+        ],
+        compiler_params=pltpu.CompilerParams(vmem_limit_bytes=12 * MIB),
+        cost_estimate=pl.CostEstimate(
+            flops=4 * count * half * width, bytes_accessed=4 * half * width, transcendentals=0
+        ),
+        name="gate_up_grads",
+    )(rows, gate_left, up_left, down)
+
+
+def write_first(block):
+    rows = block.shape[0] // 2
+
+    def kernel(block_ref, out, sem):
+        copy = pltpu.make_async_copy(block_ref.at[pl.ds(0, rows)], out.at[pl.ds(0, rows)], sem)
+        copy.start()
+        copy.wait()
+
+    return pl.pallas_call(
+        kernel,
+        out_shape=jax.ShapeDtypeStruct(block.shape, block.dtype),
+        in_specs=[VMEM],
+        out_specs=HBM,
+        scratch_shapes=[pltpu.SemaphoreType.DMA],
+        compiler_params=pltpu.CompilerParams(vmem_limit_bytes=2 * MIB),
+        cost_estimate=pl.CostEstimate(
+            flops=0, bytes_accessed=2 * block.size, transcendentals=0
+        ),
+        name="write_first",
+    )(block)
+
+
+def combine(picker, returned, block, written):
+    slots, tok_count = picker.shape
+    width = returned.shape[1]
+    rows = block.shape[0] // 2
+    chunk = 512 if width % 512 == 0 else width
+
+    def kernel(pick_ref, back_ref, block_ref, _, sum_out, block_out, held, sem):
+        rest = pl.ds(rows, rows)
+        copies = [pltpu.make_async_copy(block_ref.at[rest], block_out.at[rest], sem.at[0])]
+        copies[0].start()
+        chooser = pick_ref[...].T
+        for n, c in enumerate(range(0, width, chunk)):
+            cols = slice(c, c + chunk)
+            held[:, cols] = jnp.dot(
+                chooser, back_ref[:, cols], preferred_element_type=F32
+            ).astype(BF16)
+            copies.append(
+                pltpu.make_async_copy(held.at[:, cols], sum_out.at[:, cols], sem.at[1 + n])
+            )
+            copies[-1].start()
+        for copy in copies:
+            copy.wait()
+
+    return pl.pallas_call(
+        kernel,
+        out_shape=[
+            jax.ShapeDtypeStruct((tok_count, width), BF16),
+            jax.ShapeDtypeStruct(block.shape, block.dtype),
+        ],
+        in_specs=[VMEM, VMEM, VMEM, HBM],
+        out_specs=[HBM, HBM],
+        scratch_shapes=[
+            pltpu.VMEM((tok_count, width), BF16),
+            pltpu.SemaphoreType.DMA((1 + width // chunk,)),
+        ],
+        input_output_aliases={3: 1},
+        compiler_params=pltpu.CompilerParams(vmem_limit_bytes=4 * MIB),
+        cost_estimate=pl.CostEstimate(
+            flops=2 * slots * tok_count * width,
+            bytes_accessed=2 * tok_count * width + block.size,
             transcendentals=0,
         ),
-        name=name,
-    )(own, other, *lefts)
+        name="combine",
+    )(picker, returned, block, written)
 
 
 def per_device(
@@ -367,41 +446,27 @@
     picker, keep, give, my_tokens, my_grads = route(
         hot_experts, routing, gates, modality, tokens, grad_out
     )
-    slots = (keep, swap(give))
-    tok_rows = (my_tokens, swap(tokens))
-    grad_rows = (my_grads, swap(grad_out))
-    hops = range(len(HOPS))
-    tok_msgs = pick(slots, tok_rows, None, [(k, (0,)) for k in hops[:FAR]], 1, "pick_far")
-    rest = [(k, (1,)) for k in hops[:FAR]] + [(k, (0, 1)) for k in hops[FAR:]]
-    rest_msgs = pick(slots, tok_rows, grad_rows, rest, 2, "pick_rest")
-    scl_msgs, near_msgs = rest_msgs[:FAR], rest_msgs[FAR:]
-    got_tok = [travel(m, hop) for m, hop in zip(tok_msgs, HOPS)]
-    got_near = [travel(m, hop) for m, hop in zip(near_msgs, HOPS[FAR:])]
-    got_scl = [travel(m, hop) for m, hop in zip(scl_msgs, HOPS)]
-    half = 2 * HOTCAP
-    own_tok = jnp.concatenate(got_tok + [block[:half] for block in got_near], axis=0)
-    other_tok = swap(own_tok)
-    pre = pre_activations(own_tok, other_tok, gate_weight, up_weight, down_weight)
-    got_scl, pre = lax.optimization_barrier((got_scl, pre))
-    own_scl = jnp.concatenate(got_scl + [block[half:] for block in got_near], axis=0)
-    other_scl = swap(own_scl)
-    dh, du, act, mine, theirs = activation_grads(own_scl, other_scl, *pre)
-    (grad_down,) = weight_grads(own_scl, other_scl, [act], "down_grad")
-    added, grad_down = lax.optimization_barrier((swap(theirs), grad_down))
+    msgs = pick(keep, swap(give), my_tokens, swap(tokens), my_grads, swap(grad_out))
+    got = [travel(m, hop) for m, hop in zip(msgs, HOPS)]
+    halves = load_weights(gate_weight, up_weight, down_weight)
+    got, halves = lax.optimization_barrier((got, halves))
+    own = jnp.concatenate(got, axis=0)
+    blocks = [own, swap(own)]
+    tok, scl, dh, du, act, mine, theirs = activation_grads(blocks, *halves)
+    down_block = weight_grad(scl, act, "down_grad")
+    added, down_block = lax.optimization_barrier((swap(theirs), down_block))
     pieces = (mine + added.astype(F32)).astype(BF16)
     back = [
         travel(pieces[2 * k * HOTCAP : 2 * (k + 1) * HOTCAP], hop) for k, hop in enumerate(HOPS)
     ]
-    grad_gate, grad_up = weight_grads(own_tok, other_tok, [dh, du], "gate_up_grads")
-    back, grad_gate, grad_up = lax.optimization_barrier((back, grad_gate, grad_up))
+    grad_gate, grad_down, up_block = gate_up_grads(tok, dh, du, down_block)
+    back, up_block = lax.optimization_barrier((back[::-1], up_block))
+    back = back[::-1]
     kept = jnp.concatenate([block[:HOTCAP] for block in back], axis=0)
     given = swap(jnp.concatenate([block[HOTCAP:] for block in back], axis=0))
-    grad_tokens = lax.dot_general(
-        picker,
-        jnp.concatenate([kept, given], axis=0),
-        (((0,), (0,)), ((), ())),
-        preferred_element_type=F32,
-    ).astype(BF16)
+    given, written = lax.optimization_barrier((given, write_first(up_block)))
+    returned = jnp.concatenate([kept, given], axis=0)
+    grad_tokens, grad_up = combine(picker, returned, up_block, written)
     return grad_tokens, grad_gate, grad_up, grad_down
 
 

time: 65.8 us -> 62.8 us (0.954)
  starting transfers between devices: 21.1 us -> 18.5 us
  Pallas kernels: 28.3 us -> 30.9 us
  waiting for transfers between devices: 13.6 us -> 11.8 us
  matrix products: 1.34 us -> 0 us
    pallas_call x6 -> x7, Pallas kernels: 26.1 us -> 28.6 us  [the longest x1 8.07 us: activation_grads(): pl.pallas_call(kernel, out_shape=[pltpu.VMEM((2 * rows, width), BF16)] *...]
    ppermute x10 -> x8, starting transfers between devices: 19.5 us -> 17.1 us  [travel(): return lax.ppermute(block, ('expert', 'dp'), moves)]
    dot_general x1 -> x0, matrix products: 1.34 us -> none  [per_device(): lax.dot_general(picker, jnp.concatenate([kept, given], axis=0), (((0,), (...]
    ppermute x10 -> x8, waiting for transfers between devices: 9.45 us -> 8.46 us  [travel(): return lax.ppermute(block, ('expert', 'dp'), moves)]
    ppermute x7 -> x6, waiting for transfers between devices: 4.18 us -> 3.36 us  [swap(): return lax.ppermute(block, 'dp', [(0, 1), (1, 0)])]
    ppermute x7 -> x6, starting transfers between devices: 1.68 us -> 1.44 us  [swap(): return lax.ppermute(block, 'dp', [(0, 1), (1, 0)])]
  transfers between devices with their start and end apart: 17 -> 14, of which waited for: 7 -> 4; matrix products, arithmetic and copies ran while one was open for 0% -> 0% of each run, Pallas kernels for 34% -> 30%
where the time goes in v4:
time: 62.8 us; the launch traced here: 62.5 us
  Pallas kernels  30.9 us (49%)
  starting transfers between devices  18.5 us (29%)
  waiting for transfers between devices  11.8 us (19%)
  between operations  1.03 us (2%)
    ppermute x8, starting transfers between devices, travel(): return lax.ppermute(block, ('expert', 'dp'), moves)  17.1 us
    ppermute x8, waiting for transfers between devices, travel(): return lax.ppermute(block, ('expert', 'dp'), moves)  8.46 us
    pallas_call x1, Pallas kernels, activation_grads(): pl.pallas_call(kernel, out_shape=[pltpu.VMEM((2 * rows, width), BF16)] *...  8.07 us
    pallas_call x1, Pallas kernels, load_weights(): pl.pallas_call(kernel, out_shape=[pltpu.VMEM((half, width), BF16)] * coun...  7.3 us
    pallas_call x1, Pallas kernels, gate_up_grads(): pl.pallas_call(kernel, out_shape=[full, full, pltpu.VMEM((half, width), B...  5.36 us
    ppermute x6, waiting for transfers between devices, swap(): return lax.ppermute(block, 'dp', [(0, 1), (1, 0)])  3.36 us
    pallas_call x1, Pallas kernels, route(): pl.pallas_call(kernel, out_shape=[pltpu.VMEM((slots, tok_count), BF16), p...  2.27 us
    pallas_call x1, Pallas kernels, combine(): pl.pallas_call(kernel, out_shape=[jax.ShapeDtypeStruct((tok_count, width)...  2.2 us
  transfers between devices with their start and end apart: 14, of which 4 were waited for; matrix products, arithmetic and copies ran while one was open for 0% of the time, Pallas kernels for 30%

profile of v4, /device:TPU:0, one launch (start us, length us, event | category | flops | bytes accessed | tf_op | source)
XLA Modules:
  0.0 62.5 jit_solution(17135419970892642422)
XLA Ops:
  0.6 0.5 collective-permute-start.1
  1.2 0.1 collective-permute-start.2
  1.2 2.3 %route.1 = (bf16[64,128]{1,0:T(8,128)(2,1)S(1)}, f32[32,128]{1,0:T(8,128)S(1)}, f32[32,128]{1,0:T(8,128)S(1)}, bf16[128,3584]{1,0:T(8,128)(2,1)S(1)}, bf16[128,3584]{1,0:T(8,128)(2,1)S(1)}) custom-call(s32[2]{0:T(128)} %hot_ref.1, s32[8,128]{1,0:T(8,128)} %bitcast.3, f32[8,128]{1,0:T(8,128)} %bitcast.4, s32[1,128]{1,0:T(1,128)} %bitcast.5, ...), custom_call_target="tpu_custom_call" | custom-call | tf_op jit(solution)/shard_map/route/pallas_call | solution.py:146
  3.5 0.5 collective-permute-start
  4.0 0.8 %collective-permute-done.theirs_ref = f32[32,128]{1,0:T(8,128)S(1)} collective-permute-done((f32[32,128]{1,0:T(8,128)S(1)}, f32[32,128]{1,0:T(8,128)S(1)}, u32[]{:S(2)}, u32[]{:S(2)}) %collective-permute-start) | collective-permute-done | bytes 16416 | tf_op jit(solution)/shard_map/ppermute | solution.py:438
  4.8 0.0 collective-permute-done.1.their_tok
  4.8 0.1 collective-permute-done.2.their_grad
  4.9 1.8 %pick.1 = (bf16[32,3584]{1,0:T(8,128)(2,1)S(1)}, bf16[32,3584]{1,0:T(8,128)(2,1)S(1)}, bf16[32,3584]{1,0:T(8,128)(2,1)S(1)}, bf16[32,3584]{1,0:T(8,128)(2,1)S(1)}) custom-call(f32[32,128]{1,0:T(8,128)S(1)} %get-tuple-element.45.mine_ref, f32[32,128]{1,0:T(8,128)S(1)} %collective-permute-done.theirs_ref, bf16[128,3584]{1,0:T(8,128)(2,1)S(1)} %get-tuple-element.47.my_tok, ...), custom_call_target="tpu_custom_call" | custom-call | flops 117440512 | bytes 4587520 | tf_op jit(solution)/shard_map/pick/pallas_call | solution.py:187
  6.7 6.0 %collective-permute-start.3 = (bf16[32,3584]{1,0:T(8,128)(2,1)S(1)}, bf16[32,3584]{1,0:T(8,128)(2,1)S(1)}, u32[]{:S(2)}, u32[]{:S(2)}) collective-permute-start(bf16[32,3584]{1,0:T(8,128)(2,1)S(1)} %get-tuple-element.49), channel_id=1, source_target_pairs={{0,14},{1,13},{2,12},{3,15},{4,10},{5,9},{6,8},{7,11},{8,6},{9,5},... | collective-permute-start | bytes 688136 | tf_op jit(solution)/shard_map/ppermute | solution.py:444
  12.7 0.0 collective-permute-start.4
  12.7 0.8 %collective-permute-start.5 = (bf16[32,3584]{1,0:T(8,128)(2,1)S(1)}, bf16[32,3584]{1,0:T(8,128)(2,1)S(1)}, u32[]{:S(2)}, u32[]{:S(2)}) collective-permute-start(bf16[32,3584]{1,0:T(8,128)(2,1)S(1)} %get-tuple-element.51), channel_id=1, source_target_pairs={{0,4},{1,7},{2,6},{3,5},{4,0},{5,3},{6,2},{7,1},{8,12},{9,15},{10,... | collective-permute-start | bytes 688136 | tf_op jit(solution)/shard_map/ppermute | solution.py:444
  13.4 2.3 %collective-permute-start.6 = (bf16[32,3584]{1,0:T(8,128)(2,1)S(1)}, bf16[32,3584]{1,0:T(8,128)(2,1)S(1)}, u32[]{:S(2)}, u32[]{:S(2)}) collective-permute-start(bf16[32,3584]{1,0:T(8,128)(2,1)S(1)} %get-tuple-element.52), channel_id=1, source_target_pairs={{0,2},{1,1},{2,0},{3,3},{4,6},{5,5},{6,4},{7,7},{8,10},{9,9},{10,8... | collective-permute-start | bytes 688136 | tf_op jit(solution)/shard_map/ppermute | solution.py:444
  15.8 7.3 %load_weights.1 = (bf16[1024,3584]{1,0:T(8,128)(2,1)S(1)}, bf16[1024,3584]{1,0:T(8,128)(2,1)S(1)}, bf16[1024,3584]{1,0:T(8,128)(2,1)S(1)}) custom-call(bf16[2048,3584]{1,0:T(8,128)(2,1)} %refs_0_.1, bf16[2048,3584]{1,0:T(8,128)(2,1)} %refs_1_.1, bf16[2048,3584]{1,0:T(8,128)(2,1)} %refs_2_.1), custom_call_target="tpu_custom_call" | custom-call | bytes 44040192 | tf_op jit(solution)/shard_map/load_weights/pallas_call | solution.py:220
  23.1 0.0 collective-permute-done.3
  23.1 8.4 %collective-permute-done.4 = bf16[32,3584]{1,0:T(8,128)(2,1)S(1)} collective-permute-done((bf16[32,3584]{1,0:T(8,128)(2,1)S(1)}, bf16[32,3584]{1,0:T(8,128)(2,1)S(1)}, u32[]{:S(2)}, u32[]{:S(2)}) %collective-permute-start.4) | collective-permute-done | bytes 229408 | tf_op jit(solution)/shard_map/ppermute | solution.py:444
  31.5 0.0 collective-permute-done.5
  31.5 0.0 collective-permute-done.6
  31.6 0.1 collective-permute-start.7
  31.7 2.5 %collective-permute-done.7.refs_1_ = bf16[128,3584]{1,0:T(8,128)(2,1)S(1)} collective-permute-done((bf16[128,3584]{1,0:T(8,128)(2,1)S(1)}, bf16[128,3584]{1,0:T(8,128)(2,1)S(1)}, u32[]{:S(2)}, u32[]{:S(2)}) %collective-permute-start.7) | collective-permute-done | bytes 917536 | tf_op jit(solution)/shard_map/ppermute | solution.py:438
  34.2 8.1 %activation_grads.1 = (bf16[128,3584]{1,0:T(8,128)(2,1)S(1)}, bf16[128,3584]{1,0:T(8,128)(2,1)S(1)}, bf16[1024,128]{1,0:T(8,128)(2,1)S(1)}, bf16[1024,128]{1,0:T...) custom-call(bf16[128,3584]{1,0:T(8,128)(2,1)S(1)} %constant_dynamic-update-sli, ...), custom_call_target="tpu_custom_call" | custom-call | flops 4697620480 | bytes 22020096 | tf_op jit(solution)/shard_map/activation_grads/pallas_call | solution.py:275
  42.2 0.2 collective-permute-start.8
  42.4 2.1 %down_grad.1.down_ref = bf16[1024,3584]{1,0:T(8,128)(2,1)S(1)} custom-call(bf16[128,3584]{1,0:T(8,128)(2,1)S(1)} %get-tuple-element.65.rows_ref, bf16[1024,128]{1,0:T(8,128)(2,1)S(1)} %get-tuple-element.66.left_ref), custom_call_target="tpu_custom_call" | custom-call | flops 939524096 | bytes 7340032 | tf_op jit(solution)/shard_map/down_grad/pallas_call | solution.py:310
  44.5 0.0 collective-permute-done.8
  44.5 0.1 add_convert_fusion
  44.6 3.5 %collective-permute-start.12 = (bf16[16,3584]{1,0:T(8,128)(2,1)S(1)}, bf16[16,3584]{1,0:T(8,128)(2,1)S(1)}, u32[]{:S(2)}, u32[]{:S(2)}) collective-permute-start(bf16[16,3584]{1,0:T(8,128)(2,1)S(1)} %get-tuple-element.84), channel_id=1, source_target_pairs={{0,14},{1,13},{2,12},{3,15},{4,10},{5,9},{6,8},{7,11},{8,6},{9,5},... | collective-permute-start | bytes 344072 | tf_op jit(solution)/shard_map/ppermute | solution.py:444
  48.1 0.0 collective-permute-start.11
  48.1 1.9 %collective-permute-start.10 = (bf16[16,3584]{1,0:T(8,128)(2,1)S(1)}, bf16[16,3584]{1,0:T(8,128)(2,1)S(1)}, u32[]{:S(2)}, u32[]{:S(2)}) collective-permute-start(bf16[16,3584]{1,0:T(8,128)(2,1)S(1)} %get-tuple-element.86), channel_id=1, source_target_pairs={{0,4},{1,7},{2,6},{3,5},{4,0},{5,3},{6,2},{7,1},{8,12},{9,15},{10,... | collective-permute-start | bytes 344072 | tf_op jit(solution)/shard_map/ppermute | solution.py:444
  50.0 2.6 %collective-permute-start.9 = (bf16[16,3584]{1,0:T(8,128)(2,1)S(1)}, bf16[16,3584]{1,0:T(8,128)(2,1)S(1)}, u32[]{:S(2)}, u32[]{:S(2)}) collective-permute-start(bf16[16,3584]{1,0:T(8,128)(2,1)S(1)} %get-tuple-element.87), channel_id=1, source_target_pairs={{0,2},{1,1},{2,0},{3,3},{4,6},{5,5},{6,4},{7,7},{8,10},{9,9},{10,8... | collective-permute-start | bytes 344072 | tf_op jit(solution)/shard_map/ppermute | solution.py:444
  52.6 5.4 %gate_up_grads.1 = (bf16[1024,3584]{1,0:T(8,128)(2,1)}, bf16[1024,3584]{1,0:T(8,128)(2,1)}, bf16[1024,3584]{1,0:T(8,128)(2,1)S(1)}) custom-call(bf16[128,3584]{1,0:T(8,128)(2,1)S(1)} %get-tuple-element.68.rows_ref, bf16[1024,128]{1,0:T(8,128)(2,1)S(1)} %get-tuple-element.69.gate_ref, bf16[1024,128]{1,0:T(8,128)(2,1)S(1)} %get-tuple-element.70.up_ref, ...), custom_call_target="tpu_custom_call" | custom-call | flops 1879048192 | bytes 14680064 | tf_op jit(solution)/shard_map/gate_up_grads/pallas_call | solution.py:349
  58.0 0.0 collective-permute-done.12
  58.0 0.0 collective-permute-done.11
  58.0 0.0 collective-permute-done.10
  58.0 0.0 collective-permute-done.9
  58.1 0.1 collective-permute-start.13
  58.2 1.8 %write_first.1._ = bf16[1024,3584]{1,0:T(8,128)(2,1)} custom-call(bf16[1024,3584]{1,0:T(8,128)(2,1)S(1)} %get-tuple-element.77.block_ref), custom_call_target="tpu_custom_call" | custom-call | bytes 7340032 | tf_op jit(solution)/shard_map/write_first/pallas_call | solution.py:374
  60.1 0.0 collective-permute-done.13
  60.1 2.2 %combine.1 = (bf16[128,3584]{1,0:T(8,128)(2,1)}, bf16[1024,3584]{1,0:T(8,128)(2,1)}) custom-call(bf16[64,128]{1,0:T(8,128)(2,1)S(1)} %get-tuple-element.44.pick_ref, bf16[64,3584]{1,0:T(8,128)(2,1)S(1)} %constant_dynamic-update-slice_fusion.4.back_ref, bf16[1024,3584]{1,0:T(8,128)(2,1)S(1)} %get-tuple-element.77.block_ref, ...), custom_call_target="tpu_custom_call", output_to_operand_aliasing={{1}: (3, {})} | custom-call | flops 58720256 | bytes 4587520 | tf_op jit(solution)/shard_map/combine/pallas_call | solution.py:411
  (11 shorter events, 0.2 us)
Async XLA Ops:
  0.6 4.2 %collective-permute-start.1 = (bf16[128,3584]{1,0:T(8,128)(2,1)}, bf16[128,3584]{1,0:T(8,128)(2,1)S(1)}, u32[]{:S(2)}, u32[]{:S(2)}) collective-permute-start(bf16[128,3584]{1,0:T(8,128)(2,1)} %tok_in.1), channel_id=1, source_target_pairs={{0,1},{1,0},{2,3},{3,2},{4,5},{5,4},{6,7},{7,6},{8,9},{9,8},{10,11... | collective-permute-start | bytes 2752520 | tf_op jit(solution)/shard_map/ppermute | solution.py:438
  1.2 3.8 %collective-permute-start.2 = (bf16[128,3584]{1,0:T(8,128)(2,1)}, bf16[128,3584]{1,0:T(8,128)(2,1)}, u32[]{:S(2)}, u32[]{:S(2)}) collective-permute-start(bf16[128,3584]{1,0:T(8,128)(2,1)} %gout_in.1), channel_id=1, source_target_pairs={{0,1},{1,0},{2,3},{3,2},{4,5},{5,4},{6,7},{7,6},{8,9},{9,8},{10,11... | collective-permute-start | bytes 2752520 | tf_op jit(solution)/shard_map/ppermute | solution.py:438
  3.5 1.3 %collective-permute-start = (f32[32,128]{1,0:T(8,128)S(1)}, f32[32,128]{1,0:T(8,128)S(1)}, u32[]{:S(2)}, u32[]{:S(2)}) collective-permute-start(f32[32,128]{1,0:T(8,128)S(1)} %get-tuple-element.46), channel_id=1, source_target_pairs={{0,1},{1,0},{2,3},{3,2},{4,5},{5,4},{6,7},{7,6},{8,9},{9,8},{10,11... | collective-permute-start | bytes 49160 | tf_op jit(solution)/shard_map/ppermute | solution.py:438
  6.7 16.4 %collective-permute-start.3 = (bf16[32,3584]{1,0:T(8,128)(2,1)S(1)}, bf16[32,3584]{1,0:T(8,128)(2,1)S(1)}, u32[]{:S(2)}, u32[]{:S(2)}) collective-permute-start(bf16[32,3584]{1,0:T(8,128)(2,1)S(1)} %get-tuple-element.49), channel_id=1, source_target_pairs={{0,14},{1,13},{2,12},{3,15},{4,10},{5,9},{6,8},{7,11},{8,6},{9,5},... | collective-permute-start | bytes 688136 | tf_op jit(solution)/shard_map/ppermute | solution.py:444
  12.7 18.9 %collective-permute-start.4 = (bf16[32,3584]{1,0:T(8,128)(2,1)S(1)}, bf16[32,3584]{1,0:T(8,128)(2,1)S(1)}, u32[]{:S(2)}, u32[]{:S(2)}) collective-permute-start(bf16[32,3584]{1,0:T(8,128)(2,1)S(1)} %get-tuple-element.50), channel_id=1, source_target_pairs={{0,8},{1,11},{2,10},{3,9},{4,12},{5,15},{6,14},{7,13},{8,0},{9,3},... | collective-permute-start | bytes 688136 | tf_op jit(solution)/shard_map/ppermute | solution.py:444
  12.7 18.9 %collective-permute-start.5 = (bf16[32,3584]{1,0:T(8,128)(2,1)S(1)}, bf16[32,3584]{1,0:T(8,128)(2,1)S(1)}, u32[]{:S(2)}, u32[]{:S(2)}) collective-permute-start(bf16[32,3584]{1,0:T(8,128)(2,1)S(1)} %get-tuple-element.51), channel_id=1, source_target_pairs={{0,4},{1,7},{2,6},{3,5},{4,0},{5,3},{6,2},{7,1},{8,12},{9,15},{10,... | collective-permute-start | bytes 688136 | tf_op jit(solution)/shard_map/ppermute | solution.py:444
  13.4 18.1 %collective-permute-start.6 = (bf16[32,3584]{1,0:T(8,128)(2,1)S(1)}, bf16[32,3584]{1,0:T(8,128)(2,1)S(1)}, u32[]{:S(2)}, u32[]{:S(2)}) collective-permute-start(bf16[32,3584]{1,0:T(8,128)(2,1)S(1)} %get-tuple-element.52), channel_id=1, source_target_pairs={{0,2},{1,1},{2,0},{3,3},{4,6},{5,5},{6,4},{7,7},{8,10},{9,9},{10,8... | collective-permute-start | bytes 688136 | tf_op jit(solution)/shard_map/ppermute | solution.py:444
  31.6 2.5 %collective-permute-start.7 = (bf16[128,3584]{1,0:T(8,128)(2,1)S(1)}, bf16[128,3584]{1,0:T(8,128)(2,1)S(1)}, u32[]{:S(2)}, u32[]{:S(2)}) collective-permute-start(bf16[128,3584]{1,0:T(8,128)(2,1)S(1)} %constant_dynamic-update-slice_fusion.refs_0_), channel_id=1, source_target_pairs={{0,1},{1,0},{2,3},{3,2},{4,5},{5,4},{6,7},{7,6},{8,9},{9,8},{10,11... | collective-permute-start | bytes 2752520 | tf_op jit(solution)/shard_map/ppermute | solution.py:438
  42.2 2.3 %collective-permute-start.8 = (bf16[64,3584]{1,0:T(8,128)(2,1)S(1)}, bf16[64,3584]{1,0:T(8,128)(2,1)S(1)}, u32[]{:S(2)}, u32[]{:S(2)}) collective-permute-start(bf16[64,3584]{1,0:T(8,128)(2,1)S(1)} %get-tuple-element.64), channel_id=1, source_target_pairs={{0,1},{1,0},{2,3},{3,2},{4,5},{5,4},{6,7},{7,6},{8,9},{9,8},{10,11... | collective-permute-start | bytes 1376264 | tf_op jit(solution)/shard_map/ppermute | solution.py:438
  44.6 13.4 %collective-permute-start.12 = (bf16[16,3584]{1,0:T(8,128)(2,1)S(1)}, bf16[16,3584]{1,0:T(8,128)(2,1)S(1)}, u32[]{:S(2)}, u32[]{:S(2)}) collective-permute-start(bf16[16,3584]{1,0:T(8,128)(2,1)S(1)} %get-tuple-element.84), channel_id=1, source_target_pairs={{0,14},{1,13},{2,12},{3,15},{4,10},{5,9},{6,8},{7,11},{8,6},{9,5},... | collective-permute-start | bytes 344072 | tf_op jit(solution)/shard_map/ppermute | solution.py:444
  48.1 9.9 %collective-permute-start.11 = (bf16[16,3584]{1,0:T(8,128)(2,1)S(1)}, bf16[16,3584]{1,0:T(8,128)(2,1)S(1)}, u32[]{:S(2)}, u32[]{:S(2)}) collective-permute-start(bf16[16,3584]{1,0:T(8,128)(2,1)S(1)} %get-tuple-element.85), channel_id=1, source_target_pairs={{0,8},{1,11},{2,10},{3,9},{4,12},{5,15},{6,14},{7,13},{8,0},{9,3},... | collective-permute-start | bytes 344072 | tf_op jit(solution)/shard_map/ppermute | solution.py:444
  48.1 9.9 %collective-permute-start.10 = (bf16[16,3584]{1,0:T(8,128)(2,1)S(1)}, bf16[16,3584]{1,0:T(8,128)(2,1)S(1)}, u32[]{:S(2)}, u32[]{:S(2)}) collective-permute-start(bf16[16,3584]{1,0:T(8,128)(2,1)S(1)} %get-tuple-element.86), channel_id=1, source_target_pairs={{0,4},{1,7},{2,6},{3,5},{4,0},{5,3},{6,2},{7,1},{8,12},{9,15},{10,... | collective-permute-start | bytes 344072 | tf_op jit(solution)/shard_map/ppermute | solution.py:444
  50.0 8.0 %collective-permute-start.9 = (bf16[16,3584]{1,0:T(8,128)(2,1)S(1)}, bf16[16,3584]{1,0:T(8,128)(2,1)S(1)}, u32[]{:S(2)}, u32[]{:S(2)}) collective-permute-start(bf16[16,3584]{1,0:T(8,128)(2,1)S(1)} %get-tuple-element.87), channel_id=1, source_target_pairs={{0,2},{1,1},{2,0},{3,3},{4,6},{5,5},{6,4},{7,7},{8,10},{9,9},{10,8... | collective-permute-start | bytes 344072 | tf_op jit(solution)/shard_map/ppermute | solution.py:444
  58.1 1.9 %collective-permute-start.13 = (bf16[32,3584]{1,0:T(8,128)(2,1)S(1)}, bf16[32,3584]{1,0:T(8,128)(2,1)S(1)}, u32[]{:S(2)}, u32[]{:S(2)}) collective-permute-start(bf16[32,3584]{1,0:T(8,128)(2,1)S(1)} %pad_maximum_fusion), channel_id=1, source_target_pairs={{0,1},{1,0},{2,3},{3,2},{4,5},{5,4},{6,7},{7,6},{8,9},{9,8},{10,11... | collective-permute-start | bytes 688136 | tf_op jit(solution)/shard_map/ppermute | solution.py:438

commit v5 on v4

--- a/solution.py
+++ b/solution.py
@@ -100,20 +100,13 @@
 HBM = pl.BlockSpec(memory_space=pltpu.HBM)
 
 
-def route(hot_experts, routing, gates, modality, tokens, grad_out):
+def route(hot_experts, routing, gates, modality):
     tok_count, top_count = routing.shape
     hot_count = hot_experts.shape[0]
     slots = FLIGHT * HOTCAP
     hops = len(HOPS)
 
-    def kernel(hot_ref, route_ref, gate_ref, mod_ref, tok_in, gout_in, *rest):
-        choose_ref, keep_ref, give_ref, tok_ref, gout_ref, sem = rest
-        loads = (
-            pltpu.make_async_copy(tok_in, tok_ref, sem.at[0]),
-            pltpu.make_async_copy(gout_in, gout_ref, sem.at[1]),
-        )
-        for load in loads:
-            load.start()
+    def kernel(hot_ref, route_ref, gate_ref, mod_ref, choose_ref, keep_ref, give_ref):
         position = lax.broadcasted_iota(jnp.int32, (top_count, tok_count), 0)
         hot_pick = jnp.zeros((top_count, tok_count), jnp.int32)
         for j in range(hot_count):
@@ -140,8 +133,6 @@
         choose_ref[...] = picker.astype(BF16)
         keep_ref[...] = gated[:CARRIED]
         give_ref[...] = gated[CARRIED:]
-        for load in loads:
-            load.wait()
 
     return pl.pallas_call(
         kernel,
@@ -149,21 +140,38 @@
             pltpu.VMEM((slots, tok_count), BF16),
             pltpu.VMEM((CARRIED, tok_count), F32),
             pltpu.VMEM((slots - CARRIED, tok_count), F32),
-            pltpu.VMEM(tokens.shape, BF16),
-            pltpu.VMEM(grad_out.shape, BF16),
         ],
-        in_specs=[SMEM, VMEM, VMEM, VMEM, HBM, HBM],
-        out_specs=[VMEM] * 5,
-        scratch_shapes=[pltpu.SemaphoreType.DMA((2,))],
+        in_specs=[SMEM, VMEM, VMEM, VMEM],
+        out_specs=[VMEM] * 3,
         name="route",
-    )(
-        hot_experts,
-        routing.T,
-        gates.T,
-        modality[None, :],
-        pltpu.with_memory_space_constraint(tokens, pltpu.HBM),
-        pltpu.with_memory_space_constraint(grad_out, pltpu.HBM),
-    )
+    )(hot_experts, routing.T, gates.T, modality[None, :])
+
+
+def load_rows(*arrays):
+    count = len(arrays)
+
+    def kernel(*refs):
+        loads = [
+            pltpu.make_async_copy(refs[i], refs[count + i], refs[2 * count].at[i])
+            for i in range(count)
+        ]
+        for load in loads:
+            load.start()
+        for load in loads:
+            load.wait()
+
+    return pl.pallas_call(
+        kernel,
+        out_shape=[pltpu.VMEM(array.shape, array.dtype) for array in arrays],
+        in_specs=[HBM] * count,
+        out_specs=[VMEM] * count,
+        scratch_shapes=[pltpu.SemaphoreType.DMA((count,))],
+        compiler_params=pltpu.CompilerParams(vmem_limit_bytes=2 * MIB),
+        cost_estimate=pl.CostEstimate(
+            flops=0, bytes_accessed=4 * sum(array.size for array in arrays), transcendentals=0
+        ),
+        name="load_rows",
+    )(*(pltpu.with_memory_space_constraint(array, pltpu.HBM) for array in arrays))
 
 
 def pick(mine, theirs, my_tokens, their_tokens, my_grads, their_grads):
@@ -199,39 +207,56 @@
     )(mine, theirs, my_tokens, their_tokens, my_grads, their_grads)
 
 
-def load_weights(*weights):
-    half = weights[0].shape[0] // 2
-    width = weights[0].shape[1]
-    count = len(weights)
-
-    def kernel(*refs):
+def load_weights(gate_weight, up_weight, down_weight):
+    half = gate_weight.shape[0] // 2
+    width = gate_weight.shape[1]
+    tile = min(256, half)
+    steps = half // tile
+
+    def kernel(g_in, u_in, w_in, g_ref, u_ref, g_cols, u_cols, w_cols, w_ref, sem):
         first = pl.multiple_of(lax.axis_index("dp") * half, half)
-        loads = [
-            pltpu.make_async_copy(
-                refs[i].at[pl.ds(first, half)], refs[count + i], refs[2 * count].at[i]
+        lanes = ((g_in, g_ref, g_cols), (u_in, u_ref, u_cols), (w_in, w_ref, w_cols))
+        order = [(lane, i) for lane in range(3) for i in range(steps)]
+
+        def load(lane, i):
+            source, target, _ = lanes[lane]
+            return pltpu.make_async_copy(
+                source.at[pl.ds(first + i * tile, tile)],
+                target.at[pl.ds(i * tile, tile)],
+                sem.at[lane, i],
             )
-            for i in range(count)
-        ]
-        for load in loads:
-            load.start()
-        for load in loads:
-            load.wait()
-
-    return pl.pallas_call(
-        kernel,
-        out_shape=[pltpu.VMEM((half, width), BF16)] * count,
-        in_specs=[HBM] * count,
-        out_specs=[VMEM] * count,
-        scratch_shapes=[pltpu.SemaphoreType.DMA((count,))],
-        compiler_params=pltpu.CompilerParams(vmem_limit_bytes=2 * MIB),
-        cost_estimate=pl.CostEstimate(
-            flops=0, bytes_accessed=4 * count * half * width, transcendentals=0
+
+        depth = 3
+        for step in order[:depth]:
+            load(*step).start()
+        for n, (lane, i) in enumerate(order):
+            load(lane, i).wait()
+            if n + depth < len(order):
+                load(*order[n + depth]).start()
+            _, target, columns = lanes[lane]
+            columns[:, i * tile : (i + 1) * tile] = target[i * tile : (i + 1) * tile].T
+
+    return pl.pallas_call(
+        kernel,
+        out_shape=[pltpu.VMEM((half, width), BF16)] * 2
+        + [pltpu.VMEM((width, half), BF16)] * 3,
+        in_specs=[HBM] * 3,
+        out_specs=[VMEM] * 5,
+        scratch_shapes=[pltpu.VMEM((half, width), BF16), pltpu.SemaphoreType.DMA((3, steps))],
+        compiler_params=pltpu.CompilerParams(vmem_limit_bytes=10 * MIB),
+        cost_estimate=pl.CostEstimate(
+            flops=0, bytes_accessed=12 * half * width, transcendentals=0
         ),
         name="load_weights",
-    )(*(pltpu.with_memory_space_constraint(weight, pltpu.HBM) for weight in weights))
-
-
-def activation_grads(blocks, gate_half, up_half, down_half):
+    )(
+        *(
+            pltpu.with_memory_space_constraint(weight, pltpu.HBM)
+            for weight in (gate_weight, up_weight, down_weight)
+        )
+    )
+
+
+def activation_grads(blocks, gate_half, up_half, gate_cols, up_cols, down_cols):
     width = blocks[0].shape[1]
     rows = 2 * HOTCAP * len(HOPS)
     half = gate_half.shape[0]
@@ -240,8 +265,8 @@
 
     def kernel(*refs):
         ins, refs = refs[: len(blocks)], refs[len(blocks) :]
-        g_ref, u_ref, w_ref, tok_ref, scl_ref, dh_ref, du_ref, act_ref = refs[:8]
-        mine_ref, theirs_ref, tok_cols, scl_cols, dh_rows, du_rows = refs[8:]
+        g_ref, u_ref, g_cols, u_cols, w_cols, tok_ref, scl_ref = refs[:7]
+        dh_ref, du_ref, act_ref, mine_ref, theirs_ref, dh_rows, du_rows = refs[7:]
         message = 2 * HOTCAP
         place = 0
         for block in ins:
@@ -249,22 +274,20 @@
                 tok_ref[place : place + message] = block[start : start + message]
                 scl_ref[place : place + message] = block[start + message : start + 2 * message]
                 place += message
-        tok_cols[...] = tok_ref[...].T
-        scl_cols[...] = scl_ref[...].T
         for i in range(half // tile):
             part = slice(i * tile, (i + 1) * tile)
-            pre = jnp.dot(g_ref[part], tok_cols[...], preferred_element_type=F32)
-            up = jnp.dot(u_ref[part], tok_cols[...], preferred_element_type=F32)
-            da = jnp.dot(w_ref[part], scl_cols[...], preferred_element_type=F32)
+            pre = jnp.dot(tok_ref[...], g_cols[:, part], preferred_element_type=F32)
+            up = jnp.dot(tok_ref[...], u_cols[:, part], preferred_element_type=F32)
+            da = jnp.dot(scl_ref[...], w_cols[:, part], preferred_element_type=F32)
             sig = jax.nn.sigmoid(pre)
             swish = pre * sig
-            act_ref[part] = (swish * up).astype(BF16)
+            act_ref[part] = (swish * up).astype(BF16).T
             dh = (da * up * sig * (1.0 + pre * (1.0 - sig))).astype(BF16)
             du = (da * swish).astype(BF16)
-            dh_ref[part] = dh
-            du_ref[part] = du
-            dh_rows[:, part] = dh.T
-            du_rows[:, part] = du.T
+            dh_ref[part] = dh.T
+            du_ref[part] = du.T
+            dh_rows[:, part] = dh
+            du_rows[:, part] = du
         for c in range(0, width, chunk):
             cols = slice(c, c + chunk)
             piece = jnp.dot(dh_rows[...], g_ref[:, cols], preferred_element_type=F32)
@@ -277,22 +300,17 @@
         out_shape=[pltpu.VMEM((2 * rows, width), BF16)] * 2
         + [pltpu.VMEM((half, 2 * rows), BF16)] * 3
         + [pltpu.VMEM((rows, width), F32), pltpu.VMEM((rows, width), BF16)],
-        in_specs=[VMEM] * (len(blocks) + 3),
+        in_specs=[VMEM] * (len(blocks) + 5),
         out_specs=[VMEM] * 7,
-        scratch_shapes=[
-            pltpu.VMEM((width, 2 * rows), BF16),
-            pltpu.VMEM((width, 2 * rows), BF16),
-            pltpu.VMEM((2 * rows, half), BF16),
-            pltpu.VMEM((2 * rows, half), BF16),
-        ],
-        compiler_params=pltpu.CompilerParams(vmem_limit_bytes=12 * MIB),
+        scratch_shapes=[pltpu.VMEM((2 * rows, half), BF16)] * 2,
+        compiler_params=pltpu.CompilerParams(vmem_limit_bytes=8 * MIB),
         cost_estimate=pl.CostEstimate(
             flops=20 * rows * half * width,
             bytes_accessed=6 * half * width,
             transcendentals=2 * rows * half,
         ),
         name="activation_grads",
-    )(*blocks, gate_half, up_half, down_half)
+    )(*blocks, gate_half, up_half, gate_cols, up_cols, down_cols)
 
 
 def weight_grad(rows, left, name):
@@ -443,9 +461,8 @@
         ]
         return lax.ppermute(block, ("expert", "dp"), moves)
 
-    picker, keep, give, my_tokens, my_grads = route(
-        hot_experts, routing, gates, modality, tokens, grad_out
-    )
+    picker, keep, give = route(hot_experts, routing, gates, modality)
+    my_tokens, my_grads = load_rows(tokens, grad_out)
     msgs = pick(keep, swap(give), my_tokens, swap(tokens), my_grads, swap(grad_out))
     got = [travel(m, hop) for m, hop in zip(msgs, HOPS)]
     halves = load_weights(gate_weight, up_weight, down_weight)

time: 62.8 us -> 59.1 us (0.941)
  Pallas kernels: 30.9 us -> 29.1 us
  waiting for transfers between devices: 11.8 us -> 10.1 us
    pallas_call x1 -> x2, Pallas kernels: 7.3 us -> 10.2 us  [the longest x1 8.7 us: load_weights(): pl.pallas_call(kernel, out_shape=[pltpu.VMEM((half, width), BF16)] * 2 +...]
    pallas_call x1, Pallas kernels: 8.07 us -> 5.69 us  [activation_grads(): pl.pallas_call(kernel, out_shape=[pltpu.VMEM((2 * rows, width), BF16)] *...]
    ppermute x8, waiting for transfers between devices: 8.46 us -> 7.07 us  [travel(): return lax.ppermute(block, ('expert', 'dp'), moves)]
    pallas_call x1, Pallas kernels: 2.27 us -> 0.95 us  [route(): pl.pallas_call(kernel, out_shape=[pltpu.VMEM((slots, tok_count), BF16), p...]
    pallas_call x1, Pallas kernels: 1.78 us -> 0.61 us  [pick(): pl.pallas_call(kernel, out_shape=[pltpu.VMEM((4 * HOTCAP, width), BF16)]...]
  transfers between devices with their start and end apart: 14 -> 14, of which waited for: 4 -> 4; matrix products, arithmetic and copies ran while one was open for 0% -> 0% of each run, Pallas kernels for 30% -> 35%
where the time goes in v5:
time: 59.1 us; the launch traced here: 58.8 us
  Pallas kernels  29.1 us (49%)
  starting transfers between devices  18.3 us (31%)
  waiting for transfers between devices  10.1 us (17%)
  between operations  1.03 us (2%)
    ppermute x8, starting transfers between devices, travel(): return lax.ppermute(block, ('expert', 'dp'), moves)  16.9 us
    pallas_call x1, Pallas kernels, load_weights(): pl.pallas_call(kernel, out_shape=[pltpu.VMEM((half, width), BF16)] * 2 +...  8.7 us
    ppermute x8, waiting for transfers between devices, travel(): return lax.ppermute(block, ('expert', 'dp'), moves)  7.07 us
    pallas_call x1, Pallas kernels, activation_grads(): pl.pallas_call(kernel, out_shape=[pltpu.VMEM((2 * rows, width), BF16)] *...  5.69 us
    pallas_call x1, Pallas kernels, gate_up_grads(): pl.pallas_call(kernel, out_shape=[full, full, pltpu.VMEM((half, width), B...  5.36 us
    ppermute x6, waiting for transfers between devices, swap(): return lax.ppermute(block, 'dp', [(0, 1), (1, 0)])  3.07 us
    pallas_call x1, Pallas kernels, weight_grad(): pl.pallas_call(kernel, out_shape=pltpu.VMEM((half, width), BF16), in_spec...  2.25 us
    pallas_call x1, Pallas kernels, combine(): pl.pallas_call(kernel, out_shape=[jax.ShapeDtypeStruct((tok_count, width)...  2.2 us
  transfers between devices with their start and end apart: 14, of which 4 were waited for; matrix products, arithmetic and copies ran while one was open for 0% of the time, Pallas kernels for 35%

profile of v5, /device:TPU:0, one launch (start us, length us, event | category | flops | bytes accessed | tf_op | source)
XLA Modules:
  0.0 58.8 jit_solution(2950196147770382374)
XLA Ops:
  0.6 0.5 collective-permute-start.1
  1.1 0.1 collective-permute-start.2
  1.2 1.0 %route.1 = (bf16[64,128]{1,0:T(8,128)(2,1)S(1)}, f32[32,128]{1,0:T(8,128)S(1)}, f32[32,128]{1,0:T(8,128)S(1)}) custom-call(s32[2]{0:T(128)} %hot_ref.1, s32[8,128]{1,0:T(8,128)} %bitcast.3, f32[8,128]{1,0:T(8,128)} %bitcast.4, s32[1,128]{1,0:T(1,128)} %bitcast.5), custom_call_target="tpu_custom_call" | custom-call | tf_op jit(solution)/shard_map/route/pallas_call | solution.py:137
  2.2 0.5 collective-permute-start
  2.7 1.5 %load_rows.1 = (bf16[128,3584]{1,0:T(8,128)(2,1)S(1)}, bf16[128,3584]{1,0:T(8,128)(2,1)S(1)}) custom-call(bf16[128,3584]{1,0:T(8,128)(2,1)} %refs_0_.1, bf16[128,3584]{1,0:T(8,128)(2,1)} %refs_1_.1), custom_call_target="tpu_custom_call" | custom-call | bytes 3670016 | tf_op jit(solution)/shard_map/load_rows/pallas_call | solution.py:163
  4.2 0.4 collective-permute-done.theirs_ref
  4.6 0.0 collective-permute-done.1.their_tok
  4.6 0.2 collective-permute-done.2.their_grad
  4.8 0.6 %pick.1 = (bf16[32,3584]{1,0:T(8,128)(2,1)S(1)}, bf16[32,3584]{1,0:T(8,128)(2,1)S(1)}, bf16[32,3584]{1,0:T(8,128)(2,1)S(1)}, bf16[32,3584]{1,0:T(8,128)(2,1)S(1)}) custom-call(f32[32,128]{1,0:T(8,128)S(1)} %get-tuple-element.49.mine_ref, f32[32,128]{1,0:T(8,128)S(1)} %collective-permute-done.theirs_ref, bf16[128,3584]{1,0:T(8,128)(2,1)S(1)} %get-tuple-element.51.my_tok, ...), custom_call_target="tpu_custom_call" | custom-call | flops 117440512 | bytes 4587520 | tf_op jit(solution)/shard_map/pick/pallas_call | solution.py:195
  5.4 6.0 %collective-permute-start.3 = (bf16[32,3584]{1,0:T(8,128)(2,1)S(1)}, bf16[32,3584]{1,0:T(8,128)(2,1)S(1)}, u32[]{:S(2)}, u32[]{:S(2)}) collective-permute-start(bf16[32,3584]{1,0:T(8,128)(2,1)S(1)} %get-tuple-element.53), channel_id=1, source_target_pairs={{0,14},{1,13},{2,12},{3,15},{4,10},{5,9},{6,8},{7,11},{8,6},{9,5},... | collective-permute-start | bytes 688136 | tf_op jit(solution)/shard_map/ppermute | solution.py:462
  11.3 0.0 collective-permute-start.4
  11.3 0.8 %collective-permute-start.5 = (bf16[32,3584]{1,0:T(8,128)(2,1)S(1)}, bf16[32,3584]{1,0:T(8,128)(2,1)S(1)}, u32[]{:S(2)}, u32[]{:S(2)}) collective-permute-start(bf16[32,3584]{1,0:T(8,128)(2,1)S(1)} %get-tuple-element.55), channel_id=1, source_target_pairs={{0,4},{1,7},{2,6},{3,5},{4,0},{5,3},{6,2},{7,1},{8,12},{9,15},{10,... | collective-permute-start | bytes 688136 | tf_op jit(solution)/shard_map/ppermute | solution.py:462
  12.1 2.3 %collective-permute-start.6 = (bf16[32,3584]{1,0:T(8,128)(2,1)S(1)}, bf16[32,3584]{1,0:T(8,128)(2,1)S(1)}, u32[]{:S(2)}, u32[]{:S(2)}) collective-permute-start(bf16[32,3584]{1,0:T(8,128)(2,1)S(1)} %get-tuple-element.56), channel_id=1, source_target_pairs={{0,2},{1,1},{2,0},{3,3},{4,6},{5,5},{6,4},{7,7},{8,10},{9,9},{10,8... | collective-permute-start | bytes 688136 | tf_op jit(solution)/shard_map/ppermute | solution.py:462
  14.5 8.7 %load_weights.1 = (bf16[1024,3584]{1,0:T(8,128)(2,1)S(1)}, bf16[1024,3584]{1,0:T(8,128)(2,1)S(1)}, bf16[3584,1024]{1,0:T(8,128)(2,1)S(1)}, bf16[3584,1024]{1,0:T(8,128)(2,1)S(1)}, bf16[3584,1024]{1,0:T(8,128)(2,1)S(1)}) custom-call(bf16[2048,3584]{1,0:T(8,128)(2,1)} %g_in.1, bf16[2048,3584]{1,0:T(8,128)(2,1)} %u_in.1, bf16[2048,3584]{1,0:T(8,128)(2,1)} %w_in.1), custom_call_target="tpu_custom_call" | custom-call | bytes 44040192 | tf_op jit(solution)/shard_map/load_weights/pallas_call | solution.py:239
  23.2 0.0 collective-permute-done.3
  23.2 7.1 %collective-permute-done.4 = bf16[32,3584]{1,0:T(8,128)(2,1)S(1)} collective-permute-done((bf16[32,3584]{1,0:T(8,128)(2,1)S(1)}, bf16[32,3584]{1,0:T(8,128)(2,1)S(1)}, u32[]{:S(2)}, u32[]{:S(2)}) %collective-permute-start.4) | collective-permute-done | bytes 229408 | tf_op jit(solution)/shard_map/ppermute | solution.py:462
  30.2 0.0 collective-permute-done.5
  30.2 0.0 collective-permute-done.6
  30.3 0.1 collective-permute-start.7
  30.4 2.5 %collective-permute-done.7.refs_1_ = bf16[128,3584]{1,0:T(8,128)(2,1)S(1)} collective-permute-done((bf16[128,3584]{1,0:T(8,128)(2,1)S(1)}, bf16[128,3584]{1,0:T(8,128)(2,1)S(1)}, u32[]{:S(2)}, u32[]{:S(2)}) %collective-permute-start.7) | collective-permute-done | bytes 917536 | tf_op jit(solution)/shard_map/ppermute | solution.py:456
  32.9 5.7 %activation_grads.1 = (bf16[128,3584]{1,0:T(8,128)(2,1)S(1)}, bf16[128,3584]{1,0:T(8,128)(2,1)S(1)}, bf16[1024,128]{1,0:T(8,128)(2,1)S(1)}, bf16[1024,128]{1,0:T...) custom-call(bf16[128,3584]{1,0:T(8,128)(2,1)S(1)} %constant_dynamic-update-sli, ...), custom_call_target="tpu_custom_call" | custom-call | flops 4697620480 | bytes 22020096 | tf_op jit(solution)/shard_map/activation_grads/pallas_call | solution.py:298
  38.6 0.2 collective-permute-start.8
  38.8 2.3 %down_grad.1.down_ref = bf16[1024,3584]{1,0:T(8,128)(2,1)S(1)} custom-call(bf16[128,3584]{1,0:T(8,128)(2,1)S(1)} %get-tuple-element.73.rows_ref, bf16[1024,128]{1,0:T(8,128)(2,1)S(1)} %get-tuple-element.74.left_ref), custom_call_target="tpu_custom_call" | custom-call | flops 939524096 | bytes 7340032 | tf_op jit(solution)/shard_map/down_grad/pallas_call | solution.py:328
  41.0 0.0 collective-permute-done.8
  41.0 0.1 add_convert_fusion
  41.2 3.5 %collective-permute-start.12 = (bf16[16,3584]{1,0:T(8,128)(2,1)S(1)}, bf16[16,3584]{1,0:T(8,128)(2,1)S(1)}, u32[]{:S(2)}, u32[]{:S(2)}) collective-permute-start(bf16[16,3584]{1,0:T(8,128)(2,1)S(1)} %get-tuple-element.92), channel_id=1, source_target_pairs={{0,14},{1,13},{2,12},{3,15},{4,10},{5,9},{6,8},{7,11},{8,6},{9,5},... | collective-permute-start | bytes 344072 | tf_op jit(solution)/shard_map/ppermute | solution.py:462
  44.6 0.0 collective-permute-start.11
  44.6 1.9 %collective-permute-start.10 = (bf16[16,3584]{1,0:T(8,128)(2,1)S(1)}, bf16[16,3584]{1,0:T(8,128)(2,1)S(1)}, u32[]{:S(2)}, u32[]{:S(2)}) collective-permute-start(bf16[16,3584]{1,0:T(8,128)(2,1)S(1)} %get-tuple-element.94), channel_id=1, source_target_pairs={{0,4},{1,7},{2,6},{3,5},{4,0},{5,3},{6,2},{7,1},{8,12},{9,15},{10,... | collective-permute-start | bytes 344072 | tf_op jit(solution)/shard_map/ppermute | solution.py:462
  46.5 2.4 %collective-permute-start.9 = (bf16[16,3584]{1,0:T(8,128)(2,1)S(1)}, bf16[16,3584]{1,0:T(8,128)(2,1)S(1)}, u32[]{:S(2)}, u32[]{:S(2)}) collective-permute-start(bf16[16,3584]{1,0:T(8,128)(2,1)S(1)} %get-tuple-element.95), channel_id=1, source_target_pairs={{0,2},{1,1},{2,0},{3,3},{4,6},{5,5},{6,4},{7,7},{8,10},{9,9},{10,8... | collective-permute-start | bytes 344072 | tf_op jit(solution)/shard_map/ppermute | solution.py:462
  49.0 5.4 %gate_up_grads.1 = (bf16[1024,3584]{1,0:T(8,128)(2,1)}, bf16[1024,3584]{1,0:T(8,128)(2,1)}, bf16[1024,3584]{1,0:T(8,128)(2,1)S(1)}) custom-call(bf16[128,3584]{1,0:T(8,128)(2,1)S(1)} %get-tuple-element.76.rows_ref, bf16[1024,128]{1,0:T(8,128)(2,1)S(1)} %get-tuple-element.77.gate_ref, bf16[1024,128]{1,0:T(8,128)(2,1)S(1)} %get-tuple-element.78.up_ref, ...), custom_call_target="tpu_custom_call" | custom-call | flops 1879048192 | bytes 14680064 | tf_op jit(solution)/shard_map/gate_up_grads/pallas_call | solution.py:367
  54.3 0.0 collective-permute-done.12
  54.3 0.0 collective-permute-done.11
  54.4 0.0 collective-permute-done.10
  54.4 0.0 collective-permute-done.9
  54.5 0.1 collective-permute-start.13
  54.6 1.8 %write_first.1._ = bf16[1024,3584]{1,0:T(8,128)(2,1)} custom-call(bf16[1024,3584]{1,0:T(8,128)(2,1)S(1)} %get-tuple-element.85.block_ref), custom_call_target="tpu_custom_call" | custom-call | bytes 7340032 | tf_op jit(solution)/shard_map/write_first/pallas_call | solution.py:392
  56.4 0.0 collective-permute-done.13
  56.4 2.2 %combine.1 = (bf16[128,3584]{1,0:T(8,128)(2,1)}, bf16[1024,3584]{1,0:T(8,128)(2,1)}) custom-call(bf16[64,128]{1,0:T(8,128)(2,1)S(1)} %get-tuple-element.48.pick_ref, bf16[64,3584]{1,0:T(8,128)(2,1)S(1)} %constant_dynamic-update-slice_fusion.4.back_ref, bf16[1024,3584]{1,0:T(8,128)(2,1)S(1)} %get-tuple-element.85.block_ref, ...), custom_call_target="tpu_custom_call", output_to_operand_aliasing={{1}: (3, {})} | custom-call | flops 58720256 | bytes 4587520 | tf_op jit(solution)/shard_map/combine/pallas_call | solution.py:429
  (11 shorter events, 0.2 us)
Async XLA Ops:
  0.6 4.0 %collective-permute-start.1 = (bf16[128,3584]{1,0:T(8,128)(2,1)}, bf16[128,3584]{1,0:T(8,128)(2,1)S(1)}, u32[]{:S(2)}, u32[]{:S(2)}) collective-permute-start(bf16[128,3584]{1,0:T(8,128)(2,1)} %refs_0_.1), channel_id=1, source_target_pairs={{0,1},{1,0},{2,3},{3,2},{4,5},{5,4},{6,7},{7,6},{8,9},{9,8},{10,11... | collective-permute-start | bytes 2752520 | tf_op jit(solution)/shard_map/ppermute | solution.py:456
  1.1 3.6 %collective-permute-start.2 = (bf16[128,3584]{1,0:T(8,128)(2,1)}, bf16[128,3584]{1,0:T(8,128)(2,1)S(1)}, u32[]{:S(2)}, u32[]{:S(2)}) collective-permute-start(bf16[128,3584]{1,0:T(8,128)(2,1)} %refs_1_.1), channel_id=1, source_target_pairs={{0,1},{1,0},{2,3},{3,2},{4,5},{5,4},{6,7},{7,6},{8,9},{9,8},{10,11... | collective-permute-start | bytes 2752520 | tf_op jit(solution)/shard_map/ppermute | solution.py:456
  2.2 2.4 %collective-permute-start = (f32[32,128]{1,0:T(8,128)S(1)}, f32[32,128]{1,0:T(8,128)S(1)}, u32[]{:S(2)}, u32[]{:S(2)}) collective-permute-start(f32[32,128]{1,0:T(8,128)S(1)} %get-tuple-element.50), channel_id=1, source_target_pairs={{0,1},{1,0},{2,3},{3,2},{4,5},{5,4},{6,7},{7,6},{8,9},{9,8},{10,11... | collective-permute-start | bytes 49160 | tf_op jit(solution)/shard_map/ppermute | solution.py:456
  5.4 17.8 %collective-permute-start.3 = (bf16[32,3584]{1,0:T(8,128)(2,1)S(1)}, bf16[32,3584]{1,0:T(8,128)(2,1)S(1)}, u32[]{:S(2)}, u32[]{:S(2)}) collective-permute-start(bf16[32,3584]{1,0:T(8,128)(2,1)S(1)} %get-tuple-element.53), channel_id=1, source_target_pairs={{0,14},{1,13},{2,12},{3,15},{4,10},{5,9},{6,8},{7,11},{8,6},{9,5},... | collective-permute-start | bytes 688136 | tf_op jit(solution)/shard_map/ppermute | solution.py:462
  11.3 18.9 %collective-permute-start.4 = (bf16[32,3584]{1,0:T(8,128)(2,1)S(1)}, bf16[32,3584]{1,0:T(8,128)(2,1)S(1)}, u32[]{:S(2)}, u32[]{:S(2)}) collective-permute-start(bf16[32,3584]{1,0:T(8,128)(2,1)S(1)} %get-tuple-element.54), channel_id=1, source_target_pairs={{0,8},{1,11},{2,10},{3,9},{4,12},{5,15},{6,14},{7,13},{8,0},{9,3},... | collective-permute-start | bytes 688136 | tf_op jit(solution)/shard_map/ppermute | solution.py:462
  11.3 18.9 %collective-permute-start.5 = (bf16[32,3584]{1,0:T(8,128)(2,1)S(1)}, bf16[32,3584]{1,0:T(8,128)(2,1)S(1)}, u32[]{:S(2)}, u32[]{:S(2)}) collective-permute-start(bf16[32,3584]{1,0:T(8,128)(2,1)S(1)} %get-tuple-element.55), channel_id=1, source_target_pairs={{0,4},{1,7},{2,6},{3,5},{4,0},{5,3},{6,2},{7,1},{8,12},{9,15},{10,... | collective-permute-start | bytes 688136 | tf_op jit(solution)/shard_map/ppermute | solution.py:462
  12.1 18.1 %collective-permute-start.6 = (bf16[32,3584]{1,0:T(8,128)(2,1)S(1)}, bf16[32,3584]{1,0:T(8,128)(2,1)S(1)}, u32[]{:S(2)}, u32[]{:S(2)}) collective-permute-start(bf16[32,3584]{1,0:T(8,128)(2,1)S(1)} %get-tuple-element.56), channel_id=1, source_target_pairs={{0,2},{1,1},{2,0},{3,3},{4,6},{5,5},{6,4},{7,7},{8,10},{9,9},{10,8... | collective-permute-start | bytes 688136 | tf_op jit(solution)/shard_map/ppermute | solution.py:462
  30.3 2.5 %collective-permute-start.7 = (bf16[128,3584]{1,0:T(8,128)(2,1)S(1)}, bf16[128,3584]{1,0:T(8,128)(2,1)S(1)}, u32[]{:S(2)}, u32[]{:S(2)}) collective-permute-start(bf16[128,3584]{1,0:T(8,128)(2,1)S(1)} %constant_dynamic-update-slice_fusion.refs_0_), channel_id=1, source_target_pairs={{0,1},{1,0},{2,3},{3,2},{4,5},{5,4},{6,7},{7,6},{8,9},{9,8},{10,11... | collective-permute-start | bytes 2752520 | tf_op jit(solution)/shard_map/ppermute | solution.py:456
  38.6 2.5 %collective-permute-start.8 = (bf16[64,3584]{1,0:T(8,128)(2,1)S(1)}, bf16[64,3584]{1,0:T(8,128)(2,1)S(1)}, u32[]{:S(2)}, u32[]{:S(2)}) collective-permute-start(bf16[64,3584]{1,0:T(8,128)(2,1)S(1)} %get-tuple-element.72), channel_id=1, source_target_pairs={{0,1},{1,0},{2,3},{3,2},{4,5},{5,4},{6,7},{7,6},{8,9},{9,8},{10,11... | collective-permute-start | bytes 1376264 | tf_op jit(solution)/shard_map/ppermute | solution.py:456
  41.2 13.2 %collective-permute-start.12 = (bf16[16,3584]{1,0:T(8,128)(2,1)S(1)}, bf16[16,3584]{1,0:T(8,128)(2,1)S(1)}, u32[]{:S(2)}, u32[]{:S(2)}) collective-permute-start(bf16[16,3584]{1,0:T(8,128)(2,1)S(1)} %get-tuple-element.92), channel_id=1, source_target_pairs={{0,14},{1,13},{2,12},{3,15},{4,10},{5,9},{6,8},{7,11},{8,6},{9,5},... | collective-permute-start | bytes 344072 | tf_op jit(solution)/shard_map/ppermute | solution.py:462
  44.6 9.7 %collective-permute-start.11 = (bf16[16,3584]{1,0:T(8,128)(2,1)S(1)}, bf16[16,3584]{1,0:T(8,128)(2,1)S(1)}, u32[]{:S(2)}, u32[]{:S(2)}) collective-permute-start(bf16[16,3584]{1,0:T(8,128)(2,1)S(1)} %get-tuple-element.93), channel_id=1, source_target_pairs={{0,8},{1,11},{2,10},{3,9},{4,12},{5,15},{6,14},{7,13},{8,0},{9,3},... | collective-permute-start | bytes 344072 | tf_op jit(solution)/shard_map/ppermute | solution.py:462
  44.6 9.7 %collective-permute-start.10 = (bf16[16,3584]{1,0:T(8,128)(2,1)S(1)}, bf16[16,3584]{1,0:T(8,128)(2,1)S(1)}, u32[]{:S(2)}, u32[]{:S(2)}) collective-permute-start(bf16[16,3584]{1,0:T(8,128)(2,1)S(1)} %get-tuple-element.94), channel_id=1, source_target_pairs={{0,4},{1,7},{2,6},{3,5},{4,0},{5,3},{6,2},{7,1},{8,12},{9,15},{10,... | collective-permute-start | bytes 344072 | tf_op jit(solution)/shard_map/ppermute | solution.py:462
  46.5 7.8 %collective-permute-start.9 = (bf16[16,3584]{1,0:T(8,128)(2,1)S(1)}, bf16[16,3584]{1,0:T(8,128)(2,1)S(1)}, u32[]{:S(2)}, u32[]{:S(2)}) collective-permute-start(bf16[16,3584]{1,0:T(8,128)(2,1)S(1)} %get-tuple-element.95), channel_id=1, source_target_pairs={{0,2},{1,1},{2,0},{3,3},{4,6},{5,5},{6,4},{7,7},{8,10},{9,9},{10,8... | collective-permute-start | bytes 344072 | tf_op jit(solution)/shard_map/ppermute | solution.py:462
  54.5 1.9 %collective-permute-start.13 = (bf16[32,3584]{1,0:T(8,128)(2,1)S(1)}, bf16[32,3584]{1,0:T(8,128)(2,1)S(1)}, u32[]{:S(2)}, u32[]{:S(2)}) collective-permute-start(bf16[32,3584]{1,0:T(8,128)(2,1)S(1)} %pad_maximum_fusion), channel_id=1, source_target_pairs={{0,1},{1,0},{2,3},{3,2},{4,5},{5,4},{6,7},{7,6},{8,9},{9,8},{10,11... | collective-permute-start | bytes 688136 | tf_op jit(solution)/shard_map/ppermute | solution.py:456

commit v6 on v5

--- a/solution.py
+++ b/solution.py
@@ -313,109 +313,145 @@
     )(*blocks, gate_half, up_half, gate_cols, up_cols, down_cols)
 
 
-def weight_grad(rows, left, name):
+def column_chunks(width):
+    chunk = 512 if width % 512 == 0 else width
+    return [slice(c, c + chunk) for c in range(0, width, chunk)]
+
+
+def written_after(chunks):
+    return 2 * len(chunks) // 7, 5 * len(chunks) // 7
+
+
+def down_grads(rows, left):
     count, width = rows.shape
     half = left.shape[0]
-    chunk = 512 if width % 512 == 0 else width
-
-    def kernel(rows_ref, left_ref, out_ref):
-        for c in range(0, width, chunk):
-            cols = slice(c, c + chunk)
-            out_ref[:, cols] = jnp.dot(
+    chunks = column_chunks(width)
+    early = len(chunks) // 2
+
+    def kernel(rows_ref, left_ref, held, out, sem):
+        copies = []
+        for n, cols in enumerate(chunks):
+            held[:, cols] = jnp.dot(
                 left_ref[...], rows_ref[:, cols], preferred_element_type=F32
             ).astype(BF16)
-
-    return pl.pallas_call(
-        kernel,
-        out_shape=pltpu.VMEM((half, width), BF16),
+            if n < early:
+                copies.append(
+                    pltpu.make_async_copy(held.at[:, cols], out.at[:, cols], sem.at[n])
+                )
+                copies[-1].start()
+        for copy in copies:
+            copy.wait()
+
+    return pl.pallas_call(
+        kernel,
+        out_shape=[
+            pltpu.VMEM((half, width), BF16),
+            jax.ShapeDtypeStruct((half, width), BF16),
+        ],
         in_specs=[VMEM, VMEM],
-        out_specs=VMEM,
+        out_specs=[VMEM, HBM],
+        scratch_shapes=[pltpu.SemaphoreType.DMA((len(chunks),))],
         compiler_params=pltpu.CompilerParams(vmem_limit_bytes=8 * MIB),
         cost_estimate=pl.CostEstimate(
             flops=2 * count * half * width, bytes_accessed=2 * half * width, transcendentals=0
         ),
-        name=name,
+        name="down_grads",
     )(rows, left)
 
 
-def gate_up_grads(rows, gate_left, up_left, down):
+def gate_up_grads(rows, gate_left, up_left, down, down_written):
     count, width = rows.shape
     half = gate_left.shape[0]
-    chunk = 512 if width % 512 == 0 else width
-
-    def kernel(rows_ref, gate_ref, up_ref, down_ref, gate_out, down_out, up_out, held, sem):
-        copies = [pltpu.make_async_copy(down_ref, down_out, sem.at[0])]
-        copies[0].start()
-        for n, c in enumerate(range(0, width, chunk)):
-            cols = slice(c, c + chunk)
+    chunks = column_chunks(width)
+    early = len(chunks) // 2
+    shares = written_after(chunks)
+
+    def kernel(rows_ref, gate_ref, up_ref, down_ref, _, *refs):
+        gate_out, down_out, up_held, up_out, held, sem = refs
+        copies = []
+        for n, cols in enumerate(chunks):
+            if n >= early:
+                copies.append(
+                    pltpu.make_async_copy(down_ref.at[:, cols], down_out.at[:, cols], sem.at[0, n])
+                )
+                copies[-1].start()
+        for n, cols in enumerate(chunks):
             held[:, cols] = jnp.dot(
                 gate_ref[...], rows_ref[:, cols], preferred_element_type=F32
             ).astype(BF16)
             copies.append(
-                pltpu.make_async_copy(held.at[:, cols], gate_out.at[:, cols], sem.at[1 + n])
+                pltpu.make_async_copy(held.at[:, cols], gate_out.at[:, cols], sem.at[1, n])
             )
             copies[-1].start()
-        for c in range(0, width, chunk):
-            cols = slice(c, c + chunk)
-            up_out[:, cols] = jnp.dot(
+        for n, cols in enumerate(chunks):
+            up_held[:, cols] = jnp.dot(
                 up_ref[...], rows_ref[:, cols], preferred_element_type=F32
             ).astype(BF16)
+            if n < shares[0]:
+                copies.append(
+                    pltpu.make_async_copy(up_held.at[:, cols], up_out.at[:, cols], sem.at[2, n])
+                )
+                copies[-1].start()
         for copy in copies:
             copy.wait()
 
     full = jax.ShapeDtypeStruct((half, width), BF16)
     return pl.pallas_call(
         kernel,
-        out_shape=[full, full, pltpu.VMEM((half, width), BF16)],
-        in_specs=[VMEM] * 4,
-        out_specs=[HBM, HBM, VMEM],
+        out_shape=[full, full, pltpu.VMEM((half, width), BF16), full],
+        in_specs=[VMEM] * 4 + [HBM],
+        out_specs=[HBM, HBM, VMEM, HBM],
         scratch_shapes=[
             pltpu.VMEM((half, width), BF16),
-            pltpu.SemaphoreType.DMA((1 + width // chunk,)),
+            pltpu.SemaphoreType.DMA((3, len(chunks))),
         ],
+        input_output_aliases={4: 1},
         compiler_params=pltpu.CompilerParams(vmem_limit_bytes=12 * MIB),
         cost_estimate=pl.CostEstimate(
             flops=4 * count * half * width, bytes_accessed=4 * half * width, transcendentals=0
         ),
         name="gate_up_grads",
-    )(rows, gate_left, up_left, down)
-
-
-def write_first(block):
-    rows = block.shape[0] // 2
-
-    def kernel(block_ref, out, sem):
-        copy = pltpu.make_async_copy(block_ref.at[pl.ds(0, rows)], out.at[pl.ds(0, rows)], sem)
+    )(rows, gate_left, up_left, down, down_written)
+
+
+def write_more(block, written):
+    chunks = column_chunks(block.shape[1])
+    start, stop = written_after(chunks)
+    first = chunks[start].start
+    cols = pl.ds(first, chunks[stop].start - first)
+
+    def kernel(block_ref, _, out, sem):
+        copy = pltpu.make_async_copy(block_ref.at[:, cols], out.at[:, cols], sem)
         copy.start()
         copy.wait()
 
     return pl.pallas_call(
         kernel,
         out_shape=jax.ShapeDtypeStruct(block.shape, block.dtype),
-        in_specs=[VMEM],
+        in_specs=[VMEM, HBM],
         out_specs=HBM,
         scratch_shapes=[pltpu.SemaphoreType.DMA],
+        input_output_aliases={1: 0},
         compiler_params=pltpu.CompilerParams(vmem_limit_bytes=2 * MIB),
         cost_estimate=pl.CostEstimate(
             flops=0, bytes_accessed=2 * block.size, transcendentals=0
         ),
-        name="write_first",
-    )(block)
+        name="write_more",
+    )(block, written)
 
 
 def combine(picker, returned, block, written):
     slots, tok_count = picker.shape
     width = returned.shape[1]
-    rows = block.shape[0] // 2
-    chunk = 512 if width % 512 == 0 else width
+    chunks = column_chunks(width)
+    first = chunks[written_after(chunks)[1]].start
 
     def kernel(pick_ref, back_ref, block_ref, _, sum_out, block_out, held, sem):
-        rest = pl.ds(rows, rows)
-        copies = [pltpu.make_async_copy(block_ref.at[rest], block_out.at[rest], sem.at[0])]
+        rest = pl.ds(first, width - first)
+        copies = [pltpu.make_async_copy(block_ref.at[:, rest], block_out.at[:, rest], sem.at[0])]
         copies[0].start()
         chooser = pick_ref[...].T
-        for n, c in enumerate(range(0, width, chunk)):
-            cols = slice(c, c + chunk)
+        for n, cols in enumerate(chunks):
             held[:, cols] = jnp.dot(
                 chooser, back_ref[:, cols], preferred_element_type=F32
             ).astype(BF16)
@@ -436,7 +472,7 @@
         out_specs=[HBM, HBM],
         scratch_shapes=[
             pltpu.VMEM((tok_count, width), BF16),
-            pltpu.SemaphoreType.DMA((1 + width // chunk,)),
+            pltpu.SemaphoreType.DMA((1 + len(chunks),)),
         ],
         input_output_aliases={3: 1},
         compiler_params=pltpu.CompilerParams(vmem_limit_bytes=4 * MIB),
@@ -470,18 +506,18 @@
     own = jnp.concatenate(got, axis=0)
     blocks = [own, swap(own)]
     tok, scl, dh, du, act, mine, theirs = activation_grads(blocks, *halves)
-    down_block = weight_grad(scl, act, "down_grad")
-    added, down_block = lax.optimization_barrier((swap(theirs), down_block))
+    down = down_grads(scl, act)
+    added, down = lax.optimization_barrier((swap(theirs), down))
     pieces = (mine + added.astype(F32)).astype(BF16)
     back = [
         travel(pieces[2 * k * HOTCAP : 2 * (k + 1) * HOTCAP], hop) for k, hop in enumerate(HOPS)
     ]
-    grad_gate, grad_down, up_block = gate_up_grads(tok, dh, du, down_block)
+    grad_gate, grad_down, up_block, written = gate_up_grads(tok, dh, du, *down)
     back, up_block = lax.optimization_barrier((back[::-1], up_block))
     back = back[::-1]
     kept = jnp.concatenate([block[:HOTCAP] for block in back], axis=0)
     given = swap(jnp.concatenate([block[HOTCAP:] for block in back], axis=0))
-    given, written = lax.optimization_barrier((given, write_first(up_block)))
+    given, written = lax.optimization_barrier((given, write_more(up_block, written)))
     returned = jnp.concatenate([kept, given], axis=0)
     grad_tokens, grad_up = combine(picker, returned, up_block, written)
     return grad_tokens, grad_gate, grad_up, grad_down

time: 59.1 us -> 58.4 us (0.988)
  Pallas kernels: 29.1 us -> 28.2 us
  transfers between devices with their start and end apart: 14 -> 14, of which waited for: 4 -> 5; matrix products, arithmetic and copies ran while one was open for 0% -> 0% of each run, Pallas kernels for 35% -> 35%
where the time goes in v6:
time: 58.4 us; the launch traced here: 58.1 us
  Pallas kernels  28.2 us (48%)
  starting transfers between devices  18.3 us (31%)
  waiting for transfers between devices  10.3 us (18%)
  between operations  1.02 us (2%)
    ppermute x8, starting transfers between devices, travel(): return lax.ppermute(block, ('expert', 'dp'), moves)  16.9 us
    pallas_call x1, Pallas kernels, load_weights(): pl.pallas_call(kernel, out_shape=[pltpu.VMEM((half, width), BF16)] * 2 +...  8.7 us
    ppermute x8, waiting for transfers between devices, travel(): return lax.ppermute(block, ('expert', 'dp'), moves)  7.25 us
    pallas_call x1, Pallas kernels, activation_grads(): pl.pallas_call(kernel, out_shape=[pltpu.VMEM((2 * rows, width), BF16)] *...  5.69 us
    pallas_call x1, Pallas kernels, gate_up_grads(): pl.pallas_call(kernel, out_shape=[full, full, pltpu.VMEM((half, width), B...  5.08 us
    ppermute x6, waiting for transfers between devices, swap(): return lax.ppermute(block, 'dp', [(0, 1), (1, 0)])  3.07 us
    pallas_call x1, Pallas kernels, down_grads(): pl.pallas_call(kernel, out_shape=[pltpu.VMEM((half, width), BF16), jax.Sh...  2.35 us
    pallas_call x1, Pallas kernels, combine(): pl.pallas_call(kernel, out_shape=[jax.ShapeDtypeStruct((tok_count, width)...  1.69 us
  transfers between devices with their start and end apart: 14, of which 5 were waited for; matrix products, arithmetic and copies ran while one was open for 0% of the time, Pallas kernels for 35%

profile of v6, /device:TPU:0, one launch (start us, length us, event | category | flops | bytes accessed | tf_op | source)
XLA Modules:
  0.0 58.1 jit_solution(5798714001895683137)
XLA Ops:
  0.6 0.5 collective-permute-start.1
  1.1 0.1 collective-permute-start.2
  1.2 1.0 %route.1 = (bf16[64,128]{1,0:T(8,128)(2,1)S(1)}, f32[32,128]{1,0:T(8,128)S(1)}, f32[32,128]{1,0:T(8,128)S(1)}) custom-call(s32[2]{0:T(128)} %hot_ref.1, s32[8,128]{1,0:T(8,128)} %bitcast.3, f32[8,128]{1,0:T(8,128)} %bitcast.4, s32[1,128]{1,0:T(1,128)} %bitcast.5), custom_call_target="tpu_custom_call" | custom-call | tf_op jit(solution)/shard_map/route/pallas_call | solution.py:137
  2.2 0.5 collective-permute-start
  2.7 1.5 %load_rows.1 = (bf16[128,3584]{1,0:T(8,128)(2,1)S(1)}, bf16[128,3584]{1,0:T(8,128)(2,1)S(1)}) custom-call(bf16[128,3584]{1,0:T(8,128)(2,1)} %refs_0_.1, bf16[128,3584]{1,0:T(8,128)(2,1)} %refs_1_.1), custom_call_target="tpu_custom_call" | custom-call | bytes 3670016 | tf_op jit(solution)/shard_map/load_rows/pallas_call | solution.py:163
  4.2 0.4 collective-permute-done.theirs_ref
  4.6 0.0 collective-permute-done.1.their_tok
  4.6 0.2 collective-permute-done.2.their_grad
  4.8 0.6 %pick.1 = (bf16[32,3584]{1,0:T(8,128)(2,1)S(1)}, bf16[32,3584]{1,0:T(8,128)(2,1)S(1)}, bf16[32,3584]{1,0:T(8,128)(2,1)S(1)}, bf16[32,3584]{1,0:T(8,128)(2,1)S(1)}) custom-call(f32[32,128]{1,0:T(8,128)S(1)} %get-tuple-element.53.mine_ref, f32[32,128]{1,0:T(8,128)S(1)} %collective-permute-done.theirs_ref, bf16[128,3584]{1,0:T(8,128)(2,1)S(1)} %get-tuple-element.55.my_tok, ...), custom_call_target="tpu_custom_call" | custom-call | flops 117440512 | bytes 4587520 | tf_op jit(solution)/shard_map/pick/pallas_call | solution.py:195
  5.4 6.0 %collective-permute-start.3 = (bf16[32,3584]{1,0:T(8,128)(2,1)S(1)}, bf16[32,3584]{1,0:T(8,128)(2,1)S(1)}, u32[]{:S(2)}, u32[]{:S(2)}) collective-permute-start(bf16[32,3584]{1,0:T(8,128)(2,1)S(1)} %get-tuple-element.57), channel_id=1, source_target_pairs={{0,14},{1,13},{2,12},{3,15},{4,10},{5,9},{6,8},{7,11},{8,6},{9,5},... | collective-permute-start | bytes 688136 | tf_op jit(solution)/shard_map/ppermute | solution.py:498
  11.3 0.0 collective-permute-start.4
  11.3 0.8 %collective-permute-start.5 = (bf16[32,3584]{1,0:T(8,128)(2,1)S(1)}, bf16[32,3584]{1,0:T(8,128)(2,1)S(1)}, u32[]{:S(2)}, u32[]{:S(2)}) collective-permute-start(bf16[32,3584]{1,0:T(8,128)(2,1)S(1)} %get-tuple-element.59), channel_id=1, source_target_pairs={{0,4},{1,7},{2,6},{3,5},{4,0},{5,3},{6,2},{7,1},{8,12},{9,15},{10,... | collective-permute-start | bytes 688136 | tf_op jit(solution)/shard_map/ppermute | solution.py:498
  12.1 2.3 %collective-permute-start.6 = (bf16[32,3584]{1,0:T(8,128)(2,1)S(1)}, bf16[32,3584]{1,0:T(8,128)(2,1)S(1)}, u32[]{:S(2)}, u32[]{:S(2)}) collective-permute-start(bf16[32,3584]{1,0:T(8,128)(2,1)S(1)} %get-tuple-element.60), channel_id=1, source_target_pairs={{0,2},{1,1},{2,0},{3,3},{4,6},{5,5},{6,4},{7,7},{8,10},{9,9},{10,8... | collective-permute-start | bytes 688136 | tf_op jit(solution)/shard_map/ppermute | solution.py:498
  14.5 8.7 %load_weights.1 = (bf16[1024,3584]{1,0:T(8,128)(2,1)S(1)}, bf16[1024,3584]{1,0:T(8,128)(2,1)S(1)}, bf16[3584,1024]{1,0:T(8,128)(2,1)S(1)}, bf16[3584,1024]{1,0:T(8,128)(2,1)S(1)}, bf16[3584,1024]{1,0:T(8,128)(2,1)S(1)}) custom-call(bf16[2048,3584]{1,0:T(8,128)(2,1)} %g_in.1, bf16[2048,3584]{1,0:T(8,128)(2,1)} %u_in.1, bf16[2048,3584]{1,0:T(8,128)(2,1)} %w_in.1), custom_call_target="tpu_custom_call" | custom-call | bytes 44040192 | tf_op jit(solution)/shard_map/load_weights/pallas_call | solution.py:239
  23.2 0.0 collective-permute-done.3
  23.2 7.1 %collective-permute-done.4 = bf16[32,3584]{1,0:T(8,128)(2,1)S(1)} collective-permute-done((bf16[32,3584]{1,0:T(8,128)(2,1)S(1)}, bf16[32,3584]{1,0:T(8,128)(2,1)S(1)}, u32[]{:S(2)}, u32[]{:S(2)}) %collective-permute-start.4) | collective-permute-done | bytes 229408 | tf_op jit(solution)/shard_map/ppermute | solution.py:498
  30.2 0.0 collective-permute-done.5
  30.2 0.0 collective-permute-done.6
  30.3 0.1 collective-permute-start.7
  30.4 2.5 %collective-permute-done.7.refs_1_ = bf16[128,3584]{1,0:T(8,128)(2,1)S(1)} collective-permute-done((bf16[128,3584]{1,0:T(8,128)(2,1)S(1)}, bf16[128,3584]{1,0:T(8,128)(2,1)S(1)}, u32[]{:S(2)}, u32[]{:S(2)}) %collective-permute-start.7) | collective-permute-done | bytes 917536 | tf_op jit(solution)/shard_map/ppermute | solution.py:492
  32.9 5.7 %activation_grads.1 = (bf16[128,3584]{1,0:T(8,128)(2,1)S(1)}, bf16[128,3584]{1,0:T(8,128)(2,1)S(1)}, bf16[1024,128]{1,0:T(8,128)(2,1)S(1)}, bf16[1024,128]{1,0:T...) custom-call(bf16[128,3584]{1,0:T(8,128)(2,1)S(1)} %constant_dynamic-update-sli, ...), custom_call_target="tpu_custom_call" | custom-call | flops 4697620480 | bytes 22020096 | tf_op jit(solution)/shard_map/activation_grads/pallas_call | solution.py:298
  38.6 0.2 collective-permute-start.8
  38.8 2.3 %down_grads.1 = (bf16[1024,3584]{1,0:T(8,128)(2,1)S(1)}, bf16[1024,3584]{1,0:T(8,128)(2,1)}) custom-call(bf16[128,3584]{1,0:T(8,128)(2,1)S(1)} %get-tuple-element.77.rows_ref, bf16[1024,128]{1,0:T(8,128)(2,1)S(1)} %get-tuple-element.78.left_ref), custom_call_target="tpu_custom_call" | custom-call | flops 939524096 | bytes 7340032 | tf_op jit(solution)/shard_map/down_grads/pallas_call | solution.py:345
  41.1 0.0 collective-permute-done.8
  41.1 0.1 add_convert_fusion
  41.2 3.5 %collective-permute-start.12 = (bf16[16,3584]{1,0:T(8,128)(2,1)S(1)}, bf16[16,3584]{1,0:T(8,128)(2,1)S(1)}, u32[]{:S(2)}, u32[]{:S(2)}) collective-permute-start(bf16[16,3584]{1,0:T(8,128)(2,1)S(1)} %get-tuple-element.100), channel_id=1, source_target_pairs={{0,14},{1,13},{2,12},{3,15},{4,10},{5,9},{6,8},{7,11},{8,6},{9,5},... | collective-permute-start | bytes 344072 | tf_op jit(solution)/shard_map/ppermute | solution.py:498
  44.7 0.0 collective-permute-start.11
  44.7 1.9 %collective-permute-start.10 = (bf16[16,3584]{1,0:T(8,128)(2,1)S(1)}, bf16[16,3584]{1,0:T(8,128)(2,1)S(1)}, u32[]{:S(2)}, u32[]{:S(2)}) collective-permute-start(bf16[16,3584]{1,0:T(8,128)(2,1)S(1)} %get-tuple-element.102), channel_id=1, source_target_pairs={{0,4},{1,7},{2,6},{3,5},{4,0},{5,3},{6,2},{7,1},{8,12},{9,15},{10,... | collective-permute-start | bytes 344072 | tf_op jit(solution)/shard_map/ppermute | solution.py:498
  46.6 2.4 %collective-permute-start.9 = (bf16[16,3584]{1,0:T(8,128)(2,1)S(1)}, bf16[16,3584]{1,0:T(8,128)(2,1)S(1)}, u32[]{:S(2)}, u32[]{:S(2)}) collective-permute-start(bf16[16,3584]{1,0:T(8,128)(2,1)S(1)} %get-tuple-element.103), channel_id=1, source_target_pairs={{0,2},{1,1},{2,0},{3,3},{4,6},{5,5},{6,4},{7,7},{8,10},{9,9},{10,8... | collective-permute-start | bytes 344072 | tf_op jit(solution)/shard_map/ppermute | solution.py:498
  49.1 5.1 %gate_up_grads.1 = (bf16[1024,3584]{1,0:T(8,128)(2,1)}, bf16[1024,3584]{1,0:T(8,128)(2,1)}, bf16[1024,3584]{1,0:T(8,128)(2,1)S(1)}, bf16[1024,3584]{1,0:T(8,128)(2,1)}) custom-call(bf16[128,3584]{1,0:T(8,128)(2,1)S(1)} %get-tuple-element.82.rows_ref, bf16[1024,128]{1,0:T(8,128)(2,1)S(1)} %get-tuple-element.83.gate_ref, ...), custom_call_target="tpu_custom_call", output_to_operand_aliasing={{1}: (4, {})} | custom-call | flops 1879048192 | bytes 14680064 | tf_op jit(solution)/shard_map/gate_up_grads/pallas_call | solution.py:399
  54.2 0.0 collective-permute-done.12
  54.2 0.0 collective-permute-done.11
  54.2 0.0 collective-permute-done.10
  54.2 0.2 collective-permute-done.9
  54.5 0.1 collective-permute-start.13
  54.5 1.7 %write_more.1._ = bf16[1024,3584]{1,0:T(8,128)(2,1)} custom-call(bf16[1024,3584]{1,0:T(8,128)(2,1)S(1)} %get-tuple-element.92.block_ref, bf16[1024,3584]{1,0:T(8,128)(2,1)} %get-tuple-element.93._), custom_call_target="tpu_custom_call", output_to_operand_aliasing={{}: (1, {})} | custom-call | bytes 7340032 | tf_op jit(solution)/shard_map/write_more/pallas_call | solution.py:428
  56.2 0.0 collective-permute-done.13
  56.3 1.7 %combine.1 = (bf16[128,3584]{1,0:T(8,128)(2,1)}, bf16[1024,3584]{1,0:T(8,128)(2,1)}) custom-call(bf16[64,128]{1,0:T(8,128)(2,1)S(1)} %get-tuple-element.52.pick_ref, bf16[64,3584]{1,0:T(8,128)(2,1)S(1)} %constant_dynamic-update-slice_fusion.4.back_ref, bf16[1024,3584]{1,0:T(8,128)(2,1)S(1)} %get-tuple-element.92.block_ref, ...), custom_call_target="tpu_custom_call", output_to_operand_aliasing={{1}: (3, {})} | custom-call | flops 58720256 | bytes 4587520 | tf_op jit(solution)/shard_map/combine/pallas_call | solution.py:465
  (11 shorter events, 0.2 us)
Async XLA Ops:
  0.6 4.0 %collective-permute-start.1 = (bf16[128,3584]{1,0:T(8,128)(2,1)}, bf16[128,3584]{1,0:T(8,128)(2,1)S(1)}, u32[]{:S(2)}, u32[]{:S(2)}) collective-permute-start(bf16[128,3584]{1,0:T(8,128)(2,1)} %refs_0_.1), channel_id=1, source_target_pairs={{0,1},{1,0},{2,3},{3,2},{4,5},{5,4},{6,7},{7,6},{8,9},{9,8},{10,11... | collective-permute-start | bytes 2752520 | tf_op jit(solution)/shard_map/ppermute | solution.py:492
  1.1 3.6 %collective-permute-start.2 = (bf16[128,3584]{1,0:T(8,128)(2,1)}, bf16[128,3584]{1,0:T(8,128)(2,1)S(1)}, u32[]{:S(2)}, u32[]{:S(2)}) collective-permute-start(bf16[128,3584]{1,0:T(8,128)(2,1)} %refs_1_.1), channel_id=1, source_target_pairs={{0,1},{1,0},{2,3},{3,2},{4,5},{5,4},{6,7},{7,6},{8,9},{9,8},{10,11... | collective-permute-start | bytes 2752520 | tf_op jit(solution)/shard_map/ppermute | solution.py:492
  2.2 2.4 %collective-permute-start = (f32[32,128]{1,0:T(8,128)S(1)}, f32[32,128]{1,0:T(8,128)S(1)}, u32[]{:S(2)}, u32[]{:S(2)}) collective-permute-start(f32[32,128]{1,0:T(8,128)S(1)} %get-tuple-element.54), channel_id=1, source_target_pairs={{0,1},{1,0},{2,3},{3,2},{4,5},{5,4},{6,7},{7,6},{8,9},{9,8},{10,11... | collective-permute-start | bytes 49160 | tf_op jit(solution)/shard_map/ppermute | solution.py:492
  5.4 17.8 %collective-permute-start.3 = (bf16[32,3584]{1,0:T(8,128)(2,1)S(1)}, bf16[32,3584]{1,0:T(8,128)(2,1)S(1)}, u32[]{:S(2)}, u32[]{:S(2)}) collective-permute-start(bf16[32,3584]{1,0:T(8,128)(2,1)S(1)} %get-tuple-element.57), channel_id=1, source_target_pairs={{0,14},{1,13},{2,12},{3,15},{4,10},{5,9},{6,8},{7,11},{8,6},{9,5},... | collective-permute-start | bytes 688136 | tf_op jit(solution)/shard_map/ppermute | solution.py:498
  11.3 18.9 %collective-permute-start.4 = (bf16[32,3584]{1,0:T(8,128)(2,1)S(1)}, bf16[32,3584]{1,0:T(8,128)(2,1)S(1)}, u32[]{:S(2)}, u32[]{:S(2)}) collective-permute-start(bf16[32,3584]{1,0:T(8,128)(2,1)S(1)} %get-tuple-element.58), channel_id=1, source_target_pairs={{0,8},{1,11},{2,10},{3,9},{4,12},{5,15},{6,14},{7,13},{8,0},{9,3},... | collective-permute-start | bytes 688136 | tf_op jit(solution)/shard_map/ppermute | solution.py:498
  11.3 18.9 %collective-permute-start.5 = (bf16[32,3584]{1,0:T(8,128)(2,1)S(1)}, bf16[32,3584]{1,0:T(8,128)(2,1)S(1)}, u32[]{:S(2)}, u32[]{:S(2)}) collective-permute-start(bf16[32,3584]{1,0:T(8,128)(2,1)S(1)} %get-tuple-element.59), channel_id=1, source_target_pairs={{0,4},{1,7},{2,6},{3,5},{4,0},{5,3},{6,2},{7,1},{8,12},{9,15},{10,... | collective-permute-start | bytes 688136 | tf_op jit(solution)/shard_map/ppermute | solution.py:498
  12.1 18.1 %collective-permute-start.6 = (bf16[32,3584]{1,0:T(8,128)(2,1)S(1)}, bf16[32,3584]{1,0:T(8,128)(2,1)S(1)}, u32[]{:S(2)}, u32[]{:S(2)}) collective-permute-start(bf16[32,3584]{1,0:T(8,128)(2,1)S(1)} %get-tuple-element.60), channel_id=1, source_target_pairs={{0,2},{1,1},{2,0},{3,3},{4,6},{5,5},{6,4},{7,7},{8,10},{9,9},{10,8... | collective-permute-start | bytes 688136 | tf_op jit(solution)/shard_map/ppermute | solution.py:498
  30.3 2.5 %collective-permute-start.7 = (bf16[128,3584]{1,0:T(8,128)(2,1)S(1)}, bf16[128,3584]{1,0:T(8,128)(2,1)S(1)}, u32[]{:S(2)}, u32[]{:S(2)}) collective-permute-start(bf16[128,3584]{1,0:T(8,128)(2,1)S(1)} %constant_dynamic-update-slice_fusion.refs_0_), channel_id=1, source_target_pairs={{0,1},{1,0},{2,3},{3,2},{4,5},{5,4},{6,7},{7,6},{8,9},{9,8},{10,11... | collective-permute-start | bytes 2752520 | tf_op jit(solution)/shard_map/ppermute | solution.py:492
  38.6 2.6 %collective-permute-start.8 = (bf16[64,3584]{1,0:T(8,128)(2,1)S(1)}, bf16[64,3584]{1,0:T(8,128)(2,1)S(1)}, u32[]{:S(2)}, u32[]{:S(2)}) collective-permute-start(bf16[64,3584]{1,0:T(8,128)(2,1)S(1)} %get-tuple-element.76), channel_id=1, source_target_pairs={{0,1},{1,0},{2,3},{3,2},{4,5},{5,4},{6,7},{7,6},{8,9},{9,8},{10,11... | collective-permute-start | bytes 1376264 | tf_op jit(solution)/shard_map/ppermute | solution.py:492
  41.2 12.9 %collective-permute-start.12 = (bf16[16,3584]{1,0:T(8,128)(2,1)S(1)}, bf16[16,3584]{1,0:T(8,128)(2,1)S(1)}, u32[]{:S(2)}, u32[]{:S(2)}) collective-permute-start(bf16[16,3584]{1,0:T(8,128)(2,1)S(1)} %get-tuple-element.100), channel_id=1, source_target_pairs={{0,14},{1,13},{2,12},{3,15},{4,10},{5,9},{6,8},{7,11},{8,6},{9,5},... | collective-permute-start | bytes 344072 | tf_op jit(solution)/shard_map/ppermute | solution.py:498
  44.7 9.5 %collective-permute-start.11 = (bf16[16,3584]{1,0:T(8,128)(2,1)S(1)}, bf16[16,3584]{1,0:T(8,128)(2,1)S(1)}, u32[]{:S(2)}, u32[]{:S(2)}) collective-permute-start(bf16[16,3584]{1,0:T(8,128)(2,1)S(1)} %get-tuple-element.101), channel_id=1, source_target_pairs={{0,8},{1,11},{2,10},{3,9},{4,12},{5,15},{6,14},{7,13},{8,0},{9,3},... | collective-permute-start | bytes 344072 | tf_op jit(solution)/shard_map/ppermute | solution.py:498
  44.7 9.5 %collective-permute-start.10 = (bf16[16,3584]{1,0:T(8,128)(2,1)S(1)}, bf16[16,3584]{1,0:T(8,128)(2,1)S(1)}, u32[]{:S(2)}, u32[]{:S(2)}) collective-permute-start(bf16[16,3584]{1,0:T(8,128)(2,1)S(1)} %get-tuple-element.102), channel_id=1, source_target_pairs={{0,4},{1,7},{2,6},{3,5},{4,0},{5,3},{6,2},{7,1},{8,12},{9,15},{10,... | collective-permute-start | bytes 344072 | tf_op jit(solution)/shard_map/ppermute | solution.py:498
  46.6 7.7 %collective-permute-start.9 = (bf16[16,3584]{1,0:T(8,128)(2,1)S(1)}, bf16[16,3584]{1,0:T(8,128)(2,1)S(1)}, u32[]{:S(2)}, u32[]{:S(2)}) collective-permute-start(bf16[16,3584]{1,0:T(8,128)(2,1)S(1)} %get-tuple-element.103), channel_id=1, source_target_pairs={{0,2},{1,1},{2,0},{3,3},{4,6},{5,5},{6,4},{7,7},{8,10},{9,9},{10,8... | collective-permute-start | bytes 344072 | tf_op jit(solution)/shard_map/ppermute | solution.py:498
  54.5 1.8 %collective-permute-start.13 = (bf16[32,3584]{1,0:T(8,128)(2,1)S(1)}, bf16[32,3584]{1,0:T(8,128)(2,1)S(1)}, u32[]{:S(2)}, u32[]{:S(2)}) collective-permute-start(bf16[32,3584]{1,0:T(8,128)(2,1)S(1)} %pad_maximum_fusion), channel_id=1, source_target_pairs={{0,1},{1,0},{2,3},{3,2},{4,5},{5,4},{6,7},{7,6},{8,9},{9,8},{10,11... | collective-permute-start | bytes 688136 | tf_op jit(solution)/shard_map/ppermute | solution.py:492

commit v7 on v6

--- a/solution.py
+++ b/solution.py
@@ -260,7 +260,7 @@
     width = blocks[0].shape[1]
     rows = 2 * HOTCAP * len(HOPS)
     half = gate_half.shape[0]
-    tile = min(256, half)
+    tile = min(512, half)
     chunk = 512 if width % 512 == 0 else width
 
     def kernel(*refs):

time: 58.4 us -> 58.1 us (level)
  no operation moved by 1% of the time
where the time goes in v7:
time: 58.1 us; the launch traced here: 57.8 us
  Pallas kernels  27.9 us (48%)
  starting transfers between devices  18.3 us (31%)
  waiting for transfers between devices  10.3 us (18%)
  between operations  1.02 us (2%)
    ppermute x8, starting transfers between devices, travel(): return lax.ppermute(block, ('expert', 'dp'), moves)  16.9 us
    pallas_call x1, Pallas kernels, load_weights(): pl.pallas_call(kernel, out_shape=[pltpu.VMEM((half, width), BF16)] * 2 +...  8.7 us
    ppermute x8, waiting for transfers between devices, travel(): return lax.ppermute(block, ('expert', 'dp'), moves)  7.25 us
    pallas_call x1, Pallas kernels, activation_grads(): pl.pallas_call(kernel, out_shape=[pltpu.VMEM((2 * rows, width), BF16)] *...  5.38 us
    pallas_call x1, Pallas kernels, gate_up_grads(): pl.pallas_call(kernel, out_shape=[full, full, pltpu.VMEM((half, width), B...  5.08 us
    ppermute x6, waiting for transfers between devices, swap(): return lax.ppermute(block, 'dp', [(0, 1), (1, 0)])  3.07 us
    pallas_call x1, Pallas kernels, down_grads(): pl.pallas_call(kernel, out_shape=[pltpu.VMEM((half, width), BF16), jax.Sh...  2.32 us
    pallas_call x1, Pallas kernels, combine(): pl.pallas_call(kernel, out_shape=[jax.ShapeDtypeStruct((tok_count, width)...  1.69 us
  transfers between devices with their start and end apart: 14, of which 5 were waited for; matrix products, arithmetic and copies ran while one was open for 0% of the time, Pallas kernels for 35%

profile of v7, /device:TPU:0, one launch (start us, length us, event | category | flops | bytes accessed | tf_op | source)
XLA Modules:
  0.0 57.8 jit_solution(17723458234249320157)
XLA Ops:
  0.6 0.5 collective-permute-start.1
  1.1 0.1 collective-permute-start.2
  1.2 1.0 %route.1 = (bf16[64,128]{1,0:T(8,128)(2,1)S(1)}, f32[32,128]{1,0:T(8,128)S(1)}, f32[32,128]{1,0:T(8,128)S(1)}) custom-call(s32[2]{0:T(128)} %hot_ref.1, s32[8,128]{1,0:T(8,128)} %bitcast.3, f32[8,128]{1,0:T(8,128)} %bitcast.4, s32[1,128]{1,0:T(1,128)} %bitcast.5), custom_call_target="tpu_custom_call" | custom-call | tf_op jit(solution)/shard_map/route/pallas_call | solution.py:137
  2.2 0.5 collective-permute-start
  2.7 1.5 %load_rows.1 = (bf16[128,3584]{1,0:T(8,128)(2,1)S(1)}, bf16[128,3584]{1,0:T(8,128)(2,1)S(1)}) custom-call(bf16[128,3584]{1,0:T(8,128)(2,1)} %refs_0_.1, bf16[128,3584]{1,0:T(8,128)(2,1)} %refs_1_.1), custom_call_target="tpu_custom_call" | custom-call | bytes 3670016 | tf_op jit(solution)/shard_map/load_rows/pallas_call | solution.py:163
  4.2 0.4 collective-permute-done.theirs_ref
  4.6 0.0 collective-permute-done.1.their_tok
  4.6 0.2 collective-permute-done.2.their_grad
  4.8 0.6 %pick.1 = (bf16[32,3584]{1,0:T(8,128)(2,1)S(1)}, bf16[32,3584]{1,0:T(8,128)(2,1)S(1)}, bf16[32,3584]{1,0:T(8,128)(2,1)S(1)}, bf16[32,3584]{1,0:T(8,128)(2,1)S(1)}) custom-call(f32[32,128]{1,0:T(8,128)S(1)} %get-tuple-element.53.mine_ref, f32[32,128]{1,0:T(8,128)S(1)} %collective-permute-done.theirs_ref, bf16[128,3584]{1,0:T(8,128)(2,1)S(1)} %get-tuple-element.55.my_tok, ...), custom_call_target="tpu_custom_call" | custom-call | flops 117440512 | bytes 4587520 | tf_op jit(solution)/shard_map/pick/pallas_call | solution.py:195
  5.4 6.0 %collective-permute-start.3 = (bf16[32,3584]{1,0:T(8,128)(2,1)S(1)}, bf16[32,3584]{1,0:T(8,128)(2,1)S(1)}, u32[]{:S(2)}, u32[]{:S(2)}) collective-permute-start(bf16[32,3584]{1,0:T(8,128)(2,1)S(1)} %get-tuple-element.57), channel_id=1, source_target_pairs={{0,14},{1,13},{2,12},{3,15},{4,10},{5,9},{6,8},{7,11},{8,6},{9,5},... | collective-permute-start | bytes 688136 | tf_op jit(solution)/shard_map/ppermute | solution.py:498
  11.3 0.0 collective-permute-start.4
  11.3 0.8 %collective-permute-start.5 = (bf16[32,3584]{1,0:T(8,128)(2,1)S(1)}, bf16[32,3584]{1,0:T(8,128)(2,1)S(1)}, u32[]{:S(2)}, u32[]{:S(2)}) collective-permute-start(bf16[32,3584]{1,0:T(8,128)(2,1)S(1)} %get-tuple-element.59), channel_id=1, source_target_pairs={{0,4},{1,7},{2,6},{3,5},{4,0},{5,3},{6,2},{7,1},{8,12},{9,15},{10,... | collective-permute-start | bytes 688136 | tf_op jit(solution)/shard_map/ppermute | solution.py:498
  12.1 2.3 %collective-permute-start.6 = (bf16[32,3584]{1,0:T(8,128)(2,1)S(1)}, bf16[32,3584]{1,0:T(8,128)(2,1)S(1)}, u32[]{:S(2)}, u32[]{:S(2)}) collective-permute-start(bf16[32,3584]{1,0:T(8,128)(2,1)S(1)} %get-tuple-element.60), channel_id=1, source_target_pairs={{0,2},{1,1},{2,0},{3,3},{4,6},{5,5},{6,4},{7,7},{8,10},{9,9},{10,8... | collective-permute-start | bytes 688136 | tf_op jit(solution)/shard_map/ppermute | solution.py:498
  14.5 8.7 %load_weights.1 = (bf16[1024,3584]{1,0:T(8,128)(2,1)S(1)}, bf16[1024,3584]{1,0:T(8,128)(2,1)S(1)}, bf16[3584,1024]{1,0:T(8,128)(2,1)S(1)}, bf16[3584,1024]{1,0:T(8,128)(2,1)S(1)}, bf16[3584,1024]{1,0:T(8,128)(2,1)S(1)}) custom-call(bf16[2048,3584]{1,0:T(8,128)(2,1)} %g_in.1, bf16[2048,3584]{1,0:T(8,128)(2,1)} %u_in.1, bf16[2048,3584]{1,0:T(8,128)(2,1)} %w_in.1), custom_call_target="tpu_custom_call" | custom-call | bytes 44040192 | tf_op jit(solution)/shard_map/load_weights/pallas_call | solution.py:239
  23.2 0.0 collective-permute-done.3
  23.2 7.1 %collective-permute-done.4 = bf16[32,3584]{1,0:T(8,128)(2,1)S(1)} collective-permute-done((bf16[32,3584]{1,0:T(8,128)(2,1)S(1)}, bf16[32,3584]{1,0:T(8,128)(2,1)S(1)}, u32[]{:S(2)}, u32[]{:S(2)}) %collective-permute-start.4) | collective-permute-done | bytes 229408 | tf_op jit(solution)/shard_map/ppermute | solution.py:498
  30.2 0.0 collective-permute-done.5
  30.2 0.0 collective-permute-done.6
  30.3 0.1 collective-permute-start.7
  30.4 2.5 %collective-permute-done.7.refs_1_ = bf16[128,3584]{1,0:T(8,128)(2,1)S(1)} collective-permute-done((bf16[128,3584]{1,0:T(8,128)(2,1)S(1)}, bf16[128,3584]{1,0:T(8,128)(2,1)S(1)}, u32[]{:S(2)}, u32[]{:S(2)}) %collective-permute-start.7) | collective-permute-done | bytes 917536 | tf_op jit(solution)/shard_map/ppermute | solution.py:492
  32.9 5.4 %activation_grads.1 = (bf16[128,3584]{1,0:T(8,128)(2,1)S(1)}, bf16[128,3584]{1,0:T(8,128)(2,1)S(1)}, bf16[1024,128]{1,0:T(8,128)(2,1)S(1)}, bf16[1024,128]{1,0:T...) custom-call(bf16[128,3584]{1,0:T(8,128)(2,1)S(1)} %constant_dynamic-update-sli, ...), custom_call_target="tpu_custom_call" | custom-call | flops 4697620480 | bytes 22020096 | tf_op jit(solution)/shard_map/activation_grads/pallas_call | solution.py:298
  38.3 0.2 collective-permute-start.8
  38.5 2.3 %down_grads.1 = (bf16[1024,3584]{1,0:T(8,128)(2,1)S(1)}, bf16[1024,3584]{1,0:T(8,128)(2,1)}) custom-call(bf16[128,3584]{1,0:T(8,128)(2,1)S(1)} %get-tuple-element.77.rows_ref, bf16[1024,128]{1,0:T(8,128)(2,1)S(1)} %get-tuple-element.78.left_ref), custom_call_target="tpu_custom_call" | custom-call | flops 939524096 | bytes 7340032 | tf_op jit(solution)/shard_map/down_grads/pallas_call | solution.py:345
  40.8 0.0 collective-permute-done.8
  40.8 0.1 add_convert_fusion
  40.9 3.5 %collective-permute-start.12 = (bf16[16,3584]{1,0:T(8,128)(2,1)S(1)}, bf16[16,3584]{1,0:T(8,128)(2,1)S(1)}, u32[]{:S(2)}, u32[]{:S(2)}) collective-permute-start(bf16[16,3584]{1,0:T(8,128)(2,1)S(1)} %get-tuple-element.100), channel_id=1, source_target_pairs={{0,14},{1,13},{2,12},{3,15},{4,10},{5,9},{6,8},{7,11},{8,6},{9,5},... | collective-permute-start | bytes 344072 | tf_op jit(solution)/shard_map/ppermute | solution.py:498
  44.4 0.0 collective-permute-start.11
  44.4 1.9 %collective-permute-start.10 = (bf16[16,3584]{1,0:T(8,128)(2,1)S(1)}, bf16[16,3584]{1,0:T(8,128)(2,1)S(1)}, u32[]{:S(2)}, u32[]{:S(2)}) collective-permute-start(bf16[16,3584]{1,0:T(8,128)(2,1)S(1)} %get-tuple-element.102), channel_id=1, source_target_pairs={{0,4},{1,7},{2,6},{3,5},{4,0},{5,3},{6,2},{7,1},{8,12},{9,15},{10,... | collective-permute-start | bytes 344072 | tf_op jit(solution)/shard_map/ppermute | solution.py:498
  46.3 2.4 %collective-permute-start.9 = (bf16[16,3584]{1,0:T(8,128)(2,1)S(1)}, bf16[16,3584]{1,0:T(8,128)(2,1)S(1)}, u32[]{:S(2)}, u32[]{:S(2)}) collective-permute-start(bf16[16,3584]{1,0:T(8,128)(2,1)S(1)} %get-tuple-element.103), channel_id=1, source_target_pairs={{0,2},{1,1},{2,0},{3,3},{4,6},{5,5},{6,4},{7,7},{8,10},{9,9},{10,8... | collective-permute-start | bytes 344072 | tf_op jit(solution)/shard_map/ppermute | solution.py:498
  48.7 5.1 %gate_up_grads.1 = (bf16[1024,3584]{1,0:T(8,128)(2,1)}, bf16[1024,3584]{1,0:T(8,128)(2,1)}, bf16[1024,3584]{1,0:T(8,128)(2,1)S(1)}, bf16[1024,3584]{1,0:T(8,128)(2,1)}) custom-call(bf16[128,3584]{1,0:T(8,128)(2,1)S(1)} %get-tuple-element.82.rows_ref, bf16[1024,128]{1,0:T(8,128)(2,1)S(1)} %get-tuple-element.83.gate_ref, ...), custom_call_target="tpu_custom_call", output_to_operand_aliasing={{1}: (4, {})} | custom-call | flops 1879048192 | bytes 14680064 | tf_op jit(solution)/shard_map/gate_up_grads/pallas_call | solution.py:399
  53.8 0.0 collective-permute-done.12
  53.8 0.0 collective-permute-done.11
  53.8 0.0 collective-permute-done.10
  53.9 0.2 collective-permute-done.9
  54.1 0.1 collective-permute-start.13
  54.2 1.7 %write_more.1._ = bf16[1024,3584]{1,0:T(8,128)(2,1)} custom-call(bf16[1024,3584]{1,0:T(8,128)(2,1)S(1)} %get-tuple-element.92.block_ref, bf16[1024,3584]{1,0:T(8,128)(2,1)} %get-tuple-element.93._), custom_call_target="tpu_custom_call", output_to_operand_aliasing={{}: (1, {})} | custom-call | bytes 7340032 | tf_op jit(solution)/shard_map/write_more/pallas_call | solution.py:428
  55.9 0.0 collective-permute-done.13
  55.9 1.7 %combine.1 = (bf16[128,3584]{1,0:T(8,128)(2,1)}, bf16[1024,3584]{1,0:T(8,128)(2,1)}) custom-call(bf16[64,128]{1,0:T(8,128)(2,1)S(1)} %get-tuple-element.52.pick_ref, bf16[64,3584]{1,0:T(8,128)(2,1)S(1)} %constant_dynamic-update-slice_fusion.4.back_ref, bf16[1024,3584]{1,0:T(8,128)(2,1)S(1)} %get-tuple-element.92.block_ref, ...), custom_call_target="tpu_custom_call", output_to_operand_aliasing={{1}: (3, {})} | custom-call | flops 58720256 | bytes 4587520 | tf_op jit(solution)/shard_map/combine/pallas_call | solution.py:465
  (11 shorter events, 0.2 us)
Async XLA Ops:
  0.6 4.0 %collective-permute-start.1 = (bf16[128,3584]{1,0:T(8,128)(2,1)}, bf16[128,3584]{1,0:T(8,128)(2,1)S(1)}, u32[]{:S(2)}, u32[]{:S(2)}) collective-permute-start(bf16[128,3584]{1,0:T(8,128)(2,1)} %refs_0_.1), channel_id=1, source_target_pairs={{0,1},{1,0},{2,3},{3,2},{4,5},{5,4},{6,7},{7,6},{8,9},{9,8},{10,11... | collective-permute-start | bytes 2752520 | tf_op jit(solution)/shard_map/ppermute | solution.py:492
  1.1 3.6 %collective-permute-start.2 = (bf16[128,3584]{1,0:T(8,128)(2,1)}, bf16[128,3584]{1,0:T(8,128)(2,1)S(1)}, u32[]{:S(2)}, u32[]{:S(2)}) collective-permute-start(bf16[128,3584]{1,0:T(8,128)(2,1)} %refs_1_.1), channel_id=1, source_target_pairs={{0,1},{1,0},{2,3},{3,2},{4,5},{5,4},{6,7},{7,6},{8,9},{9,8},{10,11... | collective-permute-start | bytes 2752520 | tf_op jit(solution)/shard_map/ppermute | solution.py:492
  2.2 2.4 %collective-permute-start = (f32[32,128]{1,0:T(8,128)S(1)}, f32[32,128]{1,0:T(8,128)S(1)}, u32[]{:S(2)}, u32[]{:S(2)}) collective-permute-start(f32[32,128]{1,0:T(8,128)S(1)} %get-tuple-element.54), channel_id=1, source_target_pairs={{0,1},{1,0},{2,3},{3,2},{4,5},{5,4},{6,7},{7,6},{8,9},{9,8},{10,11... | collective-permute-start | bytes 49160 | tf_op jit(solution)/shard_map/ppermute | solution.py:492
  5.4 17.8 %collective-permute-start.3 = (bf16[32,3584]{1,0:T(8,128)(2,1)S(1)}, bf16[32,3584]{1,0:T(8,128)(2,1)S(1)}, u32[]{:S(2)}, u32[]{:S(2)}) collective-permute-start(bf16[32,3584]{1,0:T(8,128)(2,1)S(1)} %get-tuple-element.57), channel_id=1, source_target_pairs={{0,14},{1,13},{2,12},{3,15},{4,10},{5,9},{6,8},{7,11},{8,6},{9,5},... | collective-permute-start | bytes 688136 | tf_op jit(solution)/shard_map/ppermute | solution.py:498
  11.3 18.9 %collective-permute-start.4 = (bf16[32,3584]{1,0:T(8,128)(2,1)S(1)}, bf16[32,3584]{1,0:T(8,128)(2,1)S(1)}, u32[]{:S(2)}, u32[]{:S(2)}) collective-permute-start(bf16[32,3584]{1,0:T(8,128)(2,1)S(1)} %get-tuple-element.58), channel_id=1, source_target_pairs={{0,8},{1,11},{2,10},{3,9},{4,12},{5,15},{6,14},{7,13},{8,0},{9,3},... | collective-permute-start | bytes 688136 | tf_op jit(solution)/shard_map/ppermute | solution.py:498
  11.3 18.9 %collective-permute-start.5 = (bf16[32,3584]{1,0:T(8,128)(2,1)S(1)}, bf16[32,3584]{1,0:T(8,128)(2,1)S(1)}, u32[]{:S(2)}, u32[]{:S(2)}) collective-permute-start(bf16[32,3584]{1,0:T(8,128)(2,1)S(1)} %get-tuple-element.59), channel_id=1, source_target_pairs={{0,4},{1,7},{2,6},{3,5},{4,0},{5,3},{6,2},{7,1},{8,12},{9,15},{10,... | collective-permute-start | bytes 688136 | tf_op jit(solution)/shard_map/ppermute | solution.py:498
  12.1 18.1 %collective-permute-start.6 = (bf16[32,3584]{1,0:T(8,128)(2,1)S(1)}, bf16[32,3584]{1,0:T(8,128)(2,1)S(1)}, u32[]{:S(2)}, u32[]{:S(2)}) collective-permute-start(bf16[32,3584]{1,0:T(8,128)(2,1)S(1)} %get-tuple-element.60), channel_id=1, source_target_pairs={{0,2},{1,1},{2,0},{3,3},{4,6},{5,5},{6,4},{7,7},{8,10},{9,9},{10,8... | collective-permute-start | bytes 688136 | tf_op jit(solution)/shard_map/ppermute | solution.py:498
  30.3 2.5 %collective-permute-start.7 = (bf16[128,3584]{1,0:T(8,128)(2,1)S(1)}, bf16[128,3584]{1,0:T(8,128)(2,1)S(1)}, u32[]{:S(2)}, u32[]{:S(2)}) collective-permute-start(bf16[128,3584]{1,0:T(8,128)(2,1)S(1)} %constant_dynamic-update-slice_fusion.refs_0_), channel_id=1, source_target_pairs={{0,1},{1,0},{2,3},{3,2},{4,5},{5,4},{6,7},{7,6},{8,9},{9,8},{10,11... | collective-permute-start | bytes 2752520 | tf_op jit(solution)/shard_map/ppermute | solution.py:492
  38.3 2.5 %collective-permute-start.8 = (bf16[64,3584]{1,0:T(8,128)(2,1)S(1)}, bf16[64,3584]{1,0:T(8,128)(2,1)S(1)}, u32[]{:S(2)}, u32[]{:S(2)}) collective-permute-start(bf16[64,3584]{1,0:T(8,128)(2,1)S(1)} %get-tuple-element.76), channel_id=1, source_target_pairs={{0,1},{1,0},{2,3},{3,2},{4,5},{5,4},{6,7},{7,6},{8,9},{9,8},{10,11... | collective-permute-start | bytes 1376264 | tf_op jit(solution)/shard_map/ppermute | solution.py:492
  40.9 12.9 %collective-permute-start.12 = (bf16[16,3584]{1,0:T(8,128)(2,1)S(1)}, bf16[16,3584]{1,0:T(8,128)(2,1)S(1)}, u32[]{:S(2)}, u32[]{:S(2)}) collective-permute-start(bf16[16,3584]{1,0:T(8,128)(2,1)S(1)} %get-tuple-element.100), channel_id=1, source_target_pairs={{0,14},{1,13},{2,12},{3,15},{4,10},{5,9},{6,8},{7,11},{8,6},{9,5},... | collective-permute-start | bytes 344072 | tf_op jit(solution)/shard_map/ppermute | solution.py:498
  44.4 9.5 %collective-permute-start.11 = (bf16[16,3584]{1,0:T(8,128)(2,1)S(1)}, bf16[16,3584]{1,0:T(8,128)(2,1)S(1)}, u32[]{:S(2)}, u32[]{:S(2)}) collective-permute-start(bf16[16,3584]{1,0:T(8,128)(2,1)S(1)} %get-tuple-element.101), channel_id=1, source_target_pairs={{0,8},{1,11},{2,10},{3,9},{4,12},{5,15},{6,14},{7,13},{8,0},{9,3},... | collective-permute-start | bytes 344072 | tf_op jit(solution)/shard_map/ppermute | solution.py:498
  44.4 9.5 %collective-permute-start.10 = (bf16[16,3584]{1,0:T(8,128)(2,1)S(1)}, bf16[16,3584]{1,0:T(8,128)(2,1)S(1)}, u32[]{:S(2)}, u32[]{:S(2)}) collective-permute-start(bf16[16,3584]{1,0:T(8,128)(2,1)S(1)} %get-tuple-element.102), channel_id=1, source_target_pairs={{0,4},{1,7},{2,6},{3,5},{4,0},{5,3},{6,2},{7,1},{8,12},{9,15},{10,... | collective-permute-start | bytes 344072 | tf_op jit(solution)/shard_map/ppermute | solution.py:498
  46.3 7.7 %collective-permute-start.9 = (bf16[16,3584]{1,0:T(8,128)(2,1)S(1)}, bf16[16,3584]{1,0:T(8,128)(2,1)S(1)}, u32[]{:S(2)}, u32[]{:S(2)}) collective-permute-start(bf16[16,3584]{1,0:T(8,128)(2,1)S(1)} %get-tuple-element.103), channel_id=1, source_target_pairs={{0,2},{1,1},{2,0},{3,3},{4,6},{5,5},{6,4},{7,7},{8,10},{9,9},{10,8... | collective-permute-start | bytes 344072 | tf_op jit(solution)/shard_map/ppermute | solution.py:498
  54.1 1.8 %collective-permute-start.13 = (bf16[32,3584]{1,0:T(8,128)(2,1)S(1)}, bf16[32,3584]{1,0:T(8,128)(2,1)S(1)}, u32[]{:S(2)}, u32[]{:S(2)}) collective-permute-start(bf16[32,3584]{1,0:T(8,128)(2,1)S(1)} %pad_maximum_fusion), channel_id=1, source_target_pairs={{0,1},{1,0},{2,3},{3,2},{4,5},{5,4},{6,7},{7,6},{8,9},{9,8},{10,11... | collective-permute-start | bytes 688136 | tf_op jit(solution)/shard_map/ppermute | solution.py:492

commit v8 on v7

--- a/solution.py
+++ b/solution.py
@@ -491,9 +491,9 @@
     def swap(block):
         return lax.ppermute(block, "dp", [(0, 1), (1, 0)])
 
-    def travel(block, hop):
+    def travel(block, hop, cross=0):
         moves = [
-            (2 * i + c, 2 * (i ^ hop ^ c) + c) for i in range(FLIGHT) for c in range(2)
+            (2 * i + c, 2 * (i ^ hop ^ c) + (c ^ cross)) for i in range(FLIGHT) for c in range(2)
         ]
         return lax.ppermute(block, ("expert", "dp"), moves)
 
@@ -502,9 +502,10 @@
     msgs = pick(keep, swap(give), my_tokens, swap(tokens), my_grads, swap(grad_out))
     got = [travel(m, hop) for m, hop in zip(msgs, HOPS)]
     halves = load_weights(gate_weight, up_weight, down_weight)
-    got, halves = lax.optimization_barrier((got, halves))
-    own = jnp.concatenate(got, axis=0)
-    blocks = [own, swap(own)]
+    nearest = travel(msgs[-1], HOPS[-1], 1)
+    got, nearest, halves = lax.optimization_barrier((got, nearest, halves))
+    far = jnp.concatenate(got[:-1], axis=0)
+    blocks = [far, got[-1], swap(far), nearest]
     tok, scl, dh, du, act, mine, theirs = activation_grads(blocks, *halves)
     down = down_grads(scl, act)
     added, down = lax.optimization_barrier((swap(theirs), down))

time: 58.1 us -> 57.7 us (level)
  waiting for transfers between devices: 10.3 us -> 9.39 us
  starting transfers between devices: 18.3 us -> 18.9 us
    ppermute x8 -> x9, starting transfers between devices: 16.9 us -> 17.5 us  [travel(): return lax.ppermute(block, ('expert', 'dp'), moves)]
    ppermute x8 -> x9, waiting for transfers between devices: 7.25 us -> 6.65 us  [travel(): return lax.ppermute(block, ('expert', 'dp'), moves)]
  transfers between devices with their start and end apart: 14 -> 15, of which waited for: 5 -> 5; matrix products, arithmetic and copies ran while one was open for 0% -> 0% of each run, Pallas kernels for 35% -> 35%
where the time goes in v8:
time: 57.7 us; the launch traced here: 57.5 us
  Pallas kernels  27.9 us (48%)
  starting transfers between devices  18.9 us (33%)
  waiting for transfers between devices  9.39 us (16%)
  between operations  1.02 us (2%)
    ppermute x9, starting transfers between devices, travel(): return lax.ppermute(block, ('expert', 'dp'), moves)  17.5 us
    pallas_call x1, Pallas kernels, load_weights(): pl.pallas_call(kernel, out_shape=[pltpu.VMEM((half, width), BF16)] * 2 +...  8.7 us
    ppermute x9, waiting for transfers between devices, travel(): return lax.ppermute(block, ('expert', 'dp'), moves)  6.65 us
    pallas_call x1, Pallas kernels, activation_grads(): pl.pallas_call(kernel, out_shape=[pltpu.VMEM((2 * rows, width), BF16)] *...  5.39 us
    pallas_call x1, Pallas kernels, gate_up_grads(): pl.pallas_call(kernel, out_shape=[full, full, pltpu.VMEM((half, width), B...  5.08 us
    ppermute x6, waiting for transfers between devices, swap(): return lax.ppermute(block, 'dp', [(0, 1), (1, 0)])  2.75 us
    pallas_call x1, Pallas kernels, down_grads(): pl.pallas_call(kernel, out_shape=[pltpu.VMEM((half, width), BF16), jax.Sh...  2.32 us
    pallas_call x1, Pallas kernels, combine(): pl.pallas_call(kernel, out_shape=[jax.ShapeDtypeStruct((tok_count, width)...  1.69 us
  transfers between devices with their start and end apart: 15, of which 5 were waited for; matrix products, arithmetic and copies ran while one was open for 0% of the time, Pallas kernels for 35%

profile of v8, /device:TPU:0, one launch (start us, length us, event | category | flops | bytes accessed | tf_op | source)
XLA Modules:
  0.0 57.5 jit_solution(16376214992363098232)
XLA Ops:
  0.6 0.5 collective-permute-start.1
  1.1 0.1 collective-permute-start.2
  1.2 1.0 %route.1 = (bf16[64,128]{1,0:T(8,128)(2,1)S(1)}, f32[32,128]{1,0:T(8,128)S(1)}, f32[32,128]{1,0:T(8,128)S(1)}) custom-call(s32[2]{0:T(128)} %hot_ref.1, s32[8,128]{1,0:T(8,128)} %bitcast.3, f32[8,128]{1,0:T(8,128)} %bitcast.4, s32[1,128]{1,0:T(1,128)} %bitcast.5), custom_call_target="tpu_custom_call" | custom-call | tf_op jit(solution)/shard_map/route/pallas_call | solution.py:137
  2.2 0.5 collective-permute-start
  2.7 1.5 %load_rows.1 = (bf16[128,3584]{1,0:T(8,128)(2,1)S(1)}, bf16[128,3584]{1,0:T(8,128)(2,1)S(1)}) custom-call(bf16[128,3584]{1,0:T(8,128)(2,1)} %refs_0_.1, bf16[128,3584]{1,0:T(8,128)(2,1)} %refs_1_.1), custom_call_target="tpu_custom_call" | custom-call | bytes 3670016 | tf_op jit(solution)/shard_map/load_rows/pallas_call | solution.py:163
  4.2 0.4 collective-permute-done.theirs_ref
  4.6 0.0 collective-permute-done.1.their_tok
  4.6 0.2 collective-permute-done.2.their_grad
  4.8 0.6 %pick.1 = (bf16[32,3584]{1,0:T(8,128)(2,1)S(1)}, bf16[32,3584]{1,0:T(8,128)(2,1)S(1)}, bf16[32,3584]{1,0:T(8,128)(2,1)S(1)}, bf16[32,3584]{1,0:T(8,128)(2,1)S(1)}) custom-call(f32[32,128]{1,0:T(8,128)S(1)} %get-tuple-element.54.mine_ref, f32[32,128]{1,0:T(8,128)S(1)} %collective-permute-done.theirs_ref, bf16[128,3584]{1,0:T(8,128)(2,1)S(1)} %get-tuple-element.56.my_tok, ...), custom_call_target="tpu_custom_call" | custom-call | flops 117440512 | bytes 4587520 | tf_op jit(solution)/shard_map/pick/pallas_call | solution.py:195
  5.4 6.0 %collective-permute-start.3 = (bf16[32,3584]{1,0:T(8,128)(2,1)S(1)}, bf16[32,3584]{1,0:T(8,128)(2,1)S(1)}, u32[]{:S(2)}, u32[]{:S(2)}) collective-permute-start(bf16[32,3584]{1,0:T(8,128)(2,1)S(1)} %get-tuple-element.58), channel_id=1, source_target_pairs={{0,14},{1,13},{2,12},{3,15},{4,10},{5,9},{6,8},{7,11},{8,6},{9,5},... | collective-permute-start | bytes 688136 | tf_op jit(solution)/shard_map/ppermute | solution.py:498
  11.3 0.0 collective-permute-start.4
  11.3 0.8 %collective-permute-start.5 = (bf16[32,3584]{1,0:T(8,128)(2,1)S(1)}, bf16[32,3584]{1,0:T(8,128)(2,1)S(1)}, u32[]{:S(2)}, u32[]{:S(2)}) collective-permute-start(bf16[32,3584]{1,0:T(8,128)(2,1)S(1)} %get-tuple-element.60), channel_id=1, source_target_pairs={{0,4},{1,7},{2,6},{3,5},{4,0},{5,3},{6,2},{7,1},{8,12},{9,15},{10,... | collective-permute-start | bytes 688136 | tf_op jit(solution)/shard_map/ppermute | solution.py:498
  12.1 0.5 collective-permute-start.7
  12.6 2.4 %collective-permute-start.6 = (bf16[32,3584]{1,0:T(8,128)(2,1)S(1)}, bf16[32,3584]{1,0:T(8,128)(2,1)S(1)}, u32[]{:S(2)}, u32[]{:S(2)}) collective-permute-start(bf16[32,3584]{1,0:T(8,128)(2,1)S(1)} %get-tuple-element.61), channel_id=1, source_target_pairs={{0,2},{1,1},{2,0},{3,3},{4,6},{5,5},{6,4},{7,7},{8,10},{9,9},{10,8... | collective-permute-start | bytes 688136 | tf_op jit(solution)/shard_map/ppermute | solution.py:498
  15.1 8.7 %load_weights.1 = (bf16[1024,3584]{1,0:T(8,128)(2,1)S(1)}, bf16[1024,3584]{1,0:T(8,128)(2,1)S(1)}, bf16[3584,1024]{1,0:T(8,128)(2,1)S(1)}, bf16[3584,1024]{1,0:T(8,128)(2,1)S(1)}, bf16[3584,1024]{1,0:T(8,128)(2,1)S(1)}) custom-call(bf16[2048,3584]{1,0:T(8,128)(2,1)} %g_in.1, bf16[2048,3584]{1,0:T(8,128)(2,1)} %u_in.1, bf16[2048,3584]{1,0:T(8,128)(2,1)} %w_in.1), custom_call_target="tpu_custom_call" | custom-call | bytes 44040192 | tf_op jit(solution)/shard_map/load_weights/pallas_call | solution.py:239
  23.8 0.0 collective-permute-done.3
  23.8 6.4 %collective-permute-done.4 = bf16[32,3584]{1,0:T(8,128)(2,1)S(1)} collective-permute-done((bf16[32,3584]{1,0:T(8,128)(2,1)S(1)}, bf16[32,3584]{1,0:T(8,128)(2,1)S(1)}, u32[]{:S(2)}, u32[]{:S(2)}) %collective-permute-start.4) | collective-permute-done | bytes 229408 | tf_op jit(solution)/shard_map/ppermute | solution.py:498
  30.2 0.0 collective-permute-done.5
  30.2 0.0 collective-permute-done.7.refs_3_
  30.2 0.0 collective-permute-done.6.refs_1_
  30.3 0.1 collective-permute-start.8
  30.4 2.1 %collective-permute-done.8.refs_2_ = bf16[96,3584]{1,0:T(8,128)(2,1)S(1)} collective-permute-done((bf16[96,3584]{1,0:T(8,128)(2,1)S(1)}, bf16[96,3584]{1,0:T(8,128)(2,1)S(1)}, u32[]{:S(2)}, u32[]{:S(2)}) %collective-permute-start.8) | collective-permute-done | bytes 688160 | tf_op jit(solution)/shard_map/ppermute | solution.py:492
  32.5 5.4 %activation_grads.1 = (bf16[128,3584]{1,0:T(8,128)(2,1)S(1)}, bf16[128,3584]{1,0:T(8,128)(2,1)S(1)}, bf16[1024,128]{1,0:T(8,128)(2,1)S(1)}, bf16[1024,128]{1,0:T...) custom-call(bf16[96,3584]{1,0:T(8,128)(2,1)S(1)} %constant_dynamic-update-slic, ...), custom_call_target="tpu_custom_call" | custom-call | flops 4697620480 | bytes 22020096 | tf_op jit(solution)/shard_map/activation_grads/pallas_call | solution.py:298
  37.9 0.2 collective-permute-start.9
  38.1 2.3 %down_grads.1 = (bf16[1024,3584]{1,0:T(8,128)(2,1)S(1)}, bf16[1024,3584]{1,0:T(8,128)(2,1)}) custom-call(bf16[128,3584]{1,0:T(8,128)(2,1)S(1)} %get-tuple-element.79.rows_ref, bf16[1024,128]{1,0:T(8,128)(2,1)S(1)} %get-tuple-element.80.left_ref), custom_call_target="tpu_custom_call" | custom-call | flops 939524096 | bytes 7340032 | tf_op jit(solution)/shard_map/down_grads/pallas_call | solution.py:345
  40.5 0.0 collective-permute-done.9
  40.5 0.1 add_convert_fusion
  40.6 3.5 %collective-permute-start.13 = (bf16[16,3584]{1,0:T(8,128)(2,1)S(1)}, bf16[16,3584]{1,0:T(8,128)(2,1)S(1)}, u32[]{:S(2)}, u32[]{:S(2)}) collective-permute-start(bf16[16,3584]{1,0:T(8,128)(2,1)S(1)} %get-tuple-element.102), channel_id=1, source_target_pairs={{0,14},{1,13},{2,12},{3,15},{4,10},{5,9},{6,8},{7,11},{8,6},{9,5},... | collective-permute-start | bytes 344072 | tf_op jit(solution)/shard_map/ppermute | solution.py:498
  44.1 0.0 collective-permute-start.12
  44.1 1.9 %collective-permute-start.11 = (bf16[16,3584]{1,0:T(8,128)(2,1)S(1)}, bf16[16,3584]{1,0:T(8,128)(2,1)S(1)}, u32[]{:S(2)}, u32[]{:S(2)}) collective-permute-start(bf16[16,3584]{1,0:T(8,128)(2,1)S(1)} %get-tuple-element.104), channel_id=1, source_target_pairs={{0,4},{1,7},{2,6},{3,5},{4,0},{5,3},{6,2},{7,1},{8,12},{9,15},{10,... | collective-permute-start | bytes 344072 | tf_op jit(solution)/shard_map/ppermute | solution.py:498
  46.0 2.4 %collective-permute-start.10 = (bf16[16,3584]{1,0:T(8,128)(2,1)S(1)}, bf16[16,3584]{1,0:T(8,128)(2,1)S(1)}, u32[]{:S(2)}, u32[]{:S(2)}) collective-permute-start(bf16[16,3584]{1,0:T(8,128)(2,1)S(1)} %get-tuple-element.105), channel_id=1, source_target_pairs={{0,2},{1,1},{2,0},{3,3},{4,6},{5,5},{6,4},{7,7},{8,10},{9,9},{10,8... | collective-permute-start | bytes 344072 | tf_op jit(solution)/shard_map/ppermute | solution.py:498
  48.4 5.1 %gate_up_grads.1 = (bf16[1024,3584]{1,0:T(8,128)(2,1)}, bf16[1024,3584]{1,0:T(8,128)(2,1)}, bf16[1024,3584]{1,0:T(8,128)(2,1)S(1)}, bf16[1024,3584]{1,0:T(8,128)(2,1)}) custom-call(bf16[128,3584]{1,0:T(8,128)(2,1)S(1)} %get-tuple-element.84.rows_ref, bf16[1024,128]{1,0:T(8,128)(2,1)S(1)} %get-tuple-element.85.gate_ref, ...), custom_call_target="tpu_custom_call", output_to_operand_aliasing={{1}: (4, {})} | custom-call | flops 1879048192 | bytes 14680064 | tf_op jit(solution)/shard_map/gate_up_grads/pallas_call | solution.py:399
  53.5 0.0 collective-permute-done.13
  53.5 0.0 collective-permute-done.12
  53.5 0.0 collective-permute-done.11
  53.5 0.2 collective-permute-done.10
  53.8 0.1 collective-permute-start.14
  53.9 1.7 %write_more.1._ = bf16[1024,3584]{1,0:T(8,128)(2,1)} custom-call(bf16[1024,3584]{1,0:T(8,128)(2,1)S(1)} %get-tuple-element.94.block_ref, bf16[1024,3584]{1,0:T(8,128)(2,1)} %get-tuple-element.95._), custom_call_target="tpu_custom_call", output_to_operand_aliasing={{}: (1, {})} | custom-call | bytes 7340032 | tf_op jit(solution)/shard_map/write_more/pallas_call | solution.py:428
  55.6 0.0 collective-permute-done.14
  55.6 1.7 %combine.1 = (bf16[128,3584]{1,0:T(8,128)(2,1)}, bf16[1024,3584]{1,0:T(8,128)(2,1)}) custom-call(bf16[64,128]{1,0:T(8,128)(2,1)S(1)} %get-tuple-element.53.pick_ref, bf16[64,3584]{1,0:T(8,128)(2,1)S(1)} %constant_dynamic-update-slice_fusion.3.back_ref, bf16[1024,3584]{1,0:T(8,128)(2,1)S(1)} %get-tuple-element.94.block_ref, ...), custom_call_target="tpu_custom_call", output_to_operand_aliasing={{1}: (3, {})} | custom-call | flops 58720256 | bytes 4587520 | tf_op jit(solution)/shard_map/combine/pallas_call | solution.py:465
  (10 shorter events, 0.2 us)
Async XLA Ops:
  0.6 4.0 %collective-permute-start.1 = (bf16[128,3584]{1,0:T(8,128)(2,1)}, bf16[128,3584]{1,0:T(8,128)(2,1)S(1)}, u32[]{:S(2)}, u32[]{:S(2)}) collective-permute-start(bf16[128,3584]{1,0:T(8,128)(2,1)} %refs_0_.1), channel_id=1, source_target_pairs={{0,1},{1,0},{2,3},{3,2},{4,5},{5,4},{6,7},{7,6},{8,9},{9,8},{10,11... | collective-permute-start | bytes 2752520 | tf_op jit(solution)/shard_map/ppermute | solution.py:492
  1.1 3.6 %collective-permute-start.2 = (bf16[128,3584]{1,0:T(8,128)(2,1)}, bf16[128,3584]{1,0:T(8,128)(2,1)S(1)}, u32[]{:S(2)}, u32[]{:S(2)}) collective-permute-start(bf16[128,3584]{1,0:T(8,128)(2,1)} %refs_1_.1), channel_id=1, source_target_pairs={{0,1},{1,0},{2,3},{3,2},{4,5},{5,4},{6,7},{7,6},{8,9},{9,8},{10,11... | collective-permute-start | bytes 2752520 | tf_op jit(solution)/shard_map/ppermute | solution.py:492
  2.2 2.4 %collective-permute-start = (f32[32,128]{1,0:T(8,128)S(1)}, f32[32,128]{1,0:T(8,128)S(1)}, u32[]{:S(2)}, u32[]{:S(2)}) collective-permute-start(f32[32,128]{1,0:T(8,128)S(1)} %get-tuple-element.55), channel_id=1, source_target_pairs={{0,1},{1,0},{2,3},{3,2},{4,5},{5,4},{6,7},{7,6},{8,9},{9,8},{10,11... | collective-permute-start | bytes 49160 | tf_op jit(solution)/shard_map/ppermute | solution.py:492
  5.4 18.4 %collective-permute-start.3 = (bf16[32,3584]{1,0:T(8,128)(2,1)S(1)}, bf16[32,3584]{1,0:T(8,128)(2,1)S(1)}, u32[]{:S(2)}, u32[]{:S(2)}) collective-permute-start(bf16[32,3584]{1,0:T(8,128)(2,1)S(1)} %get-tuple-element.58), channel_id=1, source_target_pairs={{0,14},{1,13},{2,12},{3,15},{4,10},{5,9},{6,8},{7,11},{8,6},{9,5},... | collective-permute-start | bytes 688136 | tf_op jit(solution)/shard_map/ppermute | solution.py:498
  11.3 18.9 %collective-permute-start.4 = (bf16[32,3584]{1,0:T(8,128)(2,1)S(1)}, bf16[32,3584]{1,0:T(8,128)(2,1)S(1)}, u32[]{:S(2)}, u32[]{:S(2)}) collective-permute-start(bf16[32,3584]{1,0:T(8,128)(2,1)S(1)} %get-tuple-element.59), channel_id=1, source_target_pairs={{0,8},{1,11},{2,10},{3,9},{4,12},{5,15},{6,14},{7,13},{8,0},{9,3},... | collective-permute-start | bytes 688136 | tf_op jit(solution)/shard_map/ppermute | solution.py:498
  11.3 18.9 %collective-permute-start.5 = (bf16[32,3584]{1,0:T(8,128)(2,1)S(1)}, bf16[32,3584]{1,0:T(8,128)(2,1)S(1)}, u32[]{:S(2)}, u32[]{:S(2)}) collective-permute-start(bf16[32,3584]{1,0:T(8,128)(2,1)S(1)} %get-tuple-element.60), channel_id=1, source_target_pairs={{0,4},{1,7},{2,6},{3,5},{4,0},{5,3},{6,2},{7,1},{8,12},{9,15},{10,... | collective-permute-start | bytes 688136 | tf_op jit(solution)/shard_map/ppermute | solution.py:498
  12.1 18.1 %collective-permute-start.7 = (bf16[32,3584]{1,0:T(8,128)(2,1)S(1)}, bf16[32,3584]{1,0:T(8,128)(2,1)S(1)}, u32[]{:S(2)}, u32[]{:S(2)}) collective-permute-start(bf16[32,3584]{1,0:T(8,128)(2,1)S(1)} %get-tuple-element.61), channel_id=1, source_target_pairs={{0,3},{1,0},{2,1},{3,2},{4,7},{5,4},{6,5},{7,6},{8,11},{9,8},{10,9... | collective-permute-start | bytes 688136 | tf_op jit(solution)/shard_map/ppermute | solution.py:498
  12.6 17.6 %collective-permute-start.6 = (bf16[32,3584]{1,0:T(8,128)(2,1)S(1)}, bf16[32,3584]{1,0:T(8,128)(2,1)S(1)}, u32[]{:S(2)}, u32[]{:S(2)}) collective-permute-start(bf16[32,3584]{1,0:T(8,128)(2,1)S(1)} %get-tuple-element.61), channel_id=1, source_target_pairs={{0,2},{1,1},{2,0},{3,3},{4,6},{5,5},{6,4},{7,7},{8,10},{9,9},{10,8... | collective-permute-start | bytes 688136 | tf_op jit(solution)/shard_map/ppermute | solution.py:498
  30.3 2.2 %collective-permute-start.8 = (bf16[96,3584]{1,0:T(8,128)(2,1)S(1)}, bf16[96,3584]{1,0:T(8,128)(2,1)S(1)}, u32[]{:S(2)}, u32[]{:S(2)}) collective-permute-start(bf16[96,3584]{1,0:T(8,128)(2,1)S(1)} %constant_dynamic-update-slice_fusion.refs_0_), channel_id=1, source_target_pairs={{0,1},{1,0},{2,3},{3,2},{4,5},{5,4},{6,7},{7,6},{8,9},{9,8},{10,11... | collective-permute-start | bytes 2064392 | tf_op jit(solution)/shard_map/ppermute | solution.py:492
  37.9 2.5 %collective-permute-start.9 = (bf16[64,3584]{1,0:T(8,128)(2,1)S(1)}, bf16[64,3584]{1,0:T(8,128)(2,1)S(1)}, u32[]{:S(2)}, u32[]{:S(2)}) collective-permute-start(bf16[64,3584]{1,0:T(8,128)(2,1)S(1)} %get-tuple-element.78), channel_id=1, source_target_pairs={{0,1},{1,0},{2,3},{3,2},{4,5},{5,4},{6,7},{7,6},{8,9},{9,8},{10,11... | collective-permute-start | bytes 1376264 | tf_op jit(solution)/shard_map/ppermute | solution.py:492
  40.6 12.9 %collective-permute-start.13 = (bf16[16,3584]{1,0:T(8,128)(2,1)S(1)}, bf16[16,3584]{1,0:T(8,128)(2,1)S(1)}, u32[]{:S(2)}, u32[]{:S(2)}) collective-permute-start(bf16[16,3584]{1,0:T(8,128)(2,1)S(1)} %get-tuple-element.102), channel_id=1, source_target_pairs={{0,14},{1,13},{2,12},{3,15},{4,10},{5,9},{6,8},{7,11},{8,6},{9,5},... | collective-permute-start | bytes 344072 | tf_op jit(solution)/shard_map/ppermute | solution.py:498
  44.1 9.5 %collective-permute-start.12 = (bf16[16,3584]{1,0:T(8,128)(2,1)S(1)}, bf16[16,3584]{1,0:T(8,128)(2,1)S(1)}, u32[]{:S(2)}, u32[]{:S(2)}) collective-permute-start(bf16[16,3584]{1,0:T(8,128)(2,1)S(1)} %get-tuple-element.103), channel_id=1, source_target_pairs={{0,8},{1,11},{2,10},{3,9},{4,12},{5,15},{6,14},{7,13},{8,0},{9,3},... | collective-permute-start | bytes 344072 | tf_op jit(solution)/shard_map/ppermute | solution.py:498
  44.1 9.5 %collective-permute-start.11 = (bf16[16,3584]{1,0:T(8,128)(2,1)S(1)}, bf16[16,3584]{1,0:T(8,128)(2,1)S(1)}, u32[]{:S(2)}, u32[]{:S(2)}) collective-permute-start(bf16[16,3584]{1,0:T(8,128)(2,1)S(1)} %get-tuple-element.104), channel_id=1, source_target_pairs={{0,4},{1,7},{2,6},{3,5},{4,0},{5,3},{6,2},{7,1},{8,12},{9,15},{10,... | collective-permute-start | bytes 344072 | tf_op jit(solution)/shard_map/ppermute | solution.py:498
  46.0 7.8 %collective-permute-start.10 = (bf16[16,3584]{1,0:T(8,128)(2,1)S(1)}, bf16[16,3584]{1,0:T(8,128)(2,1)S(1)}, u32[]{:S(2)}, u32[]{:S(2)}) collective-permute-start(bf16[16,3584]{1,0:T(8,128)(2,1)S(1)} %get-tuple-element.105), channel_id=1, source_target_pairs={{0,2},{1,1},{2,0},{3,3},{4,6},{5,5},{6,4},{7,7},{8,10},{9,9},{10,8... | collective-permute-start | bytes 344072 | tf_op jit(solution)/shard_map/ppermute | solution.py:498
  53.8 1.8 %collective-permute-start.14 = (bf16[32,3584]{1,0:T(8,128)(2,1)S(1)}, bf16[32,3584]{1,0:T(8,128)(2,1)S(1)}, u32[]{:S(2)}, u32[]{:S(2)}) collective-permute-start(bf16[32,3584]{1,0:T(8,128)(2,1)S(1)} %pad_maximum_fusion), channel_id=1, source_target_pairs={{0,1},{1,0},{2,3},{3,2},{4,5},{5,4},{6,7},{7,6},{8,9},{9,8},{10,11... | collective-permute-start | bytes 688136 | tf_op jit(solution)/shard_map/ppermute | solution.py:492
